TPU v7x, 512 devices: a whole 4x8x8 slice. The times are simulated.
512 devices in a mesh: sx: 8 (over y), sy: 8 (over x, z_hi), ch: 8 (over z_lo, core).
Axes of the slice: x: 4, y: 8, z: 8 (z_hi: 2, z_lo: 4; z = z_hi * 4 + z_lo), core: 2. Of those that a mesh axis runs over, the one named last changes fastest.
Arguments:
- volume: bfloat16 [128, 2, 256, 1024], P('ch', None, 'sx', 'sy'), may hold values from -6 to 6
- weights: bfloat16 [128, 128, 3, 3, 3], P('ch'), may hold values from -0.109375 to 0.109375
- bias: float32 [128], P('ch'), may hold values from -3 to 3
Outputs:
- activated: bfloat16 [128, 2, 256, 1024], P('ch', None, 'sx', 'sy')
All inputs are finite; a program needn't handle non-finite values.
Results may differ from a plain program's by a relative error of at most 0.0065.
Values may be sent and summed in bfloat16 or wider, within the bound.
No kernel may reach another device: no remote copies, remote signals or barrier semaphores. Data moves between devices by JAX's collectives and lax.ppermute only.
A program may use at most 64 MiB of HBM per device.

v0:
```python
import jax
import jax.numpy as jnp
from jax import lax
from jax.sharding import PartitionSpec as P


def extended(array, sides, width):
    for axis, dim in sides:
        size, length = (lax.axis_size(axis), array.shape[dim])
        up = [(i, (i + 1) % size) for i in range(size - 1)]
        down = [(j, i) for i, j in up]
        last = lax.slice_in_dim(array, length - width, length, axis=dim)
        first = lax.slice_in_dim(array, 0, width, axis=dim)
        before = lax.ppermute(last, axis, up)
        after = lax.ppermute(first, axis, down)
        array = jnp.concatenate([before, array, after], axis=dim)
    return array


def in_order(pieces, dim):
    pieces = jnp.moveaxis(pieces, 0, dim)
    shape = pieces.shape
    return pieces.reshape(*shape[:dim], shape[dim] * shape[dim + 1], *shape[dim + 2 :])


def from_everyone(array, axis):
    copies = jnp.broadcast_to(array, (lax.axis_size(axis), *array.shape))
    return lax.all_to_all(copies, axis, split_axis=0, concat_axis=0, tiled=True)


def gathered_copies(array, axis, dim):
    return in_order(from_everyone(array, axis), dim)


def convolve(field, kernel):
    deeper = jnp.pad(field, ((0, 0), (1, 1), (0, 0), (0, 0)))
    return lax.conv_general_dilated(
        deeper[None],
        kernel,
        (1, 1, 1),
        "VALID",
        dimension_numbers=("NCDHW", "OIDHW", "NCDHW"),
        preferred_element_type=jnp.float32,
    )[0]


def activate(pre, offsets):
    pre = pre + offsets[:, None, None, None]
    return jnp.where(pre >= 0, pre, 0.3 * pre).astype(jnp.bfloat16)


def per_device(volume, weights, bias):
    padded = extended(volume, (("sx", 2), ("sy", 3)), 1)
    rows_here = volume.shape[2]
    groups = lax.axis_size("ch")
    band = rows_here // groups
    stacked = jnp.stack([padded[:, :, k * band : k * band + band + 2, :] for k in range(groups)], 0)
    filters, offsets = (
        gathered_copies(weights, "ch", 0),
        gathered_copies(bias.astype(jnp.bfloat16), "ch", 0).astype(bias.dtype),
    )
    arrived = lax.all_to_all(stacked, "ch", split_axis=0, concat_axis=1, tiled=True)
    result = activate(convolve(arrived[0], filters), offsets)
    return lax.all_to_all(result, "ch", split_axis=0, concat_axis=2, tiled=True)


def solution(mesh):
    in_specs = (P("ch", None, "sx", "sy"), P("ch", None, None, None, None), P("ch"))
    out_specs = P("ch", None, "sx", "sy")
    return jax.shard_map(
        per_device, mesh=mesh, in_specs=in_specs, out_specs=out_specs, check_vma=False
    )
```

profile of v0, /device:TPU:28, one launch (start us, length us, event | category | flops | bytes accessed | tf_op | source)
XLA Modules:
  0.0 115.8 jit_solution(7626409334640733001)
XLA Ops:
  0.0 0.0 copy-start.1
  0.0 0.9 fusion.22
  0.9 4.7 %collective-permute-start = (bf16[16,2,1,128]{3,0,2,1:T(8,128)(2,1)S(1)}, bf16[16,2,1,128]{3,0,2,1:T(8,128)(2,1)S(1)}, u32[]{:S(2)}, u32[]{:S(2)}) collective-permute-start(bf16[16,2,1,128]{3,0,2,1:T(8,128)(2,1)S(1)} %copy.55), channel_id=1, source_target_pairs={{0,64},{64,128},{128,192},{192,256},{256,320},{320,384},{384,448},... | collective-permute-start | bytes 24584 | tf_op jit(solution)/shard_map/ppermute | solution.py:14
  5.6 1.9 %collective-permute-start.1 = (bf16[16,2,1,128]{3,0,2,1:T(8,128)(2,1)S(1)}, bf16[16,2,1,128]{3,0,2,1:T(8,128)(2,1)S(1)}, u32[]{:S(2)}, u32[]{:S(2)}) collective-permute-start(bf16[16,2,1,128]{3,0,2,1:T(8,128)(2,1)S(1)} %copy.56), channel_id=1, source_target_pairs={{64,0},{128,64},{192,128},{256,192},{320,256},{384,320},{448,384},... | collective-permute-start | bytes 24584 | tf_op jit(solution)/shard_map/ppermute | solution.py:15
  7.6 0.0 collective-permute-done
  7.6 1.1 constant_dynamic-update-slice_fusion.1
  8.7 3.7 %collective-permute-done.1 = bf16[16,2,1,128]{3,0,2,1:T(8,128)(2,1)S(1)} collective-permute-done((bf16[16,2,1,128]{3,0,2,1:T(8,128)(2,1)S(1)}, bf16[16,2,1,128]{3,0,2,1:T(8,128)(2,1)S(1)}, u32[]{:S(2)}, u32[]{:S(2)}) %collective-permute-start.1) | collective-permute-done | bytes 8224 | tf_op jit(solution)/shard_map/ppermute | solution.py:15
  12.4 0.1 fusion.21
  12.6 10.9 %collective-permute-start.2 = (bf16[16,2,34,1]{3,0,2,1:T(8,128)(2,1)S(1)}, bf16[16,2,34,1]{3,0,2,1:T(8,128)(2,1)S(1)}, u32[]{:S(2)}, u32[]{:S(2)}) collective-permute-start(bf16[16,2,34,1]{3,0,2,1:T(8,128)(2,1)S(1)} %get-tuple-element.5), channel_id=1, source_target_pairs={{0,8},{8,16},{16,24},{24,32},{32,40},{40,48},{48,56},{1,9},{9,17},... | collective-permute-start | bytes 6536 | tf_op jit(solution)/shard_map/ppermute | solution.py:14
  23.5 1.9 %collective-permute-start.3 = (bf16[16,2,34,1]{3,0,2,1:T(8,128)(2,1)S(1)}, bf16[16,2,34,1]{3,0,2,1:T(8,128)(2,1)S(1)}, u32[]{:S(2)}, u32[]{:S(2)}) collective-permute-start(bf16[16,2,34,1]{3,0,2,1:T(8,128)(2,1)S(1)} %get-tuple-element.6), channel_id=1, source_target_pairs={{8,0},{16,8},{24,16},{32,24},{40,32},{48,40},{56,48},{9,1},{17,9},... | collective-permute-start | bytes 6536 | tf_op jit(solution)/shard_map/ppermute | solution.py:15
  25.4 0.0 copy-done.1
  25.4 0.6 broadcast_in_dim.12
  26.0 5.1 %all-to-all-start.2 = ((bf16[8,1,16]{2,1,0:T(2,128)(2,1)}), bf16[8,1,16]{2,1,0:T(2,128)(2,1)S(1)}, u32[]{:S(2)}, u32[]{:S(2)}) async-start(bf16[8,1,16]{2,1,0:T(2,128)(2,1)} %broadcast_in_dim.12), calls=%async_computation.2 | async-start | bytes 8192 | tf_op jit(solution)/shard_map/all_to_all | solution.py:28
  31.1 0.7 collective-permute-done.2
  31.8 14.1 %collective-permute-done.3 = bf16[16,2,34,1]{3,0,2,1:T(8,128)(2,1)S(1)} collective-permute-done((bf16[16,2,34,1]{3,0,2,1:T(8,128)(2,1)S(1)}, bf16[16,2,34,1]{3,0,2,1:T(8,128)(2,1)S(1)}, u32[]{:S(2)}, u32[]{:S(2)}) %collective-permute-start.3) | collective-permute-done | bytes 2208 | tf_op jit(solution)/shard_map/ppermute | solution.py:15
  46.0 0.3 pad_maximum_fusion
  46.3 0.0 copy-start
  46.5 1.5 %all-to-all-done.2 = bf16[8,1,16]{2,1,0:T(2,128)(2,1)S(1)} async-done(((bf16[8,1,16]{2,1,0:T(2,128)(2,1)}), bf16[8,1,16]{2,1,0:T(2,128)(2,1)S(1)}, u32[]{:S(2)}, u32[]{:S(2)}) %all-to-all-start.2) | async-done | bytes 288 | tf_op jit(solution)/shard_map/all_to_all | solution.py:28
  47.9 24.3 %all_to_all.38 = bf16[8,16,2,6,130]{4,1,3,2,0:T(8,128)(2,1)S(1)} all-to-all(bf16[8,16,2,6,130]{4,1,3,2,0:T(8,128)(2,1)S(1)} %fusion.10), channel_id=1, replica_groups=mesh['sx'=8,'sy'=8,'ch'=8] {'ch'}, dimensions={0} | all-to-all | bytes 798720 | tf_op jit(solution)/shard_map/all_to_all | solution.py:62
  72.3 0.0 copy-done
  72.3 1.0 broadcast_in_dim.11
  73.3 3.5 %all-to-all-start.1 = ((bf16[8,16,128,3,3,3]{2,1,5,4,3,0:T(8,128)(2,1)}), bf16[8,16,128,3,3,3]{2,1,5,4,3,0:T(8,128)(2,1)S(1)}, u32[]{:S(2)}, u32[]{:S(2)}) async-start(bf16[8,16,128,3,3,3]{2,1,5,4,3,0:T(8,128)(2,1)} %broadcast_in_dim.11), calls=%async_computation.1 | async-start | bytes 1769472 | tf_op jit(solution)/shard_map/all_to_all | solution.py:28
  76.9 0.1 reshape.28
  77.0 0.1 copy.43
  77.1 0.2 pad_bitcast_fusion
  77.3 1.0 copy.53
  78.2 0.3 pad.5.clone
  78.6 0.0 copy-start.2
  78.6 0.1 copy.46
  78.7 21.1 %all-to-all-done.1 = bf16[8,16,128,3,3,3]{2,1,5,4,3,0:T(8,128)(2,1)S(1)} async-done(((bf16[8,16,128,3,3,3]{2,1,5,4,3,0:T(8,128)(2,1)}), bf16[8,16,128,3,3,3]{2,1,5,4,3,0:T(8,128)(2,1)S(1)}, u32[]{:S(2)}, u32[]{:S(2)}) %all-to-all-start.1) | async-done | bytes 884768 | tf_op jit(solution)/shard_map/all_to_all | solution.py:28
  99.9 0.2 copy.47
  100.1 0.0 copy-done.2
  100.1 2.1 %convolution_select_fusion = f32[2,4,8,17,128]{4,2,3,1,0:T(8,128)S(1)} fusion(bf16[128,128,3,3,3]{1,0,4,3,2:T(8,128)(2,1)S(1)} %bitcast.59, bf16[128,4,6,1,7,2]{0,4,5,2,1,3:T(8,128)(2,1)S(1)} %slice.62, bf16[128,4,6,1,8,17]{0,4,5,2,1,3:T(8,128)(2,1)S(1)} %copy.46, pred[8,17]{0,1:T(8,128)(4,1)S(1)} %copy-done.2), kind=kOutput, calls=%fused_computation.4 | convolution fusion | flops 965533696 | bytes 2363528 | tf_op jit(solution)/shard_map/conv_general_dilated | solution.py:37
  102.3 0.1 copy.48
  102.4 0.2 fusion.7
  102.6 0.2 copy.49
  102.8 12.1 %all_to_all.39 = bf16[128,2,4,128]{3,2,1,0:T(4,128)(2,1)S(1)} all-to-all(bf16[128,2,4,128]{3,2,1,0:T(4,128)(2,1)S(1)} %copy.49), channel_id=1, replica_groups=mesh['sx'=8,'sy'=8,'ch'=8] {'ch'}, dimensions={0} | all-to-all | bytes 524288 | tf_op jit(solution)/shard_map/all_to_all | solution.py:64
  115.0 0.8 copy.52
  (17 shorter events, 0.2 us)
Async XLA Ops:
  0.0 25.4 %copy-start.1 = (f32[16]{0:T(128)S(1)}, f32[16]{0:T(128)}, u32[]{:S(2)}) copy-start(f32[16]{0:T(128)} %param.5) | copy-start | bytes 196
  0.9 6.6 %collective-permute-start = (bf16[16,2,1,128]{3,0,2,1:T(8,128)(2,1)S(1)}, bf16[16,2,1,128]{3,0,2,1:T(8,128)(2,1)S(1)}, u32[]{:S(2)}, u32[]{:S(2)}) collective-permute-start(bf16[16,2,1,128]{3,0,2,1:T(8,128)(2,1)S(1)} %copy.55), channel_id=1, source_target_pairs={{0,64},{64,128},{128,192},{192,256},{256,320},{320,384},{384,448},... | collective-permute-start | bytes 24584 | tf_op jit(solution)/shard_map/ppermute | solution.py:14
  5.6 6.8 %collective-permute-start.1 = (bf16[16,2,1,128]{3,0,2,1:T(8,128)(2,1)S(1)}, bf16[16,2,1,128]{3,0,2,1:T(8,128)(2,1)S(1)}, u32[]{:S(2)}, u32[]{:S(2)}) collective-permute-start(bf16[16,2,1,128]{3,0,2,1:T(8,128)(2,1)S(1)} %copy.56), channel_id=1, source_target_pairs={{64,0},{128,64},{192,128},{256,192},{320,256},{384,320},{448,384},... | collective-permute-start | bytes 24584 | tf_op jit(solution)/shard_map/ppermute | solution.py:15
  12.6 19.3 %collective-permute-start.2 = (bf16[16,2,34,1]{3,0,2,1:T(8,128)(2,1)S(1)}, bf16[16,2,34,1]{3,0,2,1:T(8,128)(2,1)S(1)}, u32[]{:S(2)}, u32[]{:S(2)}) collective-permute-start(bf16[16,2,34,1]{3,0,2,1:T(8,128)(2,1)S(1)} %get-tuple-element.5), channel_id=1, source_target_pairs={{0,8},{8,16},{16,24},{24,32},{32,40},{40,48},{48,56},{1,9},{9,17},... | collective-permute-start | bytes 6536 | tf_op jit(solution)/shard_map/ppermute | solution.py:14
  23.5 22.5 %collective-permute-start.3 = (bf16[16,2,34,1]{3,0,2,1:T(8,128)(2,1)S(1)}, bf16[16,2,34,1]{3,0,2,1:T(8,128)(2,1)S(1)}, u32[]{:S(2)}, u32[]{:S(2)}) collective-permute-start(bf16[16,2,34,1]{3,0,2,1:T(8,128)(2,1)S(1)} %get-tuple-element.6), channel_id=1, source_target_pairs={{8,0},{16,8},{24,16},{32,24},{40,32},{48,40},{56,48},{9,1},{17,9},... | collective-permute-start | bytes 6536 | tf_op jit(solution)/shard_map/ppermute | solution.py:15
  26.0 21.9 %all-to-all-start.2 = ((bf16[8,1,16]{2,1,0:T(2,128)(2,1)}), bf16[8,1,16]{2,1,0:T(2,128)(2,1)S(1)}, u32[]{:S(2)}, u32[]{:S(2)}) async-start(bf16[8,1,16]{2,1,0:T(2,128)(2,1)} %broadcast_in_dim.12), calls=%async_computation.2 | async-start | bytes 8192 | tf_op jit(solution)/shard_map/all_to_all | solution.py:28
  46.3 26.0 %copy-start = (bf16[16,128,3,3,3]{1,0,4,3,2:T(8,128)(2,1)S(1)}, bf16[16,128,3,3,3]{1,0,4,3,2:T(8,128)(2,1)}, u32[]{:S(2)}) copy-start(bf16[16,128,3,3,3]{1,0,4,3,2:T(8,128)(2,1)} %param.4) | copy-start | bytes 331780
  73.3 26.5 %all-to-all-start.1 = ((bf16[8,16,128,3,3,3]{2,1,5,4,3,0:T(8,128)(2,1)}), bf16[8,16,128,3,3,3]{2,1,5,4,3,0:T(8,128)(2,1)S(1)}, u32[]{:S(2)}, u32[]{:S(2)}) async-start(bf16[8,16,128,3,3,3]{2,1,5,4,3,0:T(8,128)(2,1)} %broadcast_in_dim.11), calls=%async_computation.1 | async-start | bytes 1769472 | tf_op jit(solution)/shard_map/all_to_all | solution.py:28
  78.6 21.6 %copy-start.2 = (pred[8,17]{0,1:T(8,128)(4,1)S(1)}, pred[8,17]{0,1:T(8,128)(4,1)}, u32[]{:S(2)}) copy-start(pred[8,17]{0,1:T(8,128)(4,1)} %constant.13) | copy-start | bytes 412
where the time goes:
time: 116 us
  waiting for transfers between devices  41.1 us (35%)
  blocking collectives  36.5 us (31%)
  starting transfers between devices  28.1 us (24%)
  local copies, waits for them, and re-layouts  7.12 us (6%)
  matrix products  2.13 us (2%)
    all_to_all x1, blocking collectives, per_device(): lax.all_to_all(stacked, 'ch', split_axis=0, concat_axis=1, tiled=True)  24.3 us
    all_to_all x2, waiting for transfers between devices, from_everyone(): return lax.all_to_all(copies, axis, split_axis=0, concat_axis=0, tiled=True)  22.6 us
    ppermute x2, waiting for transfers between devices, extended(): after = lax.ppermute(first, axis, down)  17.8 us
    ppermute x2, starting transfers between devices, extended(): before = lax.ppermute(last, axis, up)  15.6 us
    all_to_all x1, blocking collectives, per_device(): return lax.all_to_all(result, 'ch', split_axis=0, concat_axis=2, tiled=True)  12.1 us
    all_to_all x2, starting transfers between devices, from_everyone(): return lax.all_to_all(copies, axis, split_axis=0, concat_axis=0, tiled=True)  8.63 us
    ppermute x2, starting transfers between devices, extended(): after = lax.ppermute(first, axis, down)  3.84 us
  transfers between devices with their start and end apart: 6, of which 5 were waited for; matrix products, arithmetic and copies ran while one was open for 3% of the time, Pallas kernels for 0%

commit v1 on v0

v1 whole, which is shorter than its diff:
```python
import jax
import jax.numpy as jnp
from jax import lax
from jax.experimental import pallas as pl
from jax.experimental.pallas import tpu as pltpu
from jax.sharding import PartitionSpec as P

BF = jnp.bfloat16
F32 = jnp.float32
SETS = [[0, 1, 2, 3], [4, 5, 6, 7]]


def call(kernel, out_shapes, scratch, *args, flops=0, moved=0):
    vmem = pl.BlockSpec(memory_space=pltpu.VMEM)
    many = isinstance(out_shapes, (list, tuple))
    return pl.pallas_call(
        kernel,
        out_shape=out_shapes,
        in_specs=[vmem] * len(args),
        out_specs=[vmem] * len(out_shapes) if many else vmem,
        scratch_shapes=scratch,
        cost_estimate=pl.CostEstimate(flops=flops, bytes_accessed=moved, transcendentals=0),
    )(*args)


def shaped(*shape, dtype=BF):
    return jax.ShapeDtypeStruct(shape, dtype)


def lanes_of(shape):
    return lax.broadcasted_iota(jnp.int32, shape, len(shape) - 1)


def pack_kernel(vol, slabs, rows, edges, cols, flat):
    flat[...] = vol[...].reshape(1024, 128).astype(F32)
    for z in range(2):
        for row in range(32):
            tile = flat[pl.ds(z * 32 + row, 16, stride=64), :].astype(BF)
            q, r = divmod(row, 8)
            slabs[q, z * 8 + r] = tile
            slabs[q + 4, z * 8 + r] = tile
            here = pl.ds(z * 16, 16)
            if row == 0:
                rows[0, here] = tile
            if row == 31:
                rows[1, here] = tile
            if r == 7 and q < 3:
                edges[q + 1, here] = tile
            if r == 0 and q > 0:
                edges[q - 1, pl.ds(32 + z * 16, 16)] = tile
    nothing = jnp.zeros((32, 128), BF)
    edges[0, pl.ds(0, 32)] = nothing
    edges[3, pl.ds(32, 32)] = nothing
    lane = lanes_of((32, 128))
    both = jnp.zeros((32, 128), F32)
    for z in range(2):
        for c in range(16):
            tile = flat[pl.ds(c * 64 + z * 32, 32), :]
            j = z * 16 + c
            both = jnp.where(lane == j, pltpu.roll(tile, j, 1) if j else tile, both)
            both = jnp.where(lane == 32 + j, pltpu.roll(tile, 33 + j, 1), both)
    cols[...] = both


def corner_kernel(cols, top, bottom, side, buf):
    both = jnp.concatenate(
        [top[...].astype(F32), bottom[...].astype(F32), jnp.zeros((64, 128), F32)], axis=0
    )
    turned = both.T
    first, last = turned[0:1, :], turned[127:128, :]
    lane = lanes_of((1, 128))
    buf[...] = jnp.zeros((40, 128), F32)
    buf[pl.ds(1, 32), :] = cols[...]
    buf[pl.ds(0, 1), :] = jnp.where(lane < 32, first, pltpu.roll(last, 32, 1))
    buf[pl.ds(33, 1), :] = jnp.where(lane < 32, pltpu.roll(first, 96, 1), last)
    side[...] = buf[...].astype(BF)


def halo_kernel(edges, top, bottom, left, right, out):
    lane = lanes_of((40, 128))
    beside = jnp.where(
        lane < 32,
        pltpu.roll(left[...].astype(F32), 96, 1),
        pltpu.roll(right[...].astype(F32), 32, 1),
    )
    for d in range(8):
        q = d % 4
        above = top[...] if q == 0 else edges[q, pl.ds(0, 32)]
        below = bottom[...] if q == 3 else edges[q, pl.ds(32, 32)]
        out[d, pl.ds(0, 32)] = above
        out[d, pl.ds(32, 32)] = below
        out[d, pl.ds(64, 16)] = beside[8 * q : 8 * q + 16].astype(BF)


def conv_kernel(slabs, halo, filters, out, field, taps):
    for src in range(8):
        for z in range(2):
            at = z * 128 + src * 16
            field[pl.ds(at, 16), :] = halo[src, pl.ds(z * 16, 16)]
            field[pl.ds(9 * 256 + at, 16), :] = halo[src, pl.ds(32 + z * 16, 16)]
            for r in range(8):
                field[pl.ds((r + 1) * 256 + at, 16), :] = slabs[src, z * 8 + r]
    for e in range(3):
        for zo in range(2):
            for s in range(4):
                for b in range(3):
                    for zi in range(2):
                        tap = (zi - zo + 1) * 9 + b * 3 + e
                        taps[pl.ds(e * 128 + zo * 64 + s * 16, 16), pl.ds(b * 256 + zi * 128, 128)] = filters[
                            s, pl.ds(tap * 16, 16)
                        ]
    parts = jnp.concatenate([filters[s, pl.ds(432, 16)].astype(F32) for s in range(4)], axis=0)
    offset = (parts[:, 0:1] + parts[:, 1:2]) + parts[:, 2:3]
    offset = jnp.concatenate([offset, offset], axis=0)
    lane16 = lanes_of((16, 128))
    sides = []
    for side in range(2):
        depths = []
        for z in range(2):
            total = jnp.zeros((16, 128), F32)
            for src in range(8):
                piece = halo[src, pl.ds(64, 16)].astype(F32)
                shift = (src * 16 - (side * 32 + z * 16)) % 128
                piece = pltpu.roll(piece, shift, 1) if shift else piece
                total = jnp.where(lane16 // 16 == src, piece, total)
            depths.append(total)
        sides.append(jnp.concatenate(depths, axis=1))
    beside = jnp.concatenate(
        [jnp.concatenate([sides[0][b : b + 8], sides[1][b : b + 8]], axis=0) for b in range(3)], axis=1
    ).astype(BF)
    weights = taps[...]
    edge = lax.dot_general(weights, beside, (((1,), (1,)), ((), ())), preferred_element_type=F32)
    lane = lanes_of((128, 128))
    for p in range(4):
        r = 2 * p
        pair = jnp.concatenate(
            [field[pl.ds(r * 256, 768), :], field[pl.ds((r + 1) * 256, 768), :]], axis=1
        )
        total = jnp.dot(weights, pair, preferred_element_type=F32)
        for h in range(2):
            at = slice(h * 128, (h + 1) * 128)
            row = r + h
            before = pltpu.roll(total[0:128, at], 1, 1)
            after = pltpu.roll(total[256:384, at], 127, 1)
            pre = total[128:256, at]
            pre = pre + jnp.where(lane == 0, edge[0:128, row : row + 1], before)
            pre = pre + jnp.where(lane == 127, edge[256:384, 8 + row : 9 + row], after)
            pre = pre + offset
            done = jnp.where(pre >= 0, pre, 0.3 * pre).astype(BF)
            for z in range(2):
                for s in range(4):
                    out[s, z * 8 + row] = done[z * 64 + s * 16 : z * 64 + s * 16 + 16]


def unpack_kernel(got, out, flat):
    for q in range(4):
        for z in range(2):
            for r in range(8):
                flat[pl.ds(z * 32 + q * 8 + r, 16, stride=64), :] = got[q, z * 8 + r].astype(F32)
    out[...] = flat[...].reshape(16, 2, 32, 128).astype(BF)


def shifts(array, axis, up=True):
    size = lax.axis_size(axis)
    pairs = [(i, i + 1) for i in range(size - 1)]
    return lax.ppermute(array, axis, pairs if up else [(j, i) for i, j in pairs])


def thirds(bias):
    high = bias.astype(BF)
    rest = bias - high.astype(F32)
    middle = rest.astype(BF)
    low = (rest - middle.astype(F32)).astype(BF)
    return jnp.pad(jnp.stack([high, middle, low], axis=1), ((0, 0), (0, 125)))


def per_device(volume, weights, bias):
    slabs, rows, edges, cols = call(
        pack_kernel,
        [shaped(8, 16, 16, 128), shaped(2, 32, 128), shaped(4, 64, 128), shaped(32, 128, dtype=F32)],
        [pltpu.VMEM((1024, 128), F32)],
        volume,
        moved=1 << 20,
    )
    top = shifts(rows[1], "sx", True)
    bottom = shifts(rows[0], "sx", False)
    slabs = lax.all_to_all(slabs, "ch", split_axis=0, concat_axis=0, tiled=True)
    own = jnp.concatenate([weights.transpose(2, 3, 4, 0, 1).reshape(432, 128), thirds(bias)], axis=0)
    filters = lax.all_to_all(
        jnp.broadcast_to(own, (4, 448, 128)), "ch", split_axis=0, concat_axis=0, tiled=True, axis_index_groups=SETS
    )
    side = call(corner_kernel, shaped(40, 128), [pltpu.VMEM((40, 128), F32)], cols, top, bottom, moved=1 << 16)
    left = shifts(side, "sy", True)
    right = shifts(side, "sy", False)
    halo = call(halo_kernel, shaped(8, 80, 128), [], edges, top, bottom, left, right, moved=1 << 18)
    halo = lax.all_to_all(halo, "ch", split_axis=0, concat_axis=0, tiled=True)
    result = call(
        conv_kernel,
        shaped(4, 16, 16, 128),
        [pltpu.VMEM((2560, 128), BF), pltpu.VMEM((384, 768), BF)],
        slabs,
        halo,
        filters,
        flops=2 * 384 * 768 * 1024,
        moved=3 << 20,
    )
    result = lax.all_to_all(result, "ch", split_axis=0, concat_axis=0, tiled=True, axis_index_groups=SETS)
    return call(unpack_kernel, shaped(16, 2, 32, 128), [pltpu.VMEM((1024, 128), F32)], result, moved=1 << 19)


def solution(mesh):
    in_specs = (P("ch", None, "sx", "sy"), P("ch", None, None, None, None), P("ch"))
    out_specs = P("ch", None, "sx", "sy")
    return jax.shard_map(
        per_device, mesh=mesh, in_specs=in_specs, out_specs=out_specs, check_vma=False
    )
```

time: 116 us -> 96.4 us (0.83)
  the two profiles are of different devices: /device:TPU:28 before, /device:TPU:38 now
where the time goes in v1:
time: 96.4 us; the launch traced here: 95.7 us
  blocking collectives  39.8 us (41%)
  starting transfers between devices  23.6 us (24%)
  waiting for transfers between devices  18.9 us (20%)
  Pallas kernels  10.6 us (11%)
  local copies, waits for them, and re-layouts  2.67 us (3%)
    ppermute x4, starting transfers between devices, shifts(): lax.ppermute(array, axis, pairs if up else [(j, i) for i, j in pairs])  18.9 us
    all_to_all x1, blocking collectives, per_device(): slabs = lax.all_to_all(slabs, 'ch', split_axis=0, concat_axis=0, tiled=True)  18.4 us
    ppermute x4, waiting for transfers between devices, shifts(): lax.ppermute(array, axis, pairs if up else [(j, i) for i, j in pairs])  11.9 us
    all_to_all x1, blocking collectives, per_device(): lax.all_to_all(jnp.broadcast_to(own, (4, 448, 128)), 'ch', split_axis=0,...  11.3 us
    pallas_call x5, Pallas kernels, call(): pl.pallas_call(kernel, out_shape=out_shapes, in_specs=[vmem] * len(args),...  10.6 us
    all_to_all x1, blocking collectives, per_device(): lax.all_to_all(result, 'ch', split_axis=0, concat_axis=0, tiled=True, axi...  10.1 us
    all_to_all x1, waiting for transfers between devices, per_device(): halo = lax.all_to_all(halo, 'ch', split_axis=0, concat_axis=0, tiled=True)  7.04 us
    all_to_all x1, starting transfers between devices, per_device(): halo = lax.all_to_all(halo, 'ch', split_axis=0, concat_axis=0, tiled=True)  4.69 us
  transfers between devices with their start and end apart: 5, of which 3 were waited for; matrix products, arithmetic and copies ran while one was open for 0% of the time, Pallas kernels for 0%

profile of v1, /device:TPU:38, one launch (start us, length us, event | category | flops | bytes accessed | tf_op | source)
XLA Modules:
  0.0 95.7 jit_solution(7973611035342760026)
XLA Ops:
  0.0 2.2 %shard_map.37 = (bf16[8,16,16,128]{3,2,1,0:T(8,128)(2,1)}, bf16[2,32,128]{2,1,0:T(8,128)(2,1)}, bf16[4,64,128]{2,1,0:T(8,128)(2,1)}, f32[32,128]{1,0:T(8,128)}) custom-call(bf16[16,2,32,128]{3,2,1,0:T(8,128)(2,1)} %vol.1), custom_call_target="tpu_custom_call" | custom-call | bytes 1048576 | tf_op jit(solution)/shard_map/pallas_call | solution.py:16
  2.2 0.7 slice_bitcast_fusion
  2.9 2.3 %collective-permute-start.1 = (bf16[32,128]{1,0:T(8,128)(2,1)S(1)}, bf16[32,128]{1,0:T(8,128)(2,1)S(1)}, u32[]{:S(2)}, u32[]{:S(2)}) collective-permute-start(bf16[32,128]{1,0:T(8,128)(2,1)S(1)} %get-tuple-element.13), channel_id=1, source_target_pairs={{64,0},{128,64},{192,128},{256,192},{320,256},{384,320},{448,384},... | collective-permute-start | bytes 24584 | tf_op jit(solution)/shard_map/ppermute | solution.py:166
  5.3 3.5 %collective-permute-start = (bf16[32,128]{1,0:T(8,128)(2,1)S(1)}, bf16[32,128]{1,0:T(8,128)(2,1)S(1)}, u32[]{:S(2)}, u32[]{:S(2)}) collective-permute-start(bf16[32,128]{1,0:T(8,128)(2,1)S(1)} %get-tuple-element.14), channel_id=1, source_target_pairs={{0,64},{64,128},{128,192},{192,256},{256,320},{320,384},{384,448},... | collective-permute-start | bytes 24584 | tf_op jit(solution)/shard_map/ppermute | solution.py:166
  8.8 0.0 collective-permute-done.1.bottom
  8.8 0.0 copy-start.3
  8.8 3.2 %collective-permute-done.top = bf16[32,128]{1,0:T(8,128)(2,1)S(1)} collective-permute-done((bf16[32,128]{1,0:T(8,128)(2,1)S(1)}, bf16[32,128]{1,0:T(8,128)(2,1)S(1)}, u32[]{:S(2)}, u32[]{:S(2)}) %collective-permute-start) | collective-permute-done | bytes 8224 | tf_op jit(solution)/shard_map/ppermute | solution.py:166
  12.1 0.0 copy-start.4
  12.1 0.0 copy-done.3
  12.1 0.6 copy-done.4
  12.6 1.5 %shard_map.38 = bf16[40,128]{1,0:T(8,128)(2,1)} custom-call(f32[32,128]{1,0:T(8,128)} %get-tuple-element.12.cols, bf16[32,128]{1,0:T(8,128)(2,1)} %copy-done.4, bf16[32,128]{1,0:T(8,128)(2,1)} %copy-done.3), custom_call_target="tpu_custom_call" | custom-call | bytes 65536 | tf_op jit(solution)/shard_map/pallas_call | solution.py:16
  14.2 11.2 %collective-permute-start.3 = (bf16[40,128]{1,0:T(8,128)(2,1)}, bf16[40,128]{1,0:T(8,128)(2,1)S(1)}, u32[]{:S(2)}, u32[]{:S(2)}) collective-permute-start(bf16[40,128]{1,0:T(8,128)(2,1)} %shard_map.38), channel_id=1, source_target_pairs={{8,0},{16,8},{24,16},{32,24},{40,32},{48,40},{56,48},{9,1},{17,9},... | collective-permute-start | bytes 30728 | tf_op jit(solution)/shard_map/ppermute | solution.py:166
  25.3 1.9 %collective-permute-start.2 = (bf16[40,128]{1,0:T(8,128)(2,1)}, bf16[40,128]{1,0:T(8,128)(2,1)S(1)}, u32[]{:S(2)}, u32[]{:S(2)}) collective-permute-start(bf16[40,128]{1,0:T(8,128)(2,1)} %shard_map.38), channel_id=1, source_target_pairs={{0,8},{8,16},{16,24},{24,32},{32,40},{40,48},{48,56},{1,9},{9,17},... | collective-permute-start | bytes 30728 | tf_op jit(solution)/shard_map/ppermute | solution.py:166
  27.3 0.0 collective-permute-done.3.right
  27.3 0.0 copy-start.5
  27.3 8.6 %collective-permute-done.2.left = bf16[40,128]{1,0:T(8,128)(2,1)S(1)} collective-permute-done((bf16[40,128]{1,0:T(8,128)(2,1)}, bf16[40,128]{1,0:T(8,128)(2,1)S(1)}, u32[]{:S(2)}, u32[]{:S(2)}) %collective-permute-start.2) | collective-permute-done | bytes 10272 | tf_op jit(solution)/shard_map/ppermute | solution.py:166
  35.9 0.0 copy-start.6
  35.9 0.0 copy-done.5
  35.9 0.6 copy-done.6
  36.5 1.6 %shard_map.39 = bf16[8,80,128]{2,1,0:T(8,128)(2,1)} custom-call(bf16[4,64,128]{2,1,0:T(8,128)(2,1)} %get-tuple-element.10.edges, bf16[32,128]{1,0:T(8,128)(2,1)} %copy-done.4, bf16[32,128]{1,0:T(8,128)(2,1)} %copy-done.3, bf16[40,128]{1,0:T(8,128)(2,1)} %copy-done.6, bf16[40,128]{1,0:T(8,128)(2,1)} %copy-done.5), custom_call_target="tpu_custom_call" | custom-call | bytes 262144 | tf_op jit(solution)/shard_map/pallas_call | solution.py:16
  38.1 0.0 copy-start.7
  38.1 0.0 copy-start.2
  38.1 4.7 %all-to-all-start.1 = ((bf16[8,80,128]{2,1,0:T(8,128)(2,1)}), bf16[8,80,128]{2,1,0:T(8,128)(2,1)S(1)}, u32[]{:S(2)}, u32[]{:S(2)}) async-start(bf16[8,80,128]{2,1,0:T(8,128)(2,1)} %shard_map.39), calls=%async_computation.1 | async-start | bytes 327680 | tf_op jit(solution)/shard_map/all_to_all | solution.py:196
  42.8 0.0 copy-done.7
  42.9 0.1 copy.5
  43.0 0.0 copy-done.2
  43.0 7.0 %all-to-all-done.1.halo = bf16[8,80,128]{2,1,0:T(8,128)(2,1)S(1)} async-done(((bf16[8,80,128]{2,1,0:T(8,128)(2,1)}), bf16[8,80,128]{2,1,0:T(8,128)(2,1)S(1)}, u32[]{:S(2)}, u32[]{:S(2)}) %all-to-all-start.1) | async-done | bytes 163872 | tf_op jit(solution)/shard_map/all_to_all | solution.py:196
  50.0 0.0 copy-start.1
  50.0 0.1 broadcast_in_dim.3
  50.1 0.6 copy-done.1
  50.7 0.0 copy-start
  50.7 11.3 %all_to_all.20.filters = bf16[4,448,128]{2,1,0:T(8,128)(2,1)} all-to-all(bf16[4,448,128]{2,1,0:T(8,128)(2,1)S(1)} %broadcast_in_dim.3), channel_id=1, replica_groups={{0,1,2,3},{4,5,6,7},{8,9,10,11},{12,13,14,15},{16,17,18,19},{20,21,22,2..., dimensions={0} | all-to-all | bytes 917504 | tf_op jit(solution)/shard_map/all_to_all | solution.py:189
  62.0 0.0 copy-done
  62.0 18.4 %all_to_all.21.slabs = bf16[8,16,16,128]{3,2,1,0:T(8,128)(2,1)} all-to-all(bf16[8,16,16,128]{3,2,1,0:T(8,128)(2,1)S(1)} %copy-done), channel_id=1, replica_groups=mesh['sx'=8,'sy'=8,'ch'=8] {'ch'}, dimensions={0} | all-to-all | bytes 1048576 | tf_op jit(solution)/shard_map/all_to_all | solution.py:187
  80.4 3.1 %shard_map.40 = bf16[4,16,16,128]{3,2,1,0:T(8,128)(2,1)} custom-call(bf16[8,16,16,128]{3,2,1,0:T(8,128)(2,1)} %all_to_all.21.slabs, bf16[8,80,128]{2,1,0:T(8,128)(2,1)} %copy-done.1, bf16[4,448,128]{2,1,0:T(8,128)(2,1)} %all_to_all.20.filters), custom_call_target="tpu_custom_call" | custom-call | flops 603979776 | bytes 3145728 | tf_op jit(solution)/shard_map/pallas_call | solution.py:16
  83.5 10.1 %all_to_all.22.got = bf16[4,16,16,128]{3,2,1,0:T(8,128)(2,1)} all-to-all(bf16[4,16,16,128]{3,2,1,0:T(8,128)(2,1)} %shard_map.40), channel_id=1, replica_groups={{0,1,2,3},{4,5,6,7},{8,9,10,11},{12,13,14,15},{16,17,18,19},{20,21,22,2..., dimensions={0} | all-to-all | bytes 524288 | tf_op jit(solution)/shard_map/all_to_all | solution.py:207
  93.6 2.1 %shard_map.41 = bf16[16,2,32,128]{3,2,1,0:T(8,128)(2,1)} custom-call(bf16[4,16,16,128]{3,2,1,0:T(8,128)(2,1)} %all_to_all.22.got), custom_call_target="tpu_custom_call" | custom-call | bytes 524288 | tf_op jit(solution)/shard_map/pallas_call | solution.py:16
  (3 shorter events, 0.0 us)
Async XLA Ops:
  2.9 5.8 %collective-permute-start.1 = (bf16[32,128]{1,0:T(8,128)(2,1)S(1)}, bf16[32,128]{1,0:T(8,128)(2,1)S(1)}, u32[]{:S(2)}, u32[]{:S(2)}) collective-permute-start(bf16[32,128]{1,0:T(8,128)(2,1)S(1)} %get-tuple-element.13), channel_id=1, source_target_pairs={{64,0},{128,64},{192,128},{256,192},{320,256},{384,320},{448,384},... | collective-permute-start | bytes 24584 | tf_op jit(solution)/shard_map/ppermute | solution.py:166
  5.3 6.8 %collective-permute-start = (bf16[32,128]{1,0:T(8,128)(2,1)S(1)}, bf16[32,128]{1,0:T(8,128)(2,1)S(1)}, u32[]{:S(2)}, u32[]{:S(2)}) collective-permute-start(bf16[32,128]{1,0:T(8,128)(2,1)S(1)} %get-tuple-element.14), channel_id=1, source_target_pairs={{0,64},{64,128},{128,192},{192,256},{256,320},{320,384},{384,448},... | collective-permute-start | bytes 24584 | tf_op jit(solution)/shard_map/ppermute | solution.py:166
  8.8 3.3 %copy-start.3 = (bf16[32,128]{1,0:T(8,128)(2,1)}, bf16[32,128]{1,0:T(8,128)(2,1)S(1)}, u32[]{:S(2)}) copy-start(bf16[32,128]{1,0:T(8,128)(2,1)S(1)} %collective-permute-done.1.bottom) | copy-start | bytes 24580
  12.1 0.6 copy-start.4
  14.2 13.1 %collective-permute-start.3 = (bf16[40,128]{1,0:T(8,128)(2,1)}, bf16[40,128]{1,0:T(8,128)(2,1)S(1)}, u32[]{:S(2)}, u32[]{:S(2)}) collective-permute-start(bf16[40,128]{1,0:T(8,128)(2,1)} %shard_map.38), channel_id=1, source_target_pairs={{8,0},{16,8},{24,16},{32,24},{40,32},{48,40},{56,48},{9,1},{17,9},... | collective-permute-start | bytes 30728 | tf_op jit(solution)/shard_map/ppermute | solution.py:166
  25.3 10.6 %collective-permute-start.2 = (bf16[40,128]{1,0:T(8,128)(2,1)}, bf16[40,128]{1,0:T(8,128)(2,1)S(1)}, u32[]{:S(2)}, u32[]{:S(2)}) collective-permute-start(bf16[40,128]{1,0:T(8,128)(2,1)} %shard_map.38), channel_id=1, source_target_pairs={{0,8},{8,16},{16,24},{24,32},{32,40},{40,48},{48,56},{1,9},{9,17},... | collective-permute-start | bytes 30728 | tf_op jit(solution)/shard_map/ppermute | solution.py:166
  27.3 8.7 %copy-start.5 = (bf16[40,128]{1,0:T(8,128)(2,1)}, bf16[40,128]{1,0:T(8,128)(2,1)S(1)}, u32[]{:S(2)}) copy-start(bf16[40,128]{1,0:T(8,128)(2,1)S(1)} %collective-permute-done.3.right) | copy-start | bytes 30724
  35.9 0.6 copy-start.6
  38.1 4.7 %copy-start.7 = (f32[16]{0:T(128)S(1)}, f32[16]{0:T(128)}, u32[]{:S(2)}) copy-start(f32[16]{0:T(128)} %param.5) | copy-start | bytes 196
  38.1 4.8 %copy-start.2 = (bf16[16,128,3,3,3]{1,0,4,3,2:T(8,128)(2,1)S(1)}, bf16[16,128,3,3,3]{1,0,4,3,2:T(8,128)(2,1)}, u32[]{:S(2)}) copy-start(bf16[16,128,3,3,3]{1,0,4,3,2:T(8,128)(2,1)} %param.4) | copy-start | bytes 331780
  38.1 11.9 %all-to-all-start.1 = ((bf16[8,80,128]{2,1,0:T(8,128)(2,1)}), bf16[8,80,128]{2,1,0:T(8,128)(2,1)S(1)}, u32[]{:S(2)}, u32[]{:S(2)}) async-start(bf16[8,80,128]{2,1,0:T(8,128)(2,1)} %shard_map.39), calls=%async_computation.1 | async-start | bytes 327680 | tf_op jit(solution)/shard_map/all_to_all | solution.py:196
  50.0 0.7 copy-start.1
  50.7 11.3 %copy-start = (bf16[8,16,16,128]{3,2,1,0:T(8,128)(2,1)S(1)}, bf16[8,16,16,128]{3,2,1,0:T(8,128)(2,1)}, u32[]{:S(2)}) copy-start(bf16[8,16,16,128]{3,2,1,0:T(8,128)(2,1)} %get-tuple-element.9) | copy-start | bytes 1572868

commit v2 on v1

v2 whole, which is shorter than its diff:
```python
import jax
import jax.numpy as jnp
from jax import lax
from jax.experimental import pallas as pl
from jax.experimental.pallas import tpu as pltpu
from jax.sharding import PartitionSpec as P


BF = jnp.bfloat16
F32 = jnp.float32
GRANT = 16 << 20


def call(kernel, out_shapes, scratch, *args, flops=0, moved=0):
    vmem = pl.BlockSpec(memory_space=pltpu.VMEM)
    many = isinstance(out_shapes, (list, tuple))
    return pl.pallas_call(
        kernel,
        out_shape=out_shapes,
        in_specs=[vmem] * len(args),
        out_specs=[vmem] * len(out_shapes) if many else vmem,
        scratch_shapes=scratch,
        cost_estimate=pl.CostEstimate(flops=flops, bytes_accessed=moved, transcendentals=0),
        compiler_params=pltpu.CompilerParams(vmem_limit_bytes=GRANT),
    )(*args)


def shaped(*shape, dtype=BF):
    return jax.ShapeDtypeStruct(shape, dtype)


def lanes_of(shape):
    return lax.broadcasted_iota(jnp.int32, shape, len(shape) - 1)


def pack_kernel(vol, slabs, first, last, edges, flat):
    flat[...] = vol[...].reshape(1024, 128).astype(F32)
    for z in range(2):
        for row in range(32):
            tile = flat[pl.ds(z * 32 + row, 16, stride=64), :].astype(BF)
            q, r = divmod(row, 8)
            slabs[q, z * 8 + r] = tile
            slabs[q + 4, z * 8 + r] = tile
            here = pl.ds(z * 16, 16)
            if row == 0:
                first[here] = tile
            if row == 31:
                last[here] = tile
            if r == 7 and q < 3:
                edges[q + 1, here] = tile
            if r == 0 and q > 0:
                edges[q - 1, pl.ds(32 + z * 16, 16)] = tile
    nothing = jnp.zeros((32, 128), BF)
    edges[0, pl.ds(0, 32)] = nothing
    edges[3, pl.ds(32, 32)] = nothing


def columns_kernel(vol, cols):
    lane = lanes_of((32, 128))
    both = jnp.zeros((32, 128), F32)
    for z in range(2):
        for c in range(16):
            tile = vol[c, z].astype(F32)
            j = z * 16 + c
            both = jnp.where(lane == j, pltpu.roll(tile, j, 1) if j else tile, both)
            both = jnp.where(lane == 32 + j, pltpu.roll(tile, 33 + j, 1), both)
    cols[...] = both


def corner_kernel(cols, top, bottom, side, buf):
    both = jnp.concatenate(
        [top[...].astype(F32), bottom[...].astype(F32), jnp.zeros((64, 128), F32)], axis=0
    )
    turned = both.T
    first, last = turned[0:1, :], turned[127:128, :]
    lane = lanes_of((1, 128))
    buf[...] = jnp.zeros((40, 128), F32)
    buf[pl.ds(1, 32), :] = cols[...]
    buf[pl.ds(0, 1), :] = jnp.where(lane < 32, first, pltpu.roll(last, 32, 1))
    buf[pl.ds(33, 1), :] = jnp.where(lane < 32, pltpu.roll(first, 96, 1), last)
    side[...] = buf[...].astype(BF)


def halo_kernel(edges, top, bottom, left, right, out):
    lane = lanes_of((40, 128))
    beside = jnp.where(
        lane < 32,
        pltpu.roll(left[...].astype(F32), 96, 1),
        pltpu.roll(right[...].astype(F32), 32, 1),
    )
    for d in range(8):
        q = d % 4
        above = top[...] if q == 0 else edges[q, pl.ds(0, 32)]
        below = bottom[...] if q == 3 else edges[q, pl.ds(32, 32)]
        out[d, pl.ds(0, 32)] = above
        out[d, pl.ds(32, 32)] = below
        out[d, pl.ds(64, 16)] = beside[8 * q : 8 * q + 16].astype(BF)


def inner_kernel(slabs, f0, f1, f2, f3, pre, taps, field):
    for src in range(8):
        for z in range(2):
            for r in range(8):
                field[pl.ds(r * 256 + z * 128 + src * 16, 16), :] = slabs[src, z * 8 + r]
    for e in range(3):
        for zo in range(2):
            for t, own in enumerate((f0, f1, f2, f3)):
                for b in range(3):
                    for zi in range(2):
                        tap = (zi - zo + 1) * 9 + b * 3 + e
                        taps[
                            pl.ds(e * 128 + zo * 64 + t * 16, 16), pl.ds(b * 256 + zi * 128, 128)
                        ] = own[pl.ds(tap * 16, 16)]
    weights = taps[...]
    lane = lanes_of((128, 128))
    for p in range(4):
        r = 2 * p
        low = 256 if r == 0 else 0
        high = 512 if r == 6 else 768
        start = (r - 1) * 256
        one = field[pl.ds(start + low, 768 - low), :]
        two = field[pl.ds(start + 256, high), :]
        if low:
            total = jnp.concatenate(
                [
                    jnp.dot(weights[:, low:], one, preferred_element_type=F32),
                    jnp.dot(weights, two, preferred_element_type=F32),
                ],
                axis=1,
            )
        elif high < 768:
            total = jnp.concatenate(
                [
                    jnp.dot(weights, one, preferred_element_type=F32),
                    jnp.dot(weights[:, :high], two, preferred_element_type=F32),
                ],
                axis=1,
            )
        else:
            total = jnp.dot(weights, jnp.concatenate([one, two], axis=1), preferred_element_type=F32)
        for h in range(2):
            pre[r + h] = aligned(total[:, h * 128 : (h + 1) * 128], lane)


def aligned(total, lane):
    before = jnp.where(lane == 0, 0.0, pltpu.roll(total[0:128], 1, 1))
    after = jnp.where(lane == 127, 0.0, pltpu.roll(total[256:384], 127, 1))
    return total[128:256] + (before + after)


def outer_kernel(pre, taps, halo, f0, f1, f2, f3, o0, o1, o2, o3):
    parts = jnp.concatenate([f[pl.ds(432, 16)].astype(F32) for f in (f0, f1, f2, f3)], axis=0)
    offset = (parts[:, 0:1] + parts[:, 1:2]) + parts[:, 2:3]
    offset = jnp.concatenate([offset, offset], axis=0)
    lane16 = lanes_of((16, 128))
    sides = []
    for side in range(2):
        depths = []
        for z in range(2):
            total = jnp.zeros((16, 128), F32)
            for src in range(8):
                piece = halo[src, pl.ds(64, 16)].astype(F32)
                shift = (src * 16 - (side * 32 + z * 16)) % 128
                piece = pltpu.roll(piece, shift, 1) if shift else piece
                total = jnp.where(lane16 // 16 == src, piece, total)
            depths.append(total)
        sides.append(jnp.concatenate(depths, axis=1))
    beside = jnp.concatenate(
        [jnp.concatenate([sides[0][b : b + 8], sides[1][b : b + 8]], axis=0) for b in range(3)], axis=1
    ).astype(BF)
    edge = lax.dot_general(
        taps[...], beside, (((1,), (1,)), ((), ())), preferred_element_type=F32
    )
    lane = lanes_of((128, 128))
    more = []
    for side in range(2):
        beyond = jnp.concatenate(
            [halo[src, pl.ds(side * 32 + z * 16, 16)] for z in range(2) for src in range(8)], axis=0
        )
        near = taps[:, pl.ds(side * 512, 256)]
        more.append(aligned(jnp.dot(near, beyond, preferred_element_type=F32), lane))
    for row in range(8):
        total = pre[row] + offset
        if row == 0:
            total = total + more[0]
        if row == 7:
            total = total + more[1]
        total = total + jnp.where(lane == 0, edge[0:128, row : row + 1], 0.0)
        total = total + jnp.where(lane == 127, edge[256:384, 8 + row : 9 + row], 0.0)
        done = jnp.where(total >= 0, total, 0.3 * total).astype(BF)
        for z in range(2):
            for t, out in enumerate((o0, o1, o2, o3)):
                out[z * 8 + row] = done[z * 64 + t * 16 : z * 64 + t * 16 + 16]


def unpack_kernel(g0, g1, g2, g3, out, flat):
    quarter = lax.rem(lax.axis_index("ch"), 4)
    for t, got in enumerate((g0, g1, g2, g3)):
        start = 8 * (quarter ^ t)
        for z in range(2):
            for r in range(8):
                flat[pl.ds(start + z * 32 + r, 16, stride=64), :] = got[z * 8 + r].astype(F32)
    out[...] = flat[...].reshape(16, 2, 32, 128).astype(BF)


def shifts(array, axis, up=True):
    size = lax.axis_size(axis)
    pairs = [(i, i + 1) for i in range(size - 1)]
    return lax.ppermute(array, axis, pairs if up else [(j, i) for i, j in pairs])


def thirds(bias):
    high = bias.astype(BF)
    rest = bias - high.astype(F32)
    middle = rest.astype(BF)
    low = (rest - middle.astype(F32)).astype(BF)
    return jnp.pad(jnp.stack([high, middle, low], axis=1), ((0, 0), (0, 125)))


def swapped(array, t):
    return lax.ppermute(array, "ch", [(d, d ^ t) for d in range(8)])


def stages(volume, weights, bias):
    slabs, first, last, edges = call(
        pack_kernel,
        [shaped(8, 16, 16, 128), shaped(32, 128), shaped(32, 128), shaped(4, 64, 128)],
        [pltpu.VMEM((1024, 128), F32)],
        volume,
        moved=1 << 20,
    )
    slabs = lax.all_to_all(slabs, "ch", split_axis=0, concat_axis=0, tiled=True)
    top = shifts(last, "sx", True)
    bottom = shifts(first, "sx", False)
    cols = call(columns_kernel, shaped(32, 128, dtype=F32), [], volume, moved=1 << 19)
    side = call(corner_kernel, shaped(40, 128), [pltpu.VMEM((40, 128), F32)], cols, top, bottom, moved=1 << 16)
    left = shifts(side, "sy", True)
    right = shifts(side, "sy", False)
    own = jnp.concatenate([weights.transpose(2, 3, 4, 0, 1).reshape(432, 128), thirds(bias)], axis=0)
    filters = (own,) + tuple(swapped(own, t) for t in (1, 2, 3))
    halo = call(halo_kernel, shaped(8, 80, 128), [], edges, top, bottom, left, right, moved=1 << 18)
    halo = lax.all_to_all(halo, "ch", split_axis=0, concat_axis=0, tiled=True)
    pre, taps = call(
        inner_kernel,
        [shaped(8, 128, 128, dtype=F32), shaped(384, 768)],
        [pltpu.VMEM((2048, 128), BF)],
        slabs,
        *filters,
        flops=2 * 384 * 768 * 1024,
        moved=3 << 20,
    )
    mine, *others = call(
        outer_kernel,
        [shaped(16, 16, 128)] * 4,
        [],
        pre,
        taps,
        halo,
        *filters,
        flops=2 * 384 * 768 * 128,
        moved=2 << 20,
    )
    others = [swapped(others[t - 1], t) for t in (1, 2, 3)]
    return call(
        unpack_kernel,
        shaped(16, 2, 32, 128),
        [pltpu.VMEM((1024, 128), F32)],
        mine,
        *others,
        moved=1 << 19,
    )


def solution(mesh):
    in_specs = (P("ch", None, "sx", "sy"), P("ch", None, None, None, None), P("ch"))
    out_specs = P("ch", None, "sx", "sy")
    return jax.shard_map(stages, mesh=mesh, in_specs=in_specs, out_specs=out_specs, check_vma=False)
```

time: 96.4 us -> 72.6 us (0.75)
  the two profiles are of different devices: /device:TPU:38 before, /device:TPU:27 now
where the time goes in v2:
time: 72.6 us; the launch traced here: 72 us
  starting transfers between devices  48 us (66%)
  waiting for transfers between devices  17.4 us (24%)
  Pallas kernels  5.37 us (7%)
  local copies, waits for them, and re-layouts  1.06 us (1%)
    ppermute x4, starting transfers between devices, shifts(): lax.ppermute(array, axis, pairs if up else [(j, i) for i, j in pairs])  16.4 us
    ppermute x6, starting transfers between devices, swapped(): return lax.ppermute(array, 'ch', [(d, d ^ t) for d in range(8)])  15.7 us
    ppermute x4, waiting for transfers between devices, shifts(): lax.ppermute(array, axis, pairs if up else [(j, i) for i, j in pairs])  9.94 us
    all_to_all x1, starting transfers between devices, stages(): slabs = lax.all_to_all(slabs, 'ch', split_axis=0, concat_axis=0, tiled=True)  8.07 us
    all_to_all x1, starting transfers between devices, stages(): halo = lax.all_to_all(halo, 'ch', split_axis=0, concat_axis=0, tiled=True)  7.73 us
    ppermute x6, waiting for transfers between devices, swapped(): return lax.ppermute(array, 'ch', [(d, d ^ t) for d in range(8)])  7.45 us
    pallas_call x7, Pallas kernels, call(): pl.pallas_call(kernel, out_shape=out_shapes, in_specs=[vmem] * len(args),...  5.37 us
  transfers between devices with their start and end apart: 12, of which 5 were waited for; matrix products, arithmetic and copies ran while one was open for 0% of the time, Pallas kernels for 3%

profile of v2, /device:TPU:27, one launch (start us, length us, event | category | flops | bytes accessed | tf_op | source)
XLA Modules:
  0.0 72.0 jit_solution(10302150035609075170)
XLA Ops:
  0.0 0.0 copy-start
  0.0 0.9 %copy-done = bf16[16,2,32,128]{3,2,1,0:T(8,128)(2,1)S(1)} copy-done((bf16[16,2,32,128]{3,2,1,0:T(8,128)(2,1)S(1)}, bf16[16,2,32,128]{3,2,1,0:T(8,128)(2,1)}, u32[]{:S(2)}) %copy-start) | copy-done | bytes 262168
  1.0 1.1 %shard_map.37 = (bf16[8,16,16,128]{3,2,1,0:T(8,128)(2,1)}, bf16[32,128]{1,0:T(8,128)(2,1)S(1)}, bf16[32,128]{1,0:T(8,128)(2,1)S(1)}, bf16[4,64,128]{2,1,0:T(8,128)(2,1)S(1)}) custom-call(bf16[16,2,32,128]{3,2,1,0:T(8,128)(2,1)S(1)} %copy-done), custom_call_target="tpu_custom_call" | custom-call | bytes 1048576 | tf_op jit(solution)/shard_map/pallas_call | solution.py:17
  2.1 0.0 copy-start.1
  2.1 8.1 %all-to-all-start = ((bf16[8,16,16,128]{3,2,1,0:T(8,128)(2,1)}), bf16[8,16,16,128]{3,2,1,0:T(8,128)(2,1)S(1)}, u32[]{:S(2)}, u32[]{:S(2)}) async-start(bf16[8,16,16,128]{3,2,1,0:T(8,128)(2,1)} %get-tuple-element.15), calls=%async_computation | async-start | bytes 1048576 | tf_op jit(solution)/shard_map/all_to_all | solution.py:232
  10.2 4.4 %collective-permute-start.3 = (bf16[32,128]{1,0:T(8,128)(2,1)S(1)}, bf16[32,128]{1,0:T(8,128)(2,1)S(1)}, u32[]{:S(2)}, u32[]{:S(2)}) collective-permute-start(bf16[32,128]{1,0:T(8,128)(2,1)S(1)} %get-tuple-element.19), channel_id=1, source_target_pairs={{0,64},{64,128},{128,192},{192,256},{256,320},{320,384},{384,448},... | collective-permute-start | bytes 24584 | tf_op jit(solution)/shard_map/ppermute | solution.py:209
  14.6 1.9 %collective-permute-start.4 = (bf16[32,128]{1,0:T(8,128)(2,1)S(1)}, bf16[32,128]{1,0:T(8,128)(2,1)S(1)}, u32[]{:S(2)}, u32[]{:S(2)}) collective-permute-start(bf16[32,128]{1,0:T(8,128)(2,1)S(1)} %get-tuple-element.20), channel_id=1, source_target_pairs={{64,0},{128,64},{192,128},{256,192},{320,256},{384,320},{448,384},... | collective-permute-start | bytes 24584 | tf_op jit(solution)/shard_map/ppermute | solution.py:209
  16.5 0.0 copy-done.1
  16.5 0.2 shard_map.39.cols
  16.7 0.0 copy-start.3
  16.7 0.0 collective-permute-done.3.top
  16.7 3.7 %collective-permute-done.4.bottom = bf16[32,128]{1,0:T(8,128)(2,1)S(1)} collective-permute-done((bf16[32,128]{1,0:T(8,128)(2,1)S(1)}, bf16[32,128]{1,0:T(8,128)(2,1)S(1)}, u32[]{:S(2)}, u32[]{:S(2)}) %collective-permute-start.4) | collective-permute-done | bytes 8224 | tf_op jit(solution)/shard_map/ppermute | solution.py:209
  20.5 0.2 shard_map.40
  20.6 8.0 %collective-permute-start.5 = (bf16[40,128]{1,0:T(8,128)(2,1)S(1)}, bf16[40,128]{1,0:T(8,128)(2,1)S(1)}, u32[]{:S(2)}, u32[]{:S(2)}) collective-permute-start(bf16[40,128]{1,0:T(8,128)(2,1)S(1)} %shard_map.40), channel_id=1, source_target_pairs={{0,8},{8,16},{16,24},{24,32},{32,40},{40,48},{48,56},{1,9},{9,17},... | collective-permute-start | bytes 30728 | tf_op jit(solution)/shard_map/ppermute | solution.py:209
  28.6 2.1 %collective-permute-start.6 = (bf16[40,128]{1,0:T(8,128)(2,1)S(1)}, bf16[40,128]{1,0:T(8,128)(2,1)S(1)}, u32[]{:S(2)}, u32[]{:S(2)}) collective-permute-start(bf16[40,128]{1,0:T(8,128)(2,1)S(1)} %shard_map.40), channel_id=1, source_target_pairs={{8,0},{16,8},{24,16},{32,24},{40,32},{48,40},{56,48},{9,1},{17,9},... | collective-permute-start | bytes 30728 | tf_op jit(solution)/shard_map/ppermute | solution.py:209
  30.7 0.0 copy-done.3
  30.8 0.0 collective-permute-done.5.left
  30.8 6.2 %collective-permute-done.6.right = bf16[40,128]{1,0:T(8,128)(2,1)S(1)} collective-permute-done((bf16[40,128]{1,0:T(8,128)(2,1)S(1)}, bf16[40,128]{1,0:T(8,128)(2,1)S(1)}, u32[]{:S(2)}, u32[]{:S(2)}) %collective-permute-start.6) | collective-permute-done | bytes 10272 | tf_op jit(solution)/shard_map/ppermute | solution.py:209
  37.0 0.7 %shard_map.41 = bf16[8,80,128]{2,1,0:T(8,128)(2,1)} custom-call(bf16[4,64,128]{2,1,0:T(8,128)(2,1)S(1)} %get-tuple-element.18.edges, bf16[32,128]{1,0:T(8,128)(2,1)S(1)} %collective-permute-done.3.top, bf16[32,128]{1,0:T(8,128)(2,1)S(1)} %collective-permute-done.4.bottom, bf16[40,128]{1,0:T(8,128)(2,1)S(1)} %collective-permute-done.5.left, ...), custom_call_target="tpu_custom_call" | custom-call | bytes 262144 | tf_op jit(solution)/shard_map/pallas_call | solution.py:17
  37.7 0.0 copy-start.2
  37.7 0.0 all-to-all-done.slabs
  37.7 7.7 %all-to-all-start.1 = ((bf16[8,80,128]{2,1,0:T(8,128)(2,1)}), bf16[8,80,128]{2,1,0:T(8,128)(2,1)S(1)}, u32[]{:S(2)}, u32[]{:S(2)}) async-start(bf16[8,80,128]{2,1,0:T(8,128)(2,1)} %shard_map.41), calls=%async_computation.1 | async-start | bytes 327680 | tf_op jit(solution)/shard_map/all_to_all | solution.py:242
  45.5 0.1 copy.7
  45.6 0.0 copy-done.2
  45.6 1.9 %collective-permute-start = (bf16[448,128]{1,0:T(8,128)(2,1)S(1)}, bf16[448,128]{1,0:T(8,128)(2,1)S(1)}, u32[]{:S(2)}, u32[]{:S(2)}) collective-permute-start(bf16[448,128]{1,0:T(8,128)(2,1)S(1)} %fusion.1.f0), channel_id=1, source_target_pairs={{0,1},{1,0},{2,3},{3,2},{4,5},{5,4},{6,7},{7,6},{8,9},{9,8},{10,11... | collective-permute-start | bytes 344072 | tf_op jit(solution)/shard_map/ppermute | solution.py:221
  47.5 3.6 %collective-permute-start.1 = (bf16[448,128]{1,0:T(8,128)(2,1)S(1)}, bf16[448,128]{1,0:T(8,128)(2,1)S(1)}, u32[]{:S(2)}, u32[]{:S(2)}) collective-permute-start(bf16[448,128]{1,0:T(8,128)(2,1)S(1)} %fusion.1.f0), channel_id=1, source_target_pairs={{0,2},{1,3},{2,0},{3,1},{4,6},{5,7},{6,4},{7,5},{8,10},{9,11},{10,... | collective-permute-start | bytes 344072 | tf_op jit(solution)/shard_map/ppermute | solution.py:221
  51.2 2.3 %collective-permute-start.2 = (bf16[448,128]{1,0:T(8,128)(2,1)S(1)}, bf16[448,128]{1,0:T(8,128)(2,1)S(1)}, u32[]{:S(2)}, u32[]{:S(2)}) collective-permute-start(bf16[448,128]{1,0:T(8,128)(2,1)S(1)} %fusion.1.f0), channel_id=1, source_target_pairs={{0,3},{1,2},{2,1},{3,0},{4,7},{5,6},{6,5},{7,4},{8,11},{9,10},{10,... | collective-permute-start | bytes 344072 | tf_op jit(solution)/shard_map/ppermute | solution.py:221
  53.5 0.0 collective-permute-done.f1
  53.5 0.7 collective-permute-done.1.f2
  54.2 4.0 %collective-permute-done.2.f3 = bf16[448,128]{1,0:T(8,128)(2,1)S(1)} collective-permute-done((bf16[448,128]{1,0:T(8,128)(2,1)S(1)}, bf16[448,128]{1,0:T(8,128)(2,1)S(1)}, u32[]{:S(2)}, u32[]{:S(2)}) %collective-permute-start.2) | collective-permute-done | bytes 114720 | tf_op jit(solution)/shard_map/ppermute | solution.py:221
  58.2 1.1 %shard_map.38 = (f32[8,128,128]{2,1,0:T(8,128)S(1)}, bf16[384,768]{1,0:T(8,128)(2,1)S(1)}) custom-call(bf16[8,16,16,128]{3,2,1,0:T(8,128)(2,1)S(1)} %all-to-all-done.slabs, bf16[448,128]{1,0:T(8,128)(2,1)S(1)} %fusion.1.f0, bf16[448,128]{1,0:T(8,128)(2,1)S(1)} %collective-permute-done.f1, bf16[448,128]{1,0:T(8,128)(2,1)S(1)} %collective-permute-done.1.f2, ...), custom_call_target="tpu_custom_call" | custom-call | flops 603979776 | bytes 3145728 | tf_op jit(solution)/shard_map/pallas_call | solution.py:17
  59.3 0.0 all-to-all-done.1.halo
  59.3 0.9 %shard_map.42 = (bf16[16,16,128]{2,1,0:T(8,128)(2,1)S(1)}, bf16[16,16,128]{2,1,0:T(8,128)(2,1)S(1)}, bf16[16,16,128]{2,1,0:T(8,128)(2,1)S(1)}, bf16[16,16,128]{2,1,0:T(8,128)(2,1)S(1)}) custom-call(f32[8,128,128]{2,1,0:T(8,128)S(1)} %get-tuple-element.16.pre, bf16[384,768]{1,0:T(8,128)(2,1)S(1)} %get-tuple-element.17.taps, ...), custom_call_target="tpu_custom_call" | custom-call | flops 75497472 | bytes 2097152 | tf_op jit(solution)/shard_map/pallas_call | solution.py:17
  60.2 2.3 %collective-permute-start.7 = (bf16[16,16,128]{2,1,0:T(8,128)(2,1)S(1)}, bf16[16,16,128]{2,1,0:T(8,128)(2,1)S(1)}, u32[]{:S(2)}, u32[]{:S(2)}) collective-permute-start(bf16[16,16,128]{2,1,0:T(8,128)(2,1)S(1)} %get-tuple-element.22), channel_id=1, source_target_pairs={{0,1},{1,0},{2,3},{3,2},{4,5},{5,4},{6,7},{7,6},{8,9},{9,8},{10,11... | collective-permute-start | bytes 196616 | tf_op jit(solution)/shard_map/ppermute | solution.py:221
  62.5 2.3 %collective-permute-start.8 = (bf16[16,16,128]{2,1,0:T(8,128)(2,1)S(1)}, bf16[16,16,128]{2,1,0:T(8,128)(2,1)S(1)}, u32[]{:S(2)}, u32[]{:S(2)}) collective-permute-start(bf16[16,16,128]{2,1,0:T(8,128)(2,1)S(1)} %get-tuple-element.23), channel_id=1, source_target_pairs={{0,2},{1,3},{2,0},{3,1},{4,6},{5,7},{6,4},{7,5},{8,10},{9,11},{10,... | collective-permute-start | bytes 196616 | tf_op jit(solution)/shard_map/ppermute | solution.py:221
  64.8 3.2 %collective-permute-start.9 = (bf16[16,16,128]{2,1,0:T(8,128)(2,1)S(1)}, bf16[16,16,128]{2,1,0:T(8,128)(2,1)S(1)}, u32[]{:S(2)}, u32[]{:S(2)}) collective-permute-start(bf16[16,16,128]{2,1,0:T(8,128)(2,1)S(1)} %get-tuple-element.24), channel_id=1, source_target_pairs={{0,3},{1,2},{2,1},{3,0},{4,7},{5,6},{6,5},{7,4},{8,11},{9,10},{10,... | collective-permute-start | bytes 196616 | tf_op jit(solution)/shard_map/ppermute | solution.py:221
  68.1 0.0 collective-permute-done.7.g1
  68.1 0.0 collective-permute-done.8.g2
  68.1 2.7 %collective-permute-done.9.g3 = bf16[16,16,128]{2,1,0:T(8,128)(2,1)S(1)} collective-permute-done((bf16[16,16,128]{2,1,0:T(8,128)(2,1)S(1)}, bf16[16,16,128]{2,1,0:T(8,128)(2,1)S(1)}, u32[]{:S(2)}, u32[]{:S(2)}) %collective-permute-start.9) | collective-permute-done | bytes 65568 | tf_op jit(solution)/shard_map/ppermute | solution.py:221
  70.8 1.2 %shard_map.43 = bf16[16,2,32,128]{3,2,1,0:T(8,128)(2,1)} custom-call(bf16[16,16,128]{2,1,0:T(8,128)(2,1)S(1)} %get-tuple-element.21.g0, bf16[16,16,128]{2,1,0:T(8,128)(2,1)S(1)} %collective-permute-done.7.g1, bf16[16,16,128]{2,1,0:T(8,128)(2,1)S(1)} %collective-permute-done.8.g2, bf16[16,16,128]{2,1,0:T(8,128)(2,1)S(1)} %collective-permute-done.9.g3), custom_call_target="tpu_custom_call" | custom-call | bytes 524288 | tf_op jit(solution)/shard_map/pallas_call | solution.py:17
  (3 shorter events, 0.0 us)
Async XLA Ops:
  0.0 0.9 %copy-start = (bf16[16,2,32,128]{3,2,1,0:T(8,128)(2,1)S(1)}, bf16[16,2,32,128]{3,2,1,0:T(8,128)(2,1)}, u32[]{:S(2)}) copy-start(bf16[16,2,32,128]{3,2,1,0:T(8,128)(2,1)} %vol.3) | copy-start | bytes 786436
  2.1 14.4 %copy-start.1 = (bf16[16,2,32,128]{3,2,1,0:T(8,128)(2,1)S(1)}, bf16[16,2,32,128]{3,2,1,0:T(8,128)(2,1)}, u32[]{:S(2)}) copy-start(bf16[16,2,32,128]{3,2,1,0:T(8,128)(2,1)} %vol.3) | copy-start | bytes 786436
  2.1 35.6 %all-to-all-start = ((bf16[8,16,16,128]{3,2,1,0:T(8,128)(2,1)}), bf16[8,16,16,128]{3,2,1,0:T(8,128)(2,1)S(1)}, u32[]{:S(2)}, u32[]{:S(2)}) async-start(bf16[8,16,16,128]{3,2,1,0:T(8,128)(2,1)} %get-tuple-element.15), calls=%async_computation | async-start | bytes 1048576 | tf_op jit(solution)/shard_map/all_to_all | solution.py:232
  10.2 6.6 %collective-permute-start.3 = (bf16[32,128]{1,0:T(8,128)(2,1)S(1)}, bf16[32,128]{1,0:T(8,128)(2,1)S(1)}, u32[]{:S(2)}, u32[]{:S(2)}) collective-permute-start(bf16[32,128]{1,0:T(8,128)(2,1)S(1)} %get-tuple-element.19), channel_id=1, source_target_pairs={{0,64},{64,128},{128,192},{192,256},{256,320},{320,384},{384,448},... | collective-permute-start | bytes 24584 | tf_op jit(solution)/shard_map/ppermute | solution.py:209
  14.6 5.9 %collective-permute-start.4 = (bf16[32,128]{1,0:T(8,128)(2,1)S(1)}, bf16[32,128]{1,0:T(8,128)(2,1)S(1)}, u32[]{:S(2)}, u32[]{:S(2)}) collective-permute-start(bf16[32,128]{1,0:T(8,128)(2,1)S(1)} %get-tuple-element.20), channel_id=1, source_target_pairs={{64,0},{128,64},{192,128},{256,192},{320,256},{384,320},{448,384},... | collective-permute-start | bytes 24584 | tf_op jit(solution)/shard_map/ppermute | solution.py:209
  16.7 14.0 %copy-start.3 = (f32[16]{0:T(128)S(1)}, f32[16]{0:T(128)}, u32[]{:S(2)}) copy-start(f32[16]{0:T(128)} %param.5) | copy-start | bytes 196
  20.6 10.1 %collective-permute-start.5 = (bf16[40,128]{1,0:T(8,128)(2,1)S(1)}, bf16[40,128]{1,0:T(8,128)(2,1)S(1)}, u32[]{:S(2)}, u32[]{:S(2)}) collective-permute-start(bf16[40,128]{1,0:T(8,128)(2,1)S(1)} %shard_map.40), channel_id=1, source_target_pairs={{0,8},{8,16},{16,24},{24,32},{32,40},{40,48},{48,56},{1,9},{9,17},... | collective-permute-start | bytes 30728 | tf_op jit(solution)/shard_map/ppermute | solution.py:209
  28.6 8.4 %collective-permute-start.6 = (bf16[40,128]{1,0:T(8,128)(2,1)S(1)}, bf16[40,128]{1,0:T(8,128)(2,1)S(1)}, u32[]{:S(2)}, u32[]{:S(2)}) collective-permute-start(bf16[40,128]{1,0:T(8,128)(2,1)S(1)} %shard_map.40), channel_id=1, source_target_pairs={{8,0},{16,8},{24,16},{32,24},{40,32},{48,40},{56,48},{9,1},{17,9},... | collective-permute-start | bytes 30728 | tf_op jit(solution)/shard_map/ppermute | solution.py:209
  37.7 7.8 %copy-start.2 = (bf16[16,128,3,3,3]{1,0,4,3,2:T(8,128)(2,1)S(1)}, bf16[16,128,3,3,3]{1,0,4,3,2:T(8,128)(2,1)}, u32[]{:S(2)}) copy-start(bf16[16,128,3,3,3]{1,0,4,3,2:T(8,128)(2,1)} %param.4) | copy-start | bytes 331780
  37.7 21.6 %all-to-all-start.1 = ((bf16[8,80,128]{2,1,0:T(8,128)(2,1)}), bf16[8,80,128]{2,1,0:T(8,128)(2,1)S(1)}, u32[]{:S(2)}, u32[]{:S(2)}) async-start(bf16[8,80,128]{2,1,0:T(8,128)(2,1)} %shard_map.41), calls=%async_computation.1 | async-start | bytes 327680 | tf_op jit(solution)/shard_map/all_to_all | solution.py:242
  45.6 7.9 %collective-permute-start = (bf16[448,128]{1,0:T(8,128)(2,1)S(1)}, bf16[448,128]{1,0:T(8,128)(2,1)S(1)}, u32[]{:S(2)}, u32[]{:S(2)}) collective-permute-start(bf16[448,128]{1,0:T(8,128)(2,1)S(1)} %fusion.1.f0), channel_id=1, source_target_pairs={{0,1},{1,0},{2,3},{3,2},{4,5},{5,4},{6,7},{7,6},{8,9},{9,8},{10,11... | collective-permute-start | bytes 344072 | tf_op jit(solution)/shard_map/ppermute | solution.py:221
  47.5 6.7 %collective-permute-start.1 = (bf16[448,128]{1,0:T(8,128)(2,1)S(1)}, bf16[448,128]{1,0:T(8,128)(2,1)S(1)}, u32[]{:S(2)}, u32[]{:S(2)}) collective-permute-start(bf16[448,128]{1,0:T(8,128)(2,1)S(1)} %fusion.1.f0), channel_id=1, source_target_pairs={{0,2},{1,3},{2,0},{3,1},{4,6},{5,7},{6,4},{7,5},{8,10},{9,11},{10,... | collective-permute-start | bytes 344072 | tf_op jit(solution)/shard_map/ppermute | solution.py:221
  51.2 7.0 %collective-permute-start.2 = (bf16[448,128]{1,0:T(8,128)(2,1)S(1)}, bf16[448,128]{1,0:T(8,128)(2,1)S(1)}, u32[]{:S(2)}, u32[]{:S(2)}) collective-permute-start(bf16[448,128]{1,0:T(8,128)(2,1)S(1)} %fusion.1.f0), channel_id=1, source_target_pairs={{0,3},{1,2},{2,1},{3,0},{4,7},{5,6},{6,5},{7,4},{8,11},{9,10},{10,... | collective-permute-start | bytes 344072 | tf_op jit(solution)/shard_map/ppermute | solution.py:221
  60.2 7.9 %collective-permute-start.7 = (bf16[16,16,128]{2,1,0:T(8,128)(2,1)S(1)}, bf16[16,16,128]{2,1,0:T(8,128)(2,1)S(1)}, u32[]{:S(2)}, u32[]{:S(2)}) collective-permute-start(bf16[16,16,128]{2,1,0:T(8,128)(2,1)S(1)} %get-tuple-element.22), channel_id=1, source_target_pairs={{0,1},{1,0},{2,3},{3,2},{4,5},{5,4},{6,7},{7,6},{8,9},{9,8},{10,11... | collective-permute-start | bytes 196616 | tf_op jit(solution)/shard_map/ppermute | solution.py:221
  62.5 5.6 %collective-permute-start.8 = (bf16[16,16,128]{2,1,0:T(8,128)(2,1)S(1)}, bf16[16,16,128]{2,1,0:T(8,128)(2,1)S(1)}, u32[]{:S(2)}, u32[]{:S(2)}) collective-permute-start(bf16[16,16,128]{2,1,0:T(8,128)(2,1)S(1)} %get-tuple-element.23), channel_id=1, source_target_pairs={{0,2},{1,3},{2,0},{3,1},{4,6},{5,7},{6,4},{7,5},{8,10},{9,11},{10,... | collective-permute-start | bytes 196616 | tf_op jit(solution)/shard_map/ppermute | solution.py:221
  64.8 6.0 %collective-permute-start.9 = (bf16[16,16,128]{2,1,0:T(8,128)(2,1)S(1)}, bf16[16,16,128]{2,1,0:T(8,128)(2,1)S(1)}, u32[]{:S(2)}, u32[]{:S(2)}) collective-permute-start(bf16[16,16,128]{2,1,0:T(8,128)(2,1)S(1)} %get-tuple-element.24), channel_id=1, source_target_pairs={{0,3},{1,2},{2,1},{3,0},{4,7},{5,6},{6,5},{7,4},{8,11},{9,10},{10,... | collective-permute-start | bytes 196616 | tf_op jit(solution)/shard_map/ppermute | solution.py:221

commit v3 on v0

v3 whole, which is shorter than its diff:
```python
import jax
import jax.numpy as jnp
from jax import lax
from jax.experimental import pallas as pl
from jax.experimental.pallas import tpu as pltpu
from jax.sharding import PartitionSpec as P


BF = jnp.bfloat16
F32 = jnp.float32
GRANT = 16 << 20


def call(kernel, out_shapes, scratch, *args, flops=0, moved=0):
    vmem = pl.BlockSpec(memory_space=pltpu.VMEM)
    many = isinstance(out_shapes, (list, tuple))
    return pl.pallas_call(
        kernel,
        out_shape=out_shapes,
        in_specs=[vmem] * len(args),
        out_specs=[vmem] * len(out_shapes) if many else vmem,
        scratch_shapes=scratch,
        cost_estimate=pl.CostEstimate(flops=flops, bytes_accessed=moved, transcendentals=0),
        compiler_params=pltpu.CompilerParams(vmem_limit_bytes=GRANT),
    )(*args)


def shaped(*shape, dtype=BF):
    return jax.ShapeDtypeStruct(shape, dtype)


def lanes_of(shape):
    return lax.broadcasted_iota(jnp.int32, shape, len(shape) - 1)


def pack_kernel(vol, field, first, last, flat):
    flat[...] = vol[...].reshape(1024, 128).astype(F32)
    for z in range(2):
        for row in range(32):
            tile = flat[pl.ds(z * 32 + row, 16, stride=64), :].astype(BF)
            field[z * 32 + row] = tile
            if row == 0:
                first[pl.ds(z * 16, 16)] = tile
            if row == 31:
                last[pl.ds(z * 16, 16)] = tile


def columns_kernel(vol, cols):
    lane = lanes_of((32, 128))
    both = jnp.zeros((32, 128), F32)
    for z in range(2):
        for c in range(16):
            tile = vol[c, z].astype(F32)
            j = z * 16 + c
            both = jnp.where(lane == j, pltpu.roll(tile, j, 1) if j else tile, both)
            both = jnp.where(lane == 32 + j, pltpu.roll(tile, 33 + j, 1), both)
    cols[...] = both


def corner_kernel(cols, top, bottom, side, buf):
    both = jnp.concatenate(
        [top[...].astype(F32), bottom[...].astype(F32), jnp.zeros((64, 128), F32)], axis=0
    )
    turned = both.T
    first, last = turned[0:1, :], turned[127:128, :]
    lane = lanes_of((1, 128))
    buf[...] = jnp.zeros((40, 128), F32)
    buf[pl.ds(1, 32), :] = cols[...]
    buf[pl.ds(0, 1), :] = jnp.where(lane < 32, first, pltpu.roll(last, 32, 1))
    buf[pl.ds(33, 1), :] = jnp.where(lane < 32, pltpu.roll(first, 96, 1), last)
    side[...] = buf[...].astype(BF)


def halo_kernel(top, bottom, sides, out):
    me, size = lax.axis_index("sy"), lax.axis_size("sy")
    left = sides[jnp.maximum(me - 1, 0)].astype(F32)
    right = sides[jnp.minimum(me + 1, size - 1)].astype(F32)
    lane = lanes_of((40, 128))
    nothing = jnp.zeros((40, 128), F32)
    beside = jnp.where(
        lane < 32,
        jnp.where(me > 0, pltpu.roll(left, 96, 1), nothing),
        jnp.where(me < size - 1, pltpu.roll(right, 32, 1), nothing),
    )
    both = jnp.where(lanes_of((24, 128)) < 64, beside[0:24], pltpu.roll(beside[16:40], 64, 1)).astype(BF)
    for d in range(8):
        out[d, pl.ds(0, 32)] = top[...]
        out[d, pl.ds(32, 32)] = bottom[...]
        out[d, pl.ds(64, 24)] = both


def taps_kernel(own, taps):
    me = lax.axis_index("ch")
    chip, core = me // 2, lax.rem(me, 2)
    lane = lanes_of((16, 128))
    turned = []
    for tap in range(27):
        tile = pltpu.roll(own[pl.ds(tap * 16, 16)].astype(F32), lax.rem(128 - 32 * chip, 128), 1)
        other = jnp.where(lax.rem(lane // 16, 2) == 0, pltpu.roll(tile, 112, 1), pltpu.roll(tile, 16, 1))
        turned.append(jnp.where(core == 1, other, tile).astype(BF))
    for b in range(3):
        for e in range(3):
            for zo in range(2):
                for zi in range(2):
                    tile = turned[(zi - zo + 1) * 9 + b * 3 + e]
                    taps[pl.ds(((b * 3 + e) * 2 + zo) * 16, 16), pl.ds(zi * 128, 128)] = tile


def conv_kernel(p0, p1, p2, p3, p4, p5, p6, p7, halo, taps, bias, out, sums, flat):
    pieces = (p0, p1, p2, p3, p4, p5, p6, p7)
    me = lax.axis_index("ch")
    chip, core = me // 2, lax.rem(me, 2)
    sources = [2 * lax.rem(chip + j // 2, 4) + (core ^ (j % 2)) for j in range(8)]
    lane40 = lanes_of((40, 128))
    total = [[jnp.zeros((40, 128), F32) for _ in range(2)] for _ in range(2)]
    for j, source in enumerate(sources):
        both = halo[source, pl.ds(64, 24)].astype(F32)
        both = jnp.concatenate([both, pltpu.roll(both[8:24], 64, 1)], axis=0)
        for side in range(2):
            for z in range(2):
                shift = (j * 16 - side * 32 - z * 16) % 128
                piece = pltpu.roll(both, shift, 1) if shift else both
                total[side][z] = jnp.where(lane40 // 16 == j, piece, total[side][z])
    beside = jnp.concatenate(
        [jnp.concatenate(total[0], axis=1), jnp.concatenate(total[1], axis=1), jnp.zeros((48, 256), F32)], axis=0
    ).astype(BF)
    edge = lax.dot_general(taps[...], beside, (((1,), (1,)), ((), ())), preferred_element_type=F32)
    ends = [
        edge[e * 32 : e * 32 + 32]
        + pltpu.roll(edge[96 + e * 32 : 128 + e * 32], 127, 1)
        + pltpu.roll(edge[192 + e * 32 : 224 + e * 32], 126, 1)
        for e in (0, 2)
    ]
    offset = jnp.concatenate([bias[...], bias[...]], axis=0)
    lane = lanes_of((32, 128))

    def row_of(at):
        if at == 0 or at == 33:
            below = 32 if at else 0
            return jnp.concatenate(
                [halo[source, pl.ds(below + z * 16, 16)] for z in range(2) for source in sources], axis=0
            )
        return jnp.concatenate([piece[z * 32 + at - 1] for z in range(2) for piece in pieces], axis=0)

    for p in range(17):
        pair = jnp.concatenate([row_of(2 * p), row_of(2 * p + 1)], axis=1)
        got = jnp.dot(taps[...], pair, preferred_element_type=F32)
        for h in range(2):
            for b in range(3):
                row = 2 * p + h - b
                if not 0 <= row < 32:
                    continue
                part = got[b * 96 : (b + 1) * 96, h * 128 : (h + 1) * 128]
                if b == 0:
                    sums[row] = part
                    continue
                part = part + sums[row]
                if b == 1:
                    sums[row] = part
                    continue
                pre = part[32:64] + jnp.where(lane == 0, ends[0][:, row : row + 1], pltpu.roll(part[0:32], 1, 1))
                pre = pre + jnp.where(
                    lane == 127, ends[1][:, 40 + row : 41 + row], pltpu.roll(part[64:96], 127, 1)
                )
                pre = pre + offset
                pre = jnp.where(pre >= 0, pre, 0.3 * pre)
                for z in range(2):
                    flat[pl.ds(z * 32 + row, 16, stride=64), :] = pre[z * 16 : z * 16 + 16]
    out[...] = flat[...].reshape(16, 2, 32, 128).astype(BF)


def shifts(array, axis, up=True):
    size = lax.axis_size(axis)
    pairs = [(i, i + 1) for i in range(size - 1)]
    return lax.ppermute(array, axis, pairs if up else [(j, i) for i, j in pairs])


def cyclic(array, step):
    return lax.ppermute(array, "ch", [(d, (d + step) % 8) for d in range(8)])


def partner(array):
    return lax.ppermute(array, "ch", [(d, d ^ 1) for d in range(8)])


def stages(volume, weights, bias):
    field, first, last = call(
        pack_kernel,
        [shaped(64, 16, 128), shaped(32, 128), shaped(32, 128)],
        [pltpu.VMEM((1024, 128), F32)],
        volume,
        moved=1 << 20,
    )
    z4 = cyclic(field, 4)
    z2 = cyclic(field, 2)
    z6 = cyclic(field, 6)
    top = shifts(last, "sx", True)
    bottom = shifts(first, "sx", False)
    cols = call(columns_kernel, shaped(32, 128, dtype=F32), [], volume, moved=1 << 19)
    side = call(corner_kernel, shaped(40, 128), [pltpu.VMEM((40, 128), F32)], cols, top, bottom, moved=1 << 16)
    sides = lax.all_to_all(jnp.broadcast_to(side, (8, 40, 128)), "sy", split_axis=0, concat_axis=0, tiled=True)
    own = weights.transpose(2, 3, 4, 0, 1).reshape(432, 128)
    taps = call(taps_kernel, shaped(288, 256), [], own, moved=1 << 19)
    spread = jnp.broadcast_to(bias[:, None], (16, 128))
    halo = call(halo_kernel, shaped(8, 88, 128), [], top, bottom, sides, moved=1 << 18)
    halo = lax.all_to_all(halo, "ch", split_axis=0, concat_axis=0, tiled=True)
    f0 = partner(field)
    f4 = partner(z4)
    f2 = partner(z2)
    f6 = partner(z6)
    return call(
        conv_kernel,
        shaped(16, 2, 32, 128),
        [pltpu.VMEM((32, 96, 128), F32), pltpu.VMEM((1024, 128), F32)],
        field,
        f0,
        z6,
        f6,
        z4,
        f4,
        z2,
        f2,
        halo,
        taps,
        spread,
        flops=2 * 288 * 256 * 34 * 128,
        moved=3 << 20,
    )


def solution(mesh):
    in_specs = (P("ch", None, "sx", "sy"), P("ch", None, None, None, None), P("ch"))
    out_specs = P("ch", None, "sx", "sy")
    return jax.shard_map(stages, mesh=mesh, in_specs=in_specs, out_specs=out_specs, check_vma=False)
```

time: 116 us -> 64.4 us (0.56)
  the two profiles are of different devices: /device:TPU:28 before, /device:TPU:25 now
where the time goes in v3:
time: 64.4 us; the launch traced here: 63.9 us
  starting transfers between devices  34.6 us (54%)
  blocking collectives  19.6 us (30%)
  waiting for transfers between devices  4.48 us (7%)
  Pallas kernels  3.88 us (6%)
  local copies, waits for them, and re-layouts  1.07 us (2%)
    all_to_all x1, blocking collectives, stages(): lax.all_to_all(jnp.broadcast_to(side, (8, 40, 128)), 'sy', split_axis=0,...  19.6 us
    ppermute x3, starting transfers between devices, cyclic(): return lax.ppermute(array, 'ch', [(d, (d + step) % 8) for d in range(8)])  12 us
    ppermute x4, starting transfers between devices, partner(): return lax.ppermute(array, 'ch', [(d, d ^ 1) for d in range(8)])  8.64 us
    all_to_all x1, starting transfers between devices, stages(): halo = lax.all_to_all(halo, 'ch', split_axis=0, concat_axis=0, tiled=True)  7.66 us
    ppermute x2, starting transfers between devices, shifts(): lax.ppermute(array, axis, pairs if up else [(j, i) for i, j in pairs])  6.34 us
    pallas_call x6, Pallas kernels, call(): pl.pallas_call(kernel, out_shape=out_shapes, in_specs=[vmem] * len(args),...  3.88 us
    ppermute x2, waiting for transfers between devices, shifts(): lax.ppermute(array, axis, pairs if up else [(j, i) for i, j in pairs])  3.6 us
  transfers between devices with their start and end apart: 10, of which 2 were waited for; matrix products, arithmetic and copies ran while one was open for 0% of the time, Pallas kernels for 2%

profile of v3, /device:TPU:25, one launch (start us, length us, event | category | flops | bytes accessed | tf_op | source)
XLA Modules:
  0.0 63.9 jit_solution(5076505094135023397)
XLA Ops:
  0.0 0.0 copy-start
  0.0 0.9 %copy-done = bf16[16,2,32,128]{3,2,1,0:T(8,128)(2,1)S(1)} copy-done((bf16[16,2,32,128]{3,2,1,0:T(8,128)(2,1)S(1)}, bf16[16,2,32,128]{3,2,1,0:T(8,128)(2,1)}, u32[]{:S(2)}) %copy-start) | copy-done | bytes 262168
  1.0 0.3 shard_map.37
  1.3 4.0 %collective-permute-start.5 = (bf16[64,16,128]{2,1,0:T(8,128)(2,1)S(1)}, bf16[64,16,128]{2,1,0:T(8,128)(2,1)S(1)}, u32[]{:S(2)}, u32[]{:S(2)}) collective-permute-start(bf16[64,16,128]{2,1,0:T(8,128)(2,1)S(1)} %get-tuple-element.8.p0), channel_id=1, source_target_pairs={{0,2},{1,3},{2,4},{3,5},{4,6},{5,7},{6,0},{7,1},{8,10},{9,11},{10,... | collective-permute-start | bytes 786440 | tf_op jit(solution)/shard_map/ppermute | solution.py:179
  5.3 5.8 %collective-permute-start.3 = (bf16[64,16,128]{2,1,0:T(8,128)(2,1)S(1)}, bf16[64,16,128]{2,1,0:T(8,128)(2,1)S(1)}, u32[]{:S(2)}, u32[]{:S(2)}) collective-permute-start(bf16[64,16,128]{2,1,0:T(8,128)(2,1)S(1)} %get-tuple-element.8.p0), channel_id=1, source_target_pairs={{0,4},{1,5},{2,6},{3,7},{4,0},{5,1},{6,2},{7,3},{8,12},{9,13},{10,... | collective-permute-start | bytes 786440 | tf_op jit(solution)/shard_map/ppermute | solution.py:179
  11.1 2.2 %collective-permute-start.1 = (bf16[64,16,128]{2,1,0:T(8,128)(2,1)S(1)}, bf16[64,16,128]{2,1,0:T(8,128)(2,1)S(1)}, u32[]{:S(2)}, u32[]{:S(2)}) collective-permute-start(bf16[64,16,128]{2,1,0:T(8,128)(2,1)S(1)} %get-tuple-element.8.p0), channel_id=1, source_target_pairs={{0,6},{1,7},{2,0},{3,1},{4,2},{5,3},{6,4},{7,5},{8,14},{9,15},{10,... | collective-permute-start | bytes 786440 | tf_op jit(solution)/shard_map/ppermute | solution.py:179
  13.3 4.4 %collective-permute-start.7 = (bf16[32,128]{1,0:T(8,128)(2,1)S(1)}, bf16[32,128]{1,0:T(8,128)(2,1)S(1)}, u32[]{:S(2)}, u32[]{:S(2)}) collective-permute-start(bf16[32,128]{1,0:T(8,128)(2,1)S(1)} %get-tuple-element.9), channel_id=1, source_target_pairs={{0,64},{64,128},{128,192},{192,256},{256,320},{320,384},{384,448},... | collective-permute-start | bytes 24584 | tf_op jit(solution)/shard_map/ppermute | solution.py:175
  17.7 1.9 %collective-permute-start.8 = (bf16[32,128]{1,0:T(8,128)(2,1)S(1)}, bf16[32,128]{1,0:T(8,128)(2,1)S(1)}, u32[]{:S(2)}, u32[]{:S(2)}) collective-permute-start(bf16[32,128]{1,0:T(8,128)(2,1)S(1)} %get-tuple-element.10), channel_id=1, source_target_pairs={{64,0},{128,64},{192,128},{256,192},{320,256},{384,320},{448,384},... | collective-permute-start | bytes 24584 | tf_op jit(solution)/shard_map/ppermute | solution.py:175
  19.6 0.2 shard_map.38.cols
  19.9 0.0 collective-permute-done.7.top
  19.9 3.6 %collective-permute-done.8.bottom = bf16[32,128]{1,0:T(8,128)(2,1)S(1)} collective-permute-done((bf16[32,128]{1,0:T(8,128)(2,1)S(1)}, bf16[32,128]{1,0:T(8,128)(2,1)S(1)}, u32[]{:S(2)}, u32[]{:S(2)}) %collective-permute-start.8) | collective-permute-done | bytes 8224 | tf_op jit(solution)/shard_map/ppermute | solution.py:175
  23.5 0.2 shard_map.39
  23.7 19.6 %all_to_all.10.sides = bf16[8,40,128]{2,1,0:T(8,128)(2,1)S(1)} all-to-all(bf16[8,40,128]{2,1,0:T(8,128)(2,1)S(1)} %broadcast_in_dim.4), channel_id=1, replica_groups=mesh['sx'=8,'sy'=8,'ch'=8] {'sy'}, dimensions={0} | all-to-all | bytes 163840 | tf_op jit(solution)/shard_map/all_to_all | solution.py:201
  43.3 0.8 %shard_map.40 = bf16[8,88,128]{2,1,0:T(8,128)(2,1)} custom-call(bf16[32,128]{1,0:T(8,128)(2,1)S(1)} %collective-permute-done.7.top, bf16[32,128]{1,0:T(8,128)(2,1)S(1)} %collective-permute-done.8.bottom, bf16[8,40,128]{2,1,0:T(8,128)(2,1)S(1)} %all_to_all.10.sides), custom_call_target="tpu_custom_call" | custom-call | bytes 262144 | tf_op jit(solution)/shard_map/pallas_call | solution.py:17
  44.1 0.0 copy-start.1
  44.1 7.7 %all-to-all-start.1 = ((bf16[8,88,128]{2,1,0:T(8,128)(2,1)}), bf16[8,88,128]{2,1,0:T(8,128)(2,1)S(1)}, u32[]{:S(2)}, u32[]{:S(2)}) async-start(bf16[8,88,128]{2,1,0:T(8,128)(2,1)} %shard_map.40), calls=%async_computation.1 | async-start | bytes 360448 | tf_op jit(solution)/shard_map/all_to_all | solution.py:206
  51.8 2.0 %collective-permute-start = (bf16[64,16,128]{2,1,0:T(8,128)(2,1)S(1)}, bf16[64,16,128]{2,1,0:T(8,128)(2,1)S(1)}, u32[]{:S(2)}, u32[]{:S(2)}) collective-permute-start(bf16[64,16,128]{2,1,0:T(8,128)(2,1)S(1)} %get-tuple-element.8.p0), channel_id=1, source_target_pairs={{0,1},{1,0},{2,3},{3,2},{4,5},{5,4},{6,7},{7,6},{8,9},{9,8},{10,11... | collective-permute-start | bytes 786440 | tf_op jit(solution)/shard_map/ppermute | solution.py:183
  53.8 0.0 collective-permute-done.5.p6
  53.8 2.3 %collective-permute-start.6 = (bf16[64,16,128]{2,1,0:T(8,128)(2,1)S(1)}, bf16[64,16,128]{2,1,0:T(8,128)(2,1)S(1)}, u32[]{:S(2)}, u32[]{:S(2)}) collective-permute-start(bf16[64,16,128]{2,1,0:T(8,128)(2,1)S(1)} %collective-permute-done.5.p6), channel_id=1, source_target_pairs={{0,1},{1,0},{2,3},{3,2},{4,5},{5,4},{6,7},{7,6},{8,9},{9,8},{10,11... | collective-permute-start | bytes 786440 | tf_op jit(solution)/shard_map/ppermute | solution.py:183
  56.1 0.0 collective-permute-done.3.p4
  56.2 2.0 %collective-permute-start.4 = (bf16[64,16,128]{2,1,0:T(8,128)(2,1)S(1)}, bf16[64,16,128]{2,1,0:T(8,128)(2,1)S(1)}, u32[]{:S(2)}, u32[]{:S(2)}) collective-permute-start(bf16[64,16,128]{2,1,0:T(8,128)(2,1)S(1)} %collective-permute-done.3.p4), channel_id=1, source_target_pairs={{0,1},{1,0},{2,3},{3,2},{4,5},{5,4},{6,7},{7,6},{8,9},{9,8},{10,11... | collective-permute-start | bytes 786440 | tf_op jit(solution)/shard_map/ppermute | solution.py:183
  58.2 0.0 collective-permute-done.1.p2
  58.2 2.3 %collective-permute-start.2 = (bf16[64,16,128]{2,1,0:T(8,128)(2,1)S(1)}, bf16[64,16,128]{2,1,0:T(8,128)(2,1)S(1)}, u32[]{:S(2)}, u32[]{:S(2)}) collective-permute-start(bf16[64,16,128]{2,1,0:T(8,128)(2,1)S(1)} %collective-permute-done.1.p2), channel_id=1, source_target_pairs={{0,1},{1,0},{2,3},{3,2},{4,5},{5,4},{6,7},{7,6},{8,9},{9,8},{10,11... | collective-permute-start | bytes 786440 | tf_op jit(solution)/shard_map/ppermute | solution.py:183
  60.5 0.0 copy-done.1
  60.5 0.0 copy-start.2
  60.5 0.2 shard_map.41.taps
  60.7 0.0 collective-permute-done.p1
  60.8 0.0 all-to-all-done.1.halo
  60.8 0.0 collective-permute-done.6.p7
  60.8 0.0 collective-permute-done.4.p5
  60.8 0.9 %collective-permute-done.2.p3 = bf16[64,16,128]{2,1,0:T(8,128)(2,1)S(1)} collective-permute-done((bf16[64,16,128]{2,1,0:T(8,128)(2,1)S(1)}, bf16[64,16,128]{2,1,0:T(8,128)(2,1)S(1)}, u32[]{:S(2)}, u32[]{:S(2)}) %collective-permute-start.2) | collective-permute-done | bytes 262176 | tf_op jit(solution)/shard_map/ppermute | solution.py:183
  61.6 0.0 copy-done.2
  61.6 0.1 broadcast_in_dim.10.bias
  61.7 2.2 %shard_map.42 = bf16[16,2,32,128]{3,2,1,0:T(8,128)(2,1)} custom-call(bf16[64,16,128]{2,1,0:T(8,128)(2,1)S(1)} %get-tuple-element.8.p0, bf16[64,16,128]{2,1,0:T(8,128)(2,1)S(1)} %collective-permute-done.p1, bf16[64,16,128]{2,1,0:T(8,128)(2,1)S(1)} %collective-permute-done.1.p2, bf16[64,16,128]{2,1,0:T(8,128)(2,1)S(1)} %collective-permute-done.2.p3, ...), custom_call_target="tpu_custom_call" | custom-call | flops 641728512 | bytes 3145728 | tf_op jit(solution)/shard_map/pallas_call | solution.py:17
  (1 shorter events, 0.0 us)
Async XLA Ops:
  0.0 0.9 %copy-start = (bf16[16,2,32,128]{3,2,1,0:T(8,128)(2,1)S(1)}, bf16[16,2,32,128]{3,2,1,0:T(8,128)(2,1)}, u32[]{:S(2)}) copy-start(bf16[16,2,32,128]{3,2,1,0:T(8,128)(2,1)} %vol.3) | copy-start | bytes 786436
  1.3 52.5 %collective-permute-start.5 = (bf16[64,16,128]{2,1,0:T(8,128)(2,1)S(1)}, bf16[64,16,128]{2,1,0:T(8,128)(2,1)S(1)}, u32[]{:S(2)}, u32[]{:S(2)}) collective-permute-start(bf16[64,16,128]{2,1,0:T(8,128)(2,1)S(1)} %get-tuple-element.8.p0), channel_id=1, source_target_pairs={{0,2},{1,3},{2,4},{3,5},{4,6},{5,7},{6,0},{7,1},{8,10},{9,11},{10,... | collective-permute-start | bytes 786440 | tf_op jit(solution)/shard_map/ppermute | solution.py:179
  5.3 50.9 %collective-permute-start.3 = (bf16[64,16,128]{2,1,0:T(8,128)(2,1)S(1)}, bf16[64,16,128]{2,1,0:T(8,128)(2,1)S(1)}, u32[]{:S(2)}, u32[]{:S(2)}) collective-permute-start(bf16[64,16,128]{2,1,0:T(8,128)(2,1)S(1)} %get-tuple-element.8.p0), channel_id=1, source_target_pairs={{0,4},{1,5},{2,6},{3,7},{4,0},{5,1},{6,2},{7,3},{8,12},{9,13},{10,... | collective-permute-start | bytes 786440 | tf_op jit(solution)/shard_map/ppermute | solution.py:179
  11.1 47.1 %collective-permute-start.1 = (bf16[64,16,128]{2,1,0:T(8,128)(2,1)S(1)}, bf16[64,16,128]{2,1,0:T(8,128)(2,1)S(1)}, u32[]{:S(2)}, u32[]{:S(2)}) collective-permute-start(bf16[64,16,128]{2,1,0:T(8,128)(2,1)S(1)} %get-tuple-element.8.p0), channel_id=1, source_target_pairs={{0,6},{1,7},{2,0},{3,1},{4,2},{5,3},{6,4},{7,5},{8,14},{9,15},{10,... | collective-permute-start | bytes 786440 | tf_op jit(solution)/shard_map/ppermute | solution.py:179
  13.3 6.6 %collective-permute-start.7 = (bf16[32,128]{1,0:T(8,128)(2,1)S(1)}, bf16[32,128]{1,0:T(8,128)(2,1)S(1)}, u32[]{:S(2)}, u32[]{:S(2)}) collective-permute-start(bf16[32,128]{1,0:T(8,128)(2,1)S(1)} %get-tuple-element.9), channel_id=1, source_target_pairs={{0,64},{64,128},{128,192},{192,256},{256,320},{320,384},{384,448},... | collective-permute-start | bytes 24584 | tf_op jit(solution)/shard_map/ppermute | solution.py:175
  17.7 5.7 %collective-permute-start.8 = (bf16[32,128]{1,0:T(8,128)(2,1)S(1)}, bf16[32,128]{1,0:T(8,128)(2,1)S(1)}, u32[]{:S(2)}, u32[]{:S(2)}) collective-permute-start(bf16[32,128]{1,0:T(8,128)(2,1)S(1)} %get-tuple-element.10), channel_id=1, source_target_pairs={{64,0},{128,64},{192,128},{256,192},{320,256},{384,320},{448,384},... | collective-permute-start | bytes 24584 | tf_op jit(solution)/shard_map/ppermute | solution.py:175
  44.1 16.4 %copy-start.1 = (bf16[16,128,3,3,3]{1,0,4,3,2:T(8,128)(2,1)S(1)}, bf16[16,128,3,3,3]{1,0,4,3,2:T(8,128)(2,1)}, u32[]{:S(2)}) copy-start(bf16[16,128,3,3,3]{1,0,4,3,2:T(8,128)(2,1)} %param.4) | copy-start | bytes 331780
  44.1 16.6 %all-to-all-start.1 = ((bf16[8,88,128]{2,1,0:T(8,128)(2,1)}), bf16[8,88,128]{2,1,0:T(8,128)(2,1)S(1)}, u32[]{:S(2)}, u32[]{:S(2)}) async-start(bf16[8,88,128]{2,1,0:T(8,128)(2,1)} %shard_map.40), calls=%async_computation.1 | async-start | bytes 360448 | tf_op jit(solution)/shard_map/all_to_all | solution.py:206
  51.8 8.9 %collective-permute-start = (bf16[64,16,128]{2,1,0:T(8,128)(2,1)S(1)}, bf16[64,16,128]{2,1,0:T(8,128)(2,1)S(1)}, u32[]{:S(2)}, u32[]{:S(2)}) collective-permute-start(bf16[64,16,128]{2,1,0:T(8,128)(2,1)S(1)} %get-tuple-element.8.p0), channel_id=1, source_target_pairs={{0,1},{1,0},{2,3},{3,2},{4,5},{5,4},{6,7},{7,6},{8,9},{9,8},{10,11... | collective-permute-start | bytes 786440 | tf_op jit(solution)/shard_map/ppermute | solution.py:183
  53.8 6.9 %collective-permute-start.6 = (bf16[64,16,128]{2,1,0:T(8,128)(2,1)S(1)}, bf16[64,16,128]{2,1,0:T(8,128)(2,1)S(1)}, u32[]{:S(2)}, u32[]{:S(2)}) collective-permute-start(bf16[64,16,128]{2,1,0:T(8,128)(2,1)S(1)} %collective-permute-done.5.p6), channel_id=1, source_target_pairs={{0,1},{1,0},{2,3},{3,2},{4,5},{5,4},{6,7},{7,6},{8,9},{9,8},{10,11... | collective-permute-start | bytes 786440 | tf_op jit(solution)/shard_map/ppermute | solution.py:183
  56.2 4.6 %collective-permute-start.4 = (bf16[64,16,128]{2,1,0:T(8,128)(2,1)S(1)}, bf16[64,16,128]{2,1,0:T(8,128)(2,1)S(1)}, u32[]{:S(2)}, u32[]{:S(2)}) collective-permute-start(bf16[64,16,128]{2,1,0:T(8,128)(2,1)S(1)} %collective-permute-done.3.p4), channel_id=1, source_target_pairs={{0,1},{1,0},{2,3},{3,2},{4,5},{5,4},{6,7},{7,6},{8,9},{9,8},{10,11... | collective-permute-start | bytes 786440 | tf_op jit(solution)/shard_map/ppermute | solution.py:183
  58.2 3.4 %collective-permute-start.2 = (bf16[64,16,128]{2,1,0:T(8,128)(2,1)S(1)}, bf16[64,16,128]{2,1,0:T(8,128)(2,1)S(1)}, u32[]{:S(2)}, u32[]{:S(2)}) collective-permute-start(bf16[64,16,128]{2,1,0:T(8,128)(2,1)S(1)} %collective-permute-done.1.p2), channel_id=1, source_target_pairs={{0,1},{1,0},{2,3},{3,2},{4,5},{5,4},{6,7},{7,6},{8,9},{9,8},{10,11... | collective-permute-start | bytes 786440 | tf_op jit(solution)/shard_map/ppermute | solution.py:183
  60.5 1.1 %copy-start.2 = (f32[16]{0:T(128)S(1)}, f32[16]{0:T(128)}, u32[]{:S(2)}) copy-start(f32[16]{0:T(128)} %param.5) | copy-start | bytes 196

commit v4 on v0

v4 whole, which is shorter than its diff:
```python
import jax
import jax.numpy as jnp
from jax import lax
from jax.experimental import pallas as pl
from jax.experimental.pallas import tpu as pltpu
from jax.sharding import PartitionSpec as P


BF = jnp.bfloat16
F32 = jnp.float32
CORES = [[0, 2, 4, 6], [1, 3, 5, 7]]
GRANT = 16 << 20


def call(kernel, out_shapes, scratch, *args, flops=0, moved=0):
    vmem = pl.BlockSpec(memory_space=pltpu.VMEM)
    many = isinstance(out_shapes, (list, tuple))
    return pl.pallas_call(
        kernel,
        out_shape=out_shapes,
        in_specs=[vmem] * len(args),
        out_specs=[vmem] * len(out_shapes) if many else vmem,
        scratch_shapes=scratch,
        cost_estimate=pl.CostEstimate(flops=flops, bytes_accessed=moved, transcendentals=0),
        compiler_params=pltpu.CompilerParams(vmem_limit_bytes=GRANT),
    )(*args)


def shaped(*shape, dtype=BF):
    return jax.ShapeDtypeStruct(shape, dtype)


def lanes_of(shape):
    return lax.broadcasted_iota(jnp.int32, shape, len(shape) - 1)


def pack_kernel(vol, blocks, first, last, cols, flat):
    flat[...] = vol[...].reshape(1024, 128).astype(F32)
    for z in range(2):
        for row in range(32):
            tile = flat[pl.ds(z * 32 + row, 16, stride=64), :].astype(BF)
            for chip in range(4):
                at = row - 15 * (chip % 2)
                if 0 <= at < 17:
                    blocks[chip, z * 17 + at] = tile
            if row == 0:
                first[pl.ds(z * 16, 16)] = tile
            if row == 31:
                last[pl.ds(z * 16, 16)] = tile
    lane = lanes_of((32, 128))
    both = jnp.zeros((32, 128), F32)
    for z in range(2):
        for c in range(16):
            tile = flat[pl.ds(c * 64 + z * 32, 32), :]
            j = z * 16 + c
            both = jnp.where(lane == j, pltpu.roll(tile, j, 1) if j else tile, both)
            both = jnp.where(lane == 32 + j, pltpu.roll(tile, 33 + j, 1), both)
    cols[...] = both.astype(BF)


def beside_kernel(first, last, left, right, up, down, beside):
    lane = lanes_of((32, 128))
    both = jnp.where(
        lane < 32,
        pltpu.roll(left[...].astype(F32), 96, 1),
        jnp.where(lane < 64, pltpu.roll(right[...].astype(F32), 32, 1), 0.0),
    )
    beside[...] = both
    nothing = jnp.zeros((15, 128), F32)
    up[pl.ds(0, 32)] = last[...]
    up[pl.ds(32, 16)] = jnp.concatenate([both[31:32], nothing], axis=0).astype(BF)
    down[pl.ds(0, 32)] = first[...]
    down[pl.ds(32, 16)] = jnp.concatenate([both[0:1], nothing], axis=0).astype(BF)


def halo_kernel(above, below, beside, out, buf):
    buf[...] = jnp.zeros((40, 128), F32)
    buf[pl.ds(0, 1), :] = above[pl.ds(32, 16)].astype(F32)[0:1]
    buf[pl.ds(1, 32), :] = beside[...]
    buf[pl.ds(33, 1), :] = below[pl.ds(32, 16)].astype(F32)[0:1]
    for d in range(8):
        half = d // 2 % 2
        out[d, pl.ds(0, 32)] = below[pl.ds(0, 32)] if half else above[pl.ds(0, 32)]
        out[d, pl.ds(32, 24)] = buf[pl.ds(16 * half, 24), :].astype(BF)


def taps_kernel(own, other, taps):
    odd = lax.rem(lax.axis_index("ch"), 2) == 1
    even_block = lax.rem(lanes_of((16, 128)) // 16, 2) == 0
    for t, filters in enumerate((own, other)):
        for a in range(3):
            for b in range(3):
                for e in range(3):
                    tile = filters[pl.ds((a * 9 + b * 3 + e) * 16, 16)].astype(F32)
                    swapped = jnp.where(even_block, pltpu.roll(tile, 112, 1), pltpu.roll(tile, 16, 1))
                    tile = jnp.where(odd, swapped, tile).astype(BF)
                    for zo in range(2):
                        zi = a - 1 + zo
                        if 0 <= zi < 2:
                            taps[
                                pl.ds((((b * 3 + e) * 2 + zo) * 2 + t) * 16, 16), pl.ds(zi * 128, 128)
                            ] = tile


def aligned(total, lane):
    before = jnp.where(lane == 0, 0.0, pltpu.roll(total[0:64], 1, 1))
    after = jnp.where(lane == 127, 0.0, pltpu.roll(total[128:192], 127, 1))
    return total[64:128] + (before + after)


def inner_kernel(mine, theirs, taps, pre, sums):
    half = lax.rem(lax.axis_index("ch") // 2, 2)
    lane = lanes_of((64, 128))

    def row_of(row):
        return jnp.concatenate(
            [held[chip, z * 17 + row + half] for z in range(2) for chip in range(4) for held in (mine, theirs)],
            axis=0,
        )

    for p in range(8):
        pair = jnp.concatenate([row_of(2 * p), row_of(2 * p + 1)], axis=1)
        got = jnp.dot(taps[...], pair, preferred_element_type=F32)
        for h in range(2):
            for b in range(3):
                row = 2 * p + h + 1 - b
                if not 0 <= row < 16:
                    continue
                part = got[b * 192 : (b + 1) * 192, h * 128 : (h + 1) * 128]
                if not (b == 0 or (b == 1 and row == 0)):
                    part = part + sums[row]
                if b == 2 or (b == 1 and row == 15):
                    pre[row] = aligned(part, lane)
                else:
                    sums[row] = part


def outer_kernel(pre, taps, mine, theirs, halo, own, other, kept, sent):
    me = lax.axis_index("ch")
    half, core = lax.rem(me // 2, 2), lax.rem(me, 2)
    parts = jnp.concatenate([f[pl.ds(432, 16)].astype(F32) for f in (own, other)], axis=0)
    offset = (parts[:, 0:1] + parts[:, 1:2]) + parts[:, 2:3]
    offset = jnp.concatenate([offset, offset], axis=0)
    sources = [2 * chip + (core ^ t) for chip in range(4) for t in range(2)]
    lane24 = lanes_of((24, 128))
    total = [[jnp.zeros((24, 128), F32) for _ in range(2)] for _ in range(2)]
    for j, source in enumerate(sources):
        both = halo[source, pl.ds(32, 24)].astype(F32)
        for side in range(2):
            for z in range(2):
                shift = (j * 16 - side * 32 - z * 16) % 128
                piece = pltpu.roll(both, shift, 1) if shift else both
                total[side][z] = jnp.where(lane24 // 16 == j, piece, total[side][z])
    beside = jnp.concatenate(
        [jnp.concatenate(total[0], axis=1), jnp.concatenate(total[1], axis=1), jnp.zeros((80, 256), F32)], axis=0
    ).astype(BF)
    edge = lax.dot_general(taps[...], beside, (((1,), (1,)), ((), ())), preferred_element_type=F32)
    before, after = (
        edge[e * 64 : e * 64 + 64]
        + pltpu.roll(edge[192 + e * 64 : 256 + e * 64], 127, 1)
        + pltpu.roll(edge[384 + e * 64 : 448 + e * 64], 126, 1)
        for e in (0, 2)
    )
    lane = lanes_of((64, 128))
    ends = [
        jnp.concatenate(
            [halo[source, pl.ds(z * 16, 16)] for z in range(2) for source in sources], axis=0
        )
    ]
    ends.append(
        jnp.concatenate(
            [
                held[chip, z * 17 + 16 * (1 - half)]
                for z in range(2)
                for chip in range(4)
                for held in (mine, theirs)
            ],
            axis=0,
        )
    )
    first_half = half == 0
    above = jnp.where(first_half, ends[0].astype(F32), ends[1].astype(F32)).astype(BF)
    below = jnp.where(first_half, ends[1].astype(F32), ends[0].astype(F32)).astype(BF)
    above = aligned(jnp.dot(taps[pl.ds(0, 192)], above, preferred_element_type=F32), lane)
    below = aligned(jnp.dot(taps[pl.ds(384, 192)], below, preferred_element_type=F32), lane)
    for row in range(16):
        total = pre[row] + offset
        if row == 0:
            total = total + above
        if row == 15:
            total = total + below
        total = total + jnp.where(lane == 0, before[:, row : row + 1], 0.0)
        total = total + jnp.where(lane == 127, after[:, 24 + row : 25 + row], 0.0)
        done = jnp.where(total >= 0, total, 0.3 * total).astype(BF)
        for z in range(2):
            kept[z * 16 + row] = done[z * 32 : z * 32 + 16]
            sent[z * 16 + row] = done[z * 32 + 16 : z * 32 + 32]


def unpack_kernel(kept, got, out, flat):
    half = lax.rem(lax.axis_index("ch") // 2, 2)
    for held, start in ((kept, 16 * half), (got, 16 * (1 - half))):
        for z in range(2):
            for row in range(16):
                flat[pl.ds(start + z * 32 + row, 16, stride=64), :] = held[z * 16 + row].astype(F32)
    out[...] = flat[...].reshape(16, 2, 32, 128).astype(BF)


def shifts(array, axis, up=True):
    size = lax.axis_size(axis)
    pairs = [(i, i + 1) for i in range(size - 1)]
    return lax.ppermute(array, axis, pairs if up else [(j, i) for i, j in pairs])


def swapped(array, t):
    return lax.ppermute(array, "ch", [(d, d ^ t) for d in range(8)])


def thirds(bias):
    high = bias.astype(BF)
    rest = bias - high.astype(F32)
    middle = rest.astype(BF)
    low = (rest - middle.astype(F32)).astype(BF)
    return jnp.pad(jnp.stack([high, middle, low], axis=1), ((0, 0), (0, 125)))


def stages(volume, weights, bias):
    blocks, first, last, cols = call(
        pack_kernel,
        [shaped(4, 34, 16, 128), shaped(32, 128), shaped(32, 128), shaped(32, 128)],
        [pltpu.VMEM((1024, 128), F32)],
        volume,
        moved=1 << 20,
    )
    mine = lax.all_to_all(blocks, "ch", split_axis=0, concat_axis=0, tiled=True, axis_index_groups=CORES)
    left = shifts(cols, "sy", True)
    right = shifts(cols, "sy", False)
    own = jnp.concatenate([weights.transpose(2, 3, 4, 0, 1).reshape(432, 128), thirds(bias)], axis=0)
    other = swapped(own, 2)
    up, down, beside = call(
        beside_kernel,
        [shaped(48, 128), shaped(48, 128), shaped(32, 128, dtype=F32)],
        [],
        first,
        last,
        left,
        right,
        moved=1 << 16,
    )
    above = shifts(up, "sx", True)
    below = shifts(down, "sx", False)
    theirs = swapped(mine, 1)
    taps = call(taps_kernel, shaped(576, 256), [], own, other, moved=1 << 19)
    halo = call(halo_kernel, shaped(8, 56, 128), [pltpu.VMEM((40, 128), F32)], above, below, beside, moved=1 << 17)
    halo = lax.all_to_all(halo, "ch", split_axis=0, concat_axis=0, tiled=True)
    pre = call(
        inner_kernel,
        shaped(16, 64, 128, dtype=F32),
        [pltpu.VMEM((16, 192, 128), F32)],
        mine,
        theirs,
        taps,
        flops=2 * 576 * 256 * 2048,
        moved=3 << 20,
    )
    kept, sent = call(
        outer_kernel,
        [shaped(32, 16, 128)] * 2,
        [],
        pre,
        taps,
        mine,
        theirs,
        halo,
        own,
        other,
        flops=2 * 576 * 256 * 256,
        moved=2 << 20,
    )
    got = swapped(sent, 2)
    return call(
        unpack_kernel,
        shaped(16, 2, 32, 128),
        [pltpu.VMEM((1024, 128), F32)],
        kept,
        got,
        moved=1 << 19,
    )


def solution(mesh):
    in_specs = (P("ch", None, "sx", "sy"), P("ch", None, None, None, None), P("ch"))
    out_specs = P("ch", None, "sx", "sy")
    return jax.shard_map(stages, mesh=mesh, in_specs=in_specs, out_specs=out_specs, check_vma=False)
```

time: 116 us -> 65.1 us (0.56)
  the two profiles are of different devices: /device:TPU:28 before, /device:TPU:30 now
where the time goes in v4:
time: 65.1 us; the launch traced here: 64.6 us
  starting transfers between devices  38 us (58%)
  waiting for transfers between devices  20.4 us (31%)
  Pallas kernels  5.06 us (8%)
  local copies, waits for them, and re-layouts  1.05 us (2%)
    ppermute x4, starting transfers between devices, shifts(): lax.ppermute(array, axis, pairs if up else [(j, i) for i, j in pairs])  17.1 us
    ppermute x3, waiting for transfers between devices, swapped(): return lax.ppermute(array, 'ch', [(d, d ^ t) for d in range(8)])  9.05 us
    ppermute x3, starting transfers between devices, swapped(): return lax.ppermute(array, 'ch', [(d, d ^ t) for d in range(8)])  8.46 us
    all_to_all x1, starting transfers between devices, stages(): lax.all_to_all(blocks, 'ch', split_axis=0, concat_axis=0, tiled=True, axi...  7.26 us
    ppermute x4, waiting for transfers between devices, shifts(): lax.ppermute(array, axis, pairs if up else [(j, i) for i, j in pairs])  6.24 us
    all_to_all x1, starting transfers between devices, stages(): halo = lax.all_to_all(halo, 'ch', split_axis=0, concat_axis=0, tiled=True)  5.13 us
    all_to_all x1, waiting for transfers between devices, stages(): lax.all_to_all(blocks, 'ch', split_axis=0, concat_axis=0, tiled=True, axi...  5.09 us
    pallas_call x7, Pallas kernels, call(): pl.pallas_call(kernel, out_shape=out_shapes, in_specs=[vmem] * len(args),...  5.06 us
  transfers between devices with their start and end apart: 9, of which 5 were waited for; matrix products, arithmetic and copies ran while one was open for 0% of the time, Pallas kernels for 3%

profile of v4, /device:TPU:30, one launch (start us, length us, event | category | flops | bytes accessed | tf_op | source)
XLA Modules:
  0.0 64.6 jit_solution(7990585602362322913)
XLA Ops:
  0.0 0.0 copy-start
  0.0 0.9 %copy-done = bf16[16,2,32,128]{3,2,1,0:T(8,128)(2,1)S(1)} copy-done((bf16[16,2,32,128]{3,2,1,0:T(8,128)(2,1)S(1)}, bf16[16,2,32,128]{3,2,1,0:T(8,128)(2,1)}, u32[]{:S(2)}) %copy-start) | copy-done | bytes 262168
  1.0 1.2 %shard_map.37 = (bf16[4,34,16,128]{3,2,1,0:T(8,128)(2,1)}, bf16[32,128]{1,0:T(8,128)(2,1)S(1)}, bf16[32,128]{1,0:T(8,128)(2,1)S(1)}, bf16[32,128]{1,0:T(8,128)(2,1)S(1)}) custom-call(bf16[16,2,32,128]{3,2,1,0:T(8,128)(2,1)S(1)} %copy-done), custom_call_target="tpu_custom_call" | custom-call | bytes 1048576 | tf_op jit(solution)/shard_map/pallas_call | solution.py:18
  2.2 7.3 %all-to-all-start = ((bf16[4,34,16,128]{3,2,1,0:T(8,128)(2,1)}), bf16[4,34,16,128]{3,2,1,0:T(8,128)(2,1)S(1)}, u32[]{:S(2)}, u32[]{:S(2)}) async-start(bf16[4,34,16,128]{3,2,1,0:T(8,128)(2,1)} %get-tuple-element.14), calls=%async_computation | async-start | bytes 1114112 | tf_op jit(solution)/shard_map/all_to_all | solution.py:235
  9.4 0.0 copy-start.2
  9.4 8.6 %collective-permute-start.3 = (bf16[32,128]{1,0:T(8,128)(2,1)S(1)}, bf16[32,128]{1,0:T(8,128)(2,1)S(1)}, u32[]{:S(2)}, u32[]{:S(2)}) collective-permute-start(bf16[32,128]{1,0:T(8,128)(2,1)S(1)} %get-tuple-element.17), channel_id=1, source_target_pairs={{8,0},{16,8},{24,16},{32,24},{40,32},{48,40},{56,48},{9,1},{17,9},... | collective-permute-start | bytes 24584 | tf_op jit(solution)/shard_map/ppermute | solution.py:212
  18.0 1.9 %collective-permute-start.2 = (bf16[32,128]{1,0:T(8,128)(2,1)S(1)}, bf16[32,128]{1,0:T(8,128)(2,1)S(1)}, u32[]{:S(2)}, u32[]{:S(2)}) collective-permute-start(bf16[32,128]{1,0:T(8,128)(2,1)S(1)} %get-tuple-element.17), channel_id=1, source_target_pairs={{0,8},{8,16},{16,24},{24,32},{32,40},{40,48},{48,56},{1,9},{9,17},... | collective-permute-start | bytes 24584 | tf_op jit(solution)/shard_map/ppermute | solution.py:212
  20.0 5.1 %all-to-all-done.mine = bf16[4,34,16,128]{3,2,1,0:T(8,128)(2,1)S(1)} async-done(((bf16[4,34,16,128]{3,2,1,0:T(8,128)(2,1)}), bf16[4,34,16,128]{3,2,1,0:T(8,128)(2,1)S(1)}, u32[]{:S(2)}, u32[]{:S(2)}) %all-to-all-start) | async-done | bytes 557088 | tf_op jit(solution)/shard_map/all_to_all | solution.py:235
  25.1 1.9 %collective-permute-start = (bf16[4,34,16,128]{3,2,1,0:T(8,128)(2,1)S(1)}, bf16[4,34,16,128]{3,2,1,0:T(8,128)(2,1)S(1)}, u32[]{:S(2)}, u32[]{:S(2)}) collective-permute-start(bf16[4,34,16,128]{3,2,1,0:T(8,128)(2,1)S(1)} %all-to-all-done.mine), channel_id=1, source_target_pairs={{0,1},{1,0},{2,3},{3,2},{4,5},{5,4},{6,7},{7,6},{8,9},{9,8},{10,11... | collective-permute-start | bytes 1671176 | tf_op jit(solution)/shard_map/ppermute | solution.py:216
  27.0 0.0 copy-done.2
  27.0 0.0 collective-permute-done.3.right
  27.0 1.5 %collective-permute-done.2.left = bf16[32,128]{1,0:T(8,128)(2,1)S(1)} collective-permute-done((bf16[32,128]{1,0:T(8,128)(2,1)S(1)}, bf16[32,128]{1,0:T(8,128)(2,1)S(1)}, u32[]{:S(2)}, u32[]{:S(2)}) %collective-permute-start.2) | collective-permute-done | bytes 8224 | tf_op jit(solution)/shard_map/ppermute | solution.py:212
  28.5 0.1 shard_map.40
  28.6 4.7 %collective-permute-start.4 = (bf16[48,128]{1,0:T(8,128)(2,1)S(1)}, bf16[48,128]{1,0:T(8,128)(2,1)S(1)}, u32[]{:S(2)}, u32[]{:S(2)}) collective-permute-start(bf16[48,128]{1,0:T(8,128)(2,1)S(1)} %get-tuple-element.18), channel_id=1, source_target_pairs={{0,64},{64,128},{128,192},{192,256},{256,320},{320,384},{384,448},... | collective-permute-start | bytes 36872 | tf_op jit(solution)/shard_map/ppermute | solution.py:212
  33.3 1.9 %collective-permute-start.5 = (bf16[48,128]{1,0:T(8,128)(2,1)S(1)}, bf16[48,128]{1,0:T(8,128)(2,1)S(1)}, u32[]{:S(2)}, u32[]{:S(2)}) collective-permute-start(bf16[48,128]{1,0:T(8,128)(2,1)S(1)} %get-tuple-element.19), channel_id=1, source_target_pairs={{64,0},{128,64},{192,128},{256,192},{320,256},{384,320},{448,384},... | collective-permute-start | bytes 36872 | tf_op jit(solution)/shard_map/ppermute | solution.py:212
  35.2 0.1 copy.7
  35.3 0.0 collective-permute-done.4.above
  35.3 4.8 %collective-permute-done.5.below = bf16[48,128]{1,0:T(8,128)(2,1)S(1)} collective-permute-done((bf16[48,128]{1,0:T(8,128)(2,1)S(1)}, bf16[48,128]{1,0:T(8,128)(2,1)S(1)}, u32[]{:S(2)}, u32[]{:S(2)}) %collective-permute-start.5) | collective-permute-done | bytes 12320 | tf_op jit(solution)/shard_map/ppermute | solution.py:212
  40.1 0.7 %shard_map.41 = bf16[8,56,128]{2,1,0:T(8,128)(2,1)} custom-call(bf16[48,128]{1,0:T(8,128)(2,1)S(1)} %collective-permute-done.4.above, bf16[48,128]{1,0:T(8,128)(2,1)S(1)} %collective-permute-done.5.below, f32[32,128]{1,0:T(8,128)S(1)} %get-tuple-element.20.beside), custom_call_target="tpu_custom_call" | custom-call | bytes 131072 | tf_op jit(solution)/shard_map/pallas_call | solution.py:18
  40.7 0.0 copy-start.1
  40.7 5.1 %all-to-all-start.1 = ((bf16[8,56,128]{2,1,0:T(8,128)(2,1)}), bf16[8,56,128]{2,1,0:T(8,128)(2,1)S(1)}, u32[]{:S(2)}, u32[]{:S(2)}) async-start(bf16[8,56,128]{2,1,0:T(8,128)(2,1)} %shard_map.41), calls=%async_computation.1 | async-start | bytes 229376 | tf_op jit(solution)/shard_map/all_to_all | solution.py:255
  45.9 0.0 copy-done.1
  45.9 3.9 %collective-permute-start.1 = (bf16[448,128]{1,0:T(8,128)(2,1)S(1)}, bf16[448,128]{1,0:T(8,128)(2,1)S(1)}, u32[]{:S(2)}, u32[]{:S(2)}) collective-permute-start(bf16[448,128]{1,0:T(8,128)(2,1)S(1)} %fusion.1.own), channel_id=1, source_target_pairs={{0,2},{1,3},{2,0},{3,1},{4,6},{5,7},{6,4},{7,5},{8,10},{9,11},{10,... | collective-permute-start | bytes 344072 | tf_op jit(solution)/shard_map/ppermute | solution.py:216
  49.8 4.4 %collective-permute-done.1.other = bf16[448,128]{1,0:T(8,128)(2,1)S(1)} collective-permute-done((bf16[448,128]{1,0:T(8,128)(2,1)S(1)}, bf16[448,128]{1,0:T(8,128)(2,1)S(1)}, u32[]{:S(2)}, u32[]{:S(2)}) %collective-permute-start.1) | collective-permute-done | bytes 114720 | tf_op jit(solution)/shard_map/ppermute | solution.py:216
  54.3 0.2 shard_map.38.taps
  54.4 0.0 collective-permute-done.theirs
  54.5 0.9 %shard_map.39.pre = f32[16,64,128]{2,1,0:T(8,128)S(1)} custom-call(bf16[4,34,16,128]{3,2,1,0:T(8,128)(2,1)S(1)} %all-to-all-done.mine, bf16[4,34,16,128]{3,2,1,0:T(8,128)(2,1)S(1)} %collective-permute-done.theirs, bf16[576,256]{1,0:T(8,128)(2,1)S(1)} %shard_map.38.taps), custom_call_target="tpu_custom_call" | custom-call | flops 603979776 | bytes 3145728 | tf_op jit(solution)/shard_map/pallas_call | solution.py:18
  55.3 0.0 all-to-all-done.1.halo
  55.4 0.9 %shard_map.42 = (bf16[32,16,128]{2,1,0:T(8,128)(2,1)S(1)}, bf16[32,16,128]{2,1,0:T(8,128)(2,1)S(1)}) custom-call(f32[16,64,128]{2,1,0:T(8,128)S(1)} %shard_map.39.pre, bf16[576,256]{1,0:T(8,128)(2,1)S(1)} %shard_map.38.taps, bf16[4,34,16,128]{3,2,1,0:T(8,128)(2,1)S(1)} %all-to-all-done.mine, bf16[4,34,16,128]{3,2,1,0:T(8,128)(2,1)S(1)} %collective-permute-done.theirs, ...), custom_call_target="tpu_custom_call" | custom-call | flops 75497472 | bytes 2097152 | tf_op jit(solution)/shard_map/pallas_call | solution.py:18
  56.2 2.6 %collective-permute-start.6 = (bf16[32,16,128]{2,1,0:T(8,128)(2,1)S(1)}, bf16[32,16,128]{2,1,0:T(8,128)(2,1)S(1)}, u32[]{:S(2)}, u32[]{:S(2)}) collective-permute-start(bf16[32,16,128]{2,1,0:T(8,128)(2,1)S(1)} %get-tuple-element.22), channel_id=1, source_target_pairs={{0,2},{1,3},{2,0},{3,1},{4,6},{5,7},{6,4},{7,5},{8,10},{9,11},{10,... | collective-permute-start | bytes 393224 | tf_op jit(solution)/shard_map/ppermute | solution.py:216
  58.9 4.6 %collective-permute-done.6.got = bf16[32,16,128]{2,1,0:T(8,128)(2,1)S(1)} collective-permute-done((bf16[32,16,128]{2,1,0:T(8,128)(2,1)S(1)}, bf16[32,16,128]{2,1,0:T(8,128)(2,1)S(1)}, u32[]{:S(2)}, u32[]{:S(2)}) %collective-permute-start.6) | collective-permute-done | bytes 131104 | tf_op jit(solution)/shard_map/ppermute | solution.py:216
  63.5 1.2 %shard_map.43 = bf16[16,2,32,128]{3,2,1,0:T(8,128)(2,1)} custom-call(bf16[32,16,128]{2,1,0:T(8,128)(2,1)S(1)} %get-tuple-element.21.kept, bf16[32,16,128]{2,1,0:T(8,128)(2,1)S(1)} %collective-permute-done.6.got), custom_call_target="tpu_custom_call" | custom-call | bytes 524288 | tf_op jit(solution)/shard_map/pallas_call | solution.py:18
  (3 shorter events, 0.0 us)
Async XLA Ops:
  0.0 0.9 %copy-start = (bf16[16,2,32,128]{3,2,1,0:T(8,128)(2,1)S(1)}, bf16[16,2,32,128]{3,2,1,0:T(8,128)(2,1)}, u32[]{:S(2)}) copy-start(bf16[16,2,32,128]{3,2,1,0:T(8,128)(2,1)} %vol.1) | copy-start | bytes 786436
  2.2 22.9 %all-to-all-start = ((bf16[4,34,16,128]{3,2,1,0:T(8,128)(2,1)}), bf16[4,34,16,128]{3,2,1,0:T(8,128)(2,1)S(1)}, u32[]{:S(2)}, u32[]{:S(2)}) async-start(bf16[4,34,16,128]{3,2,1,0:T(8,128)(2,1)} %get-tuple-element.14), calls=%async_computation | async-start | bytes 1114112 | tf_op jit(solution)/shard_map/all_to_all | solution.py:235
  9.4 17.6 %copy-start.2 = (f32[16]{0:T(128)S(1)}, f32[16]{0:T(128)}, u32[]{:S(2)}) copy-start(f32[16]{0:T(128)} %param.5) | copy-start | bytes 196
  9.4 17.6 %collective-permute-start.3 = (bf16[32,128]{1,0:T(8,128)(2,1)S(1)}, bf16[32,128]{1,0:T(8,128)(2,1)S(1)}, u32[]{:S(2)}, u32[]{:S(2)}) collective-permute-start(bf16[32,128]{1,0:T(8,128)(2,1)S(1)} %get-tuple-element.17), channel_id=1, source_target_pairs={{8,0},{16,8},{24,16},{32,24},{40,32},{48,40},{56,48},{9,1},{17,9},... | collective-permute-start | bytes 24584 | tf_op jit(solution)/shard_map/ppermute | solution.py:212
  18.0 10.5 %collective-permute-start.2 = (bf16[32,128]{1,0:T(8,128)(2,1)S(1)}, bf16[32,128]{1,0:T(8,128)(2,1)S(1)}, u32[]{:S(2)}, u32[]{:S(2)}) collective-permute-start(bf16[32,128]{1,0:T(8,128)(2,1)S(1)} %get-tuple-element.17), channel_id=1, source_target_pairs={{0,8},{8,16},{16,24},{24,32},{32,40},{40,48},{48,56},{1,9},{9,17},... | collective-permute-start | bytes 24584 | tf_op jit(solution)/shard_map/ppermute | solution.py:212
  25.1 29.4 %collective-permute-start = (bf16[4,34,16,128]{3,2,1,0:T(8,128)(2,1)S(1)}, bf16[4,34,16,128]{3,2,1,0:T(8,128)(2,1)S(1)}, u32[]{:S(2)}, u32[]{:S(2)}) collective-permute-start(bf16[4,34,16,128]{3,2,1,0:T(8,128)(2,1)S(1)} %all-to-all-done.mine), channel_id=1, source_target_pairs={{0,1},{1,0},{2,3},{3,2},{4,5},{5,4},{6,7},{7,6},{8,9},{9,8},{10,11... | collective-permute-start | bytes 1671176 | tf_op jit(solution)/shard_map/ppermute | solution.py:216
  28.6 6.7 %collective-permute-start.4 = (bf16[48,128]{1,0:T(8,128)(2,1)S(1)}, bf16[48,128]{1,0:T(8,128)(2,1)S(1)}, u32[]{:S(2)}, u32[]{:S(2)}) collective-permute-start(bf16[48,128]{1,0:T(8,128)(2,1)S(1)} %get-tuple-element.18), channel_id=1, source_target_pairs={{0,64},{64,128},{128,192},{192,256},{256,320},{320,384},{384,448},... | collective-permute-start | bytes 36872 | tf_op jit(solution)/shard_map/ppermute | solution.py:212
  33.3 6.8 %collective-permute-start.5 = (bf16[48,128]{1,0:T(8,128)(2,1)S(1)}, bf16[48,128]{1,0:T(8,128)(2,1)S(1)}, u32[]{:S(2)}, u32[]{:S(2)}) collective-permute-start(bf16[48,128]{1,0:T(8,128)(2,1)S(1)} %get-tuple-element.19), channel_id=1, source_target_pairs={{64,0},{128,64},{192,128},{256,192},{320,256},{384,320},{448,384},... | collective-permute-start | bytes 36872 | tf_op jit(solution)/shard_map/ppermute | solution.py:212
  40.7 5.1 %copy-start.1 = (bf16[16,128,3,3,3]{1,0,4,3,2:T(8,128)(2,1)S(1)}, bf16[16,128,3,3,3]{1,0,4,3,2:T(8,128)(2,1)}, u32[]{:S(2)}) copy-start(bf16[16,128,3,3,3]{1,0,4,3,2:T(8,128)(2,1)} %param.4) | copy-start | bytes 331780
  40.7 14.6 %all-to-all-start.1 = ((bf16[8,56,128]{2,1,0:T(8,128)(2,1)}), bf16[8,56,128]{2,1,0:T(8,128)(2,1)S(1)}, u32[]{:S(2)}, u32[]{:S(2)}) async-start(bf16[8,56,128]{2,1,0:T(8,128)(2,1)} %shard_map.41), calls=%async_computation.1 | async-start | bytes 229376 | tf_op jit(solution)/shard_map/all_to_all | solution.py:255
  45.9 8.4 %collective-permute-start.1 = (bf16[448,128]{1,0:T(8,128)(2,1)S(1)}, bf16[448,128]{1,0:T(8,128)(2,1)S(1)}, u32[]{:S(2)}, u32[]{:S(2)}) collective-permute-start(bf16[448,128]{1,0:T(8,128)(2,1)S(1)} %fusion.1.own), channel_id=1, source_target_pairs={{0,2},{1,3},{2,0},{3,1},{4,6},{5,7},{6,4},{7,5},{8,10},{9,11},{10,... | collective-permute-start | bytes 344072 | tf_op jit(solution)/shard_map/ppermute | solution.py:216
  56.2 7.3 %collective-permute-start.6 = (bf16[32,16,128]{2,1,0:T(8,128)(2,1)S(1)}, bf16[32,16,128]{2,1,0:T(8,128)(2,1)S(1)}, u32[]{:S(2)}, u32[]{:S(2)}) collective-permute-start(bf16[32,16,128]{2,1,0:T(8,128)(2,1)S(1)} %get-tuple-element.22), channel_id=1, source_target_pairs={{0,2},{1,3},{2,0},{3,1},{4,6},{5,7},{6,4},{7,5},{8,10},{9,11},{10,... | collective-permute-start | bytes 393224 | tf_op jit(solution)/shard_map/ppermute | solution.py:216

commit v5 on v4

v5 whole, which is shorter than its diff:
```python
import jax
import jax.numpy as jnp
from jax import lax
from jax.experimental import pallas as pl
from jax.experimental.pallas import tpu as pltpu
from jax.sharding import PartitionSpec as P


BF = jnp.bfloat16
F32 = jnp.float32
CORES = [[0, 2, 4, 6], [1, 3, 5, 7]]
GRANT = 16 << 20


def call(kernel, out_shapes, scratch, *args, flops=0, moved=0):
    vmem = pl.BlockSpec(memory_space=pltpu.VMEM)
    many = isinstance(out_shapes, (list, tuple))
    return pl.pallas_call(
        kernel,
        out_shape=out_shapes,
        in_specs=[vmem] * len(args),
        out_specs=[vmem] * len(out_shapes) if many else vmem,
        scratch_shapes=scratch,
        cost_estimate=pl.CostEstimate(flops=flops, bytes_accessed=moved, transcendentals=0),
        compiler_params=pltpu.CompilerParams(vmem_limit_bytes=GRANT),
    )(*args)


def shaped(*shape, dtype=BF):
    return jax.ShapeDtypeStruct(shape, dtype)


def lanes_of(shape):
    return lax.broadcasted_iota(jnp.int32, shape, len(shape) - 1)


def pack_kernel(vol, blocks, flat):
    flat[...] = vol[...].reshape(1024, 128).astype(F32)
    for z in range(2):
        for row in range(32):
            tile = flat[pl.ds(z * 32 + row, 16, stride=64), :].astype(BF)
            for chip in range(4):
                at = row - 15 * (chip % 2)
                if 0 <= at < 17:
                    blocks[chip, z * 17 + at] = tile


def half_of():
    return lax.rem(lax.axis_index("ch") // 2, 2)


def row_kernel(mine, row):
    at = 16 * half_of()
    for z in range(2):
        for chip in range(4):
            row[pl.ds(z * 64 + chip * 16, 16)] = mine[chip, z * 17 + at]


def columns_kernel(mine, cols):
    lane = lanes_of((128, 128))
    both = jnp.zeros((128, 128), F32)
    for i in range(17):
        tile = jnp.concatenate([mine[chip, z * 17 + i] for z in range(2) for chip in range(4)], axis=0).astype(F32)
        both = jnp.where(lane == i + 1, pltpu.roll(tile, i + 1, 1), both)
        both = jnp.where(lane == 65 + i, pltpu.roll(tile, 66 + i, 1), both)
    cols[...] = both


def edges_kernel(cols, beyond, edges):
    lane = lanes_of((128, 128))
    at = 18 * half_of()
    tile = beyond[...].astype(F32)
    both = cols[...]
    both = jnp.where(
        lane == at, jnp.broadcast_to(tile[:, 0:1], (128, 128)), both
    )
    both = jnp.where(lane == 64 + at, jnp.broadcast_to(tile[:, 127:128], (128, 128)), both)
    edges[...] = both.astype(BF)


def beside_kernel(beyond, left, right, halo):
    halo[pl.ds(0, 128)] = beyond[...]
    lane = lanes_of((128, 128))
    halo[pl.ds(128, 128)] = jnp.where(
        lane < 64, pltpu.roll(left[...].astype(F32), 64, 1), pltpu.roll(right[...].astype(F32), 64, 1)
    ).astype(BF)


def taps_kernel(own, other, taps):
    odd = lax.rem(lax.axis_index("ch"), 2) == 1
    even_block = lax.rem(lanes_of((16, 128)) // 16, 2) == 0
    for t, filters in enumerate((own, other)):
        for a in range(3):
            for b in range(3):
                for e in range(3):
                    tile = filters[pl.ds((a * 9 + b * 3 + e) * 16, 16)].astype(F32)
                    swapped = jnp.where(even_block, pltpu.roll(tile, 112, 1), pltpu.roll(tile, 16, 1))
                    tile = jnp.where(odd, swapped, tile).astype(BF)
                    for zo in range(2):
                        zi = a - 1 + zo
                        if 0 <= zi < 2:
                            taps[
                                pl.ds((((b * 3 + e) * 2 + zo) * 2 + t) * 16, 16), pl.ds(zi * 128, 128)
                            ] = tile


def aligned(total, lane):
    before = jnp.where(lane == 0, 0.0, pltpu.roll(total[0:64], 1, 1))
    after = jnp.where(lane == 127, 0.0, pltpu.roll(total[128:192], 127, 1))
    return total[64:128] + (before + after)


def inner_kernel(mine, theirs, taps, pre, sums):
    half = lax.rem(lax.axis_index("ch") // 2, 2)
    lane = lanes_of((64, 128))

    def row_of(row):
        return jnp.concatenate(
            [held[chip, z * 17 + row + half] for z in range(2) for chip in range(4) for held in (mine, theirs)],
            axis=0,
        )

    for p in range(8):
        pair = jnp.concatenate([row_of(2 * p), row_of(2 * p + 1)], axis=1)
        got = jnp.dot(taps[...], pair, preferred_element_type=F32)
        for h in range(2):
            for b in range(3):
                row = 2 * p + h + 1 - b
                if not 0 <= row < 16:
                    continue
                part = got[b * 192 : (b + 1) * 192, h * 128 : (h + 1) * 128]
                if not (b == 0 or (b == 1 and row == 0)):
                    part = part + sums[row]
                if b == 2 or (b == 1 and row == 15):
                    pre[row] = aligned(part, lane)
                else:
                    sums[row] = part


def outer_kernel(pre, taps, mine, theirs, halo, halo2, own, other, kept, sent):
    half = half_of()
    first_half = half == 0
    parts = jnp.concatenate([f[pl.ds(432, 16)].astype(F32) for f in (own, other)], axis=0)
    offset = (parts[:, 0:1] + parts[:, 1:2]) + parts[:, 2:3]
    offset = jnp.concatenate([offset, offset], axis=0)

    def joined(start):
        return jnp.concatenate(
            [
                held[pl.ds(start + z * 64 + chip * 16, 16)]
                for z in range(2)
                for chip in range(4)
                for held in (halo, halo2)
            ],
            axis=0,
        )

    edge = jnp.dot(taps[...], joined(128), preferred_element_type=F32)
    moved = []
    for e in (0, 2):
        total = (
            edge[e * 64 : e * 64 + 64]
            + pltpu.roll(edge[192 + e * 64 : 256 + e * 64], 127, 1)
            + pltpu.roll(edge[384 + e * 64 : 448 + e * 64], 126, 1)
        )
        moved.append(jnp.where(first_half, total, pltpu.roll(total, 127, 1)))
    before, after = moved
    lane = lanes_of((64, 128))
    far = joined(0).astype(F32)
    near = jnp.concatenate(
        [
            held[chip, z * 17 + 16 * (1 - half)]
            for z in range(2)
            for chip in range(4)
            for held in (mine, theirs)
        ],
        axis=0,
    ).astype(F32)
    above = jnp.where(first_half, far, near).astype(BF)
    below = jnp.where(first_half, near, far).astype(BF)
    above = aligned(jnp.dot(taps[pl.ds(0, 192)], above, preferred_element_type=F32), lane)
    below = aligned(jnp.dot(taps[pl.ds(384, 192)], below, preferred_element_type=F32), lane)
    for row in range(16):
        total = pre[row] + offset
        if row == 0:
            total = total + above
        if row == 15:
            total = total + below
        total = total + jnp.where(lane == 0, before[:, row : row + 1], 0.0)
        total = total + jnp.where(lane == 127, after[:, 64 + row : 65 + row], 0.0)
        done = jnp.where(total >= 0, total, 0.3 * total).astype(BF)
        for z in range(2):
            kept[z * 16 + row] = done[z * 32 : z * 32 + 16]
            sent[z * 16 + row] = done[z * 32 + 16 : z * 32 + 32]


def unpack_kernel(kept, got, out, flat):
    half = lax.rem(lax.axis_index("ch") // 2, 2)
    for held, start in ((kept, 16 * half), (got, 16 * (1 - half))):
        for z in range(2):
            for row in range(16):
                flat[pl.ds(start + z * 32 + row, 16, stride=64), :] = held[z * 16 + row].astype(F32)
    out[...] = flat[...].reshape(16, 2, 32, 128).astype(BF)


def along_y(array, step):
    size = lax.axis_size("sy")
    pairs = [
        (y * 8 + d, (y + step) * 8 + (d ^ 4)) for y in range(size) for d in range(8) if 0 <= y + step < size
    ]
    return lax.ppermute(array, ("sy", "ch"), pairs)


def along_x(array):
    size = lax.axis_size("sx")
    pairs = []
    for x in range(size):
        for d in range(8):
            to = x + (1 if d // 2 % 2 else -1)
            if 0 <= to < size:
                pairs.append((x * 8 + d, to * 8 + (d ^ 2)))
    return lax.ppermute(array, ("sx", "ch"), pairs)


def swapped(array, t):
    return lax.ppermute(array, "ch", [(d, d ^ t) for d in range(8)])


def thirds(bias):
    high = bias.astype(BF)
    rest = bias - high.astype(F32)
    middle = rest.astype(BF)
    low = (rest - middle.astype(F32)).astype(BF)
    return jnp.pad(jnp.stack([high, middle, low], axis=1), ((0, 0), (0, 125)))


def stages(volume, weights, bias):
    blocks = call(
        pack_kernel, shaped(4, 34, 16, 128), [pltpu.VMEM((1024, 128), F32)], volume, moved=1 << 20
    )
    mine = lax.all_to_all(blocks, "ch", split_axis=0, concat_axis=0, tiled=True, axis_index_groups=CORES)
    own = jnp.concatenate([weights.transpose(2, 3, 4, 0, 1).reshape(432, 128), thirds(bias)], axis=0)
    other = swapped(own, 2)
    row = call(row_kernel, shaped(128, 128), [], mine, moved=1 << 16)
    beyond = along_x(row)
    theirs = swapped(mine, 1)
    cols = call(columns_kernel, shaped(128, 128, dtype=F32), [], mine, moved=1 << 18)
    edges = call(edges_kernel, shaped(128, 128), [], cols, beyond, moved=1 << 17)
    left = along_y(edges, 1)
    right = along_y(edges, -1)
    taps = call(taps_kernel, shaped(576, 256), [], own, other, moved=1 << 19)
    pre = call(
        inner_kernel,
        shaped(16, 64, 128, dtype=F32),
        [pltpu.VMEM((16, 192, 128), F32)],
        mine,
        theirs,
        taps,
        flops=2 * 576 * 256 * 2048,
        moved=3 << 20,
    )
    halo = call(beside_kernel, shaped(256, 128), [], beyond, left, right, moved=1 << 17)
    halo2 = swapped(halo, 1)
    kept, sent = call(
        outer_kernel,
        [shaped(32, 16, 128)] * 2,
        [],
        pre,
        taps,
        mine,
        theirs,
        halo,
        halo2,
        own,
        other,
        flops=2 * 576 * 256 * 256,
        moved=2 << 20,
    )
    got = swapped(sent, 2)
    return call(
        unpack_kernel,
        shaped(16, 2, 32, 128),
        [pltpu.VMEM((1024, 128), F32)],
        kept,
        got,
        moved=1 << 19,
    )


def solution(mesh):
    in_specs = (P("ch", None, "sx", "sy"), P("ch", None, None, None, None), P("ch"))
    out_specs = P("ch", None, "sx", "sy")
    return jax.shard_map(stages, mesh=mesh, in_specs=in_specs, out_specs=out_specs, check_vma=False)
```

time: 65.1 us -> 65.9 us (1.012)
  the two profiles are of different devices: /device:TPU:30 before, /device:TPU:38 now
where the time goes in v5:
time: 65.9 us; the launch traced here: 65.6 us
  blocking collectives  22.4 us (34%)
  starting transfers between devices  21.1 us (32%)
  waiting for transfers between devices  17 us (26%)
  Pallas kernels  3.93 us (6%)
  local copies, waits for them, and re-layouts  1.06 us (2%)
    all_to_all x1, blocking collectives, stages(): lax.all_to_all(blocks, 'ch', split_axis=0, concat_axis=0, tiled=True, axi...  22.4 us
    ppermute x2, starting transfers between devices, along_y(): return lax.ppermute(array, ('sy', 'ch'), pairs)  9.59 us
    ppermute x4, starting transfers between devices, swapped(): return lax.ppermute(array, 'ch', [(d, d ^ t) for d in range(8)])  8.13 us
    ppermute x2, waiting for transfers between devices, along_y(): return lax.ppermute(array, ('sy', 'ch'), pairs)  6.88 us
    ppermute x4, waiting for transfers between devices, swapped(): return lax.ppermute(array, 'ch', [(d, d ^ t) for d in range(8)])  5.88 us
    ppermute x1, waiting for transfers between devices, along_x(): return lax.ppermute(array, ('sx', 'ch'), pairs)  4.2 us
    pallas_call x9, Pallas kernels, call(): pl.pallas_call(kernel, out_shape=out_shapes, in_specs=[vmem] * len(args),...  3.93 us
    ppermute x1, starting transfers between devices, along_x(): return lax.ppermute(array, ('sx', 'ch'), pairs)  3.34 us
  transfers between devices with their start and end apart: 7, of which 4 were waited for; matrix products, arithmetic and copies ran while one was open for 0% of the time, Pallas kernels for 2%

profile of v5, /device:TPU:38, one launch (start us, length us, event | category | flops | bytes accessed | tf_op | source)
XLA Modules:
  0.0 65.6 jit_solution(11091398698670999770)
XLA Ops:
  0.0 0.0 copy-start
  0.0 0.9 %copy-done = bf16[16,2,32,128]{3,2,1,0:T(8,128)(2,1)S(1)} copy-done((bf16[16,2,32,128]{3,2,1,0:T(8,128)(2,1)S(1)}, bf16[16,2,32,128]{3,2,1,0:T(8,128)(2,1)}, u32[]{:S(2)}) %copy-start) | copy-done | bytes 262168
  1.0 0.3 shard_map.37
  1.3 0.0 copy-start.2
  1.3 0.0 copy-start.1
  1.3 22.4 %all_to_all.5.mine = bf16[4,34,16,128]{3,2,1,0:T(8,128)(2,1)S(1)} all-to-all(bf16[4,34,16,128]{3,2,1,0:T(8,128)(2,1)S(1)} %shard_map.37), channel_id=1, replica_groups={{0,2,4,6},{1,3,5,7},{8,10,12,14},{9,11,13,15},{16,18,20,22},{17,19,21,2..., dimensions={0} | all-to-all | bytes 1114112 | tf_op jit(solution)/shard_map/all_to_all | solution.py:241
  23.7 1.9 %collective-permute-start = (bf16[4,34,16,128]{3,2,1,0:T(8,128)(2,1)S(1)}, bf16[4,34,16,128]{3,2,1,0:T(8,128)(2,1)S(1)}, u32[]{:S(2)}, u32[]{:S(2)}) collective-permute-start(bf16[4,34,16,128]{3,2,1,0:T(8,128)(2,1)S(1)} %all_to_all.5.mine), channel_id=1, source_target_pairs={{0,1},{1,0},{2,3},{3,2},{4,5},{5,4},{6,7},{7,6},{8,9},{9,8},{10,11... | collective-permute-start | bytes 1671176 | tf_op jit(solution)/shard_map/ppermute | solution.py:226
  25.6 0.0 copy-done.2
  25.6 0.1 copy.7
  25.7 0.0 copy-done.1
  25.8 2.4 %collective-permute-start.1 = (bf16[448,128]{1,0:T(8,128)(2,1)S(1)}, bf16[448,128]{1,0:T(8,128)(2,1)S(1)}, u32[]{:S(2)}, u32[]{:S(2)}) collective-permute-start(bf16[448,128]{1,0:T(8,128)(2,1)S(1)} %fusion.1.own), channel_id=1, source_target_pairs={{0,2},{1,3},{2,0},{3,1},{4,6},{5,7},{6,4},{7,5},{8,10},{9,11},{10,... | collective-permute-start | bytes 344072 | tf_op jit(solution)/shard_map/ppermute | solution.py:226
  28.2 3.3 %collective-permute-start.2 = (bf16[128,128]{1,0:T(8,128)(2,1)S(1)}, bf16[128,128]{1,0:T(8,128)(2,1)S(1)}, u32[]{:S(2)}, u32[]{:S(2)}) collective-permute-start(bf16[128,128]{1,0:T(8,128)(2,1)S(1)} %shard_map.40), channel_id=1, source_target_pairs={{2,64},{3,65},{6,68},{7,69},{64,2},{65,3},{66,128},{67,129},{68,6}... | collective-permute-start | bytes 98312 | tf_op jit(solution)/shard_map/ppermute | solution.py:222
  31.5 0.4 shard_map.41.cols
  31.9 4.2 %collective-permute-done.2.beyond = bf16[128,128]{1,0:T(8,128)(2,1)S(1)} collective-permute-done((bf16[128,128]{1,0:T(8,128)(2,1)S(1)}, bf16[128,128]{1,0:T(8,128)(2,1)S(1)}, u32[]{:S(2)}, u32[]{:S(2)}) %collective-permute-start.2) | collective-permute-done | bytes 32800 | tf_op jit(solution)/shard_map/ppermute | solution.py:222
  36.1 0.1 shard_map.42
  36.2 7.7 %collective-permute-start.4 = (bf16[128,128]{1,0:T(8,128)(2,1)S(1)}, bf16[128,128]{1,0:T(8,128)(2,1)S(1)}, u32[]{:S(2)}, u32[]{:S(2)}) collective-permute-start(bf16[128,128]{1,0:T(8,128)(2,1)S(1)} %shard_map.42), channel_id=1, source_target_pairs={{8,4},{9,5},{10,6},{11,7},{12,0},{13,1},{14,2},{15,3},{16,12},{17,... | collective-permute-start | bytes 98312 | tf_op jit(solution)/shard_map/ppermute | solution.py:211
  43.9 1.9 %collective-permute-start.3 = (bf16[128,128]{1,0:T(8,128)(2,1)S(1)}, bf16[128,128]{1,0:T(8,128)(2,1)S(1)}, u32[]{:S(2)}, u32[]{:S(2)}) collective-permute-start(bf16[128,128]{1,0:T(8,128)(2,1)S(1)} %shard_map.42), channel_id=1, source_target_pairs={{0,12},{1,13},{2,14},{3,15},{4,8},{5,9},{6,10},{7,11},{8,20},{9,21... | collective-permute-start | bytes 98312 | tf_op jit(solution)/shard_map/ppermute | solution.py:211
  45.8 0.0 collective-permute-done.4.right
  45.8 6.9 %collective-permute-done.3.left = bf16[128,128]{1,0:T(8,128)(2,1)S(1)} collective-permute-done((bf16[128,128]{1,0:T(8,128)(2,1)S(1)}, bf16[128,128]{1,0:T(8,128)(2,1)S(1)}, u32[]{:S(2)}, u32[]{:S(2)}) %collective-permute-start.3) | collective-permute-done | bytes 32800 | tf_op jit(solution)/shard_map/ppermute | solution.py:211
  52.7 0.1 shard_map.43.halo
  52.8 1.9 %collective-permute-start.5 = (bf16[256,128]{1,0:T(8,128)(2,1)S(1)}, bf16[256,128]{1,0:T(8,128)(2,1)S(1)}, u32[]{:S(2)}, u32[]{:S(2)}) collective-permute-start(bf16[256,128]{1,0:T(8,128)(2,1)S(1)} %shard_map.43.halo), channel_id=1, source_target_pairs={{0,1},{1,0},{2,3},{3,2},{4,5},{5,4},{6,7},{7,6},{8,9},{9,8},{10,11... | collective-permute-start | bytes 196616 | tf_op jit(solution)/shard_map/ppermute | solution.py:226
  54.7 0.0 collective-permute-done.1.other
  54.7 0.2 shard_map.38.taps
  54.9 0.0 collective-permute-done.theirs
  54.9 0.9 %shard_map.39.pre = f32[16,64,128]{2,1,0:T(8,128)S(1)} custom-call(bf16[4,34,16,128]{3,2,1,0:T(8,128)(2,1)S(1)} %all_to_all.5.mine, bf16[4,34,16,128]{3,2,1,0:T(8,128)(2,1)S(1)} %collective-permute-done.theirs, bf16[576,256]{1,0:T(8,128)(2,1)S(1)} %shard_map.38.taps), custom_call_target="tpu_custom_call" | custom-call | flops 603979776 | bytes 3145728 | tf_op jit(solution)/shard_map/pallas_call | solution.py:18
  55.8 0.1 collective-permute-done.5.halo2
  55.9 0.8 %shard_map.44 = (bf16[32,16,128]{2,1,0:T(8,128)(2,1)S(1)}, bf16[32,16,128]{2,1,0:T(8,128)(2,1)S(1)}) custom-call(f32[16,64,128]{2,1,0:T(8,128)S(1)} %shard_map.39.pre, bf16[576,256]{1,0:T(8,128)(2,1)S(1)} %shard_map.38.taps, bf16[4,34,16,128]{3,2,1,0:T(8,128)(2,1)S(1)} %all_to_all.5.mine, bf16[4,34,16,128]{3,2,1,0:T(8,128)(2,1)S(1)} %collective-permute-done.theirs, ...), custom_call_target="tpu_custom_call" | custom-call | flops 75497472 | bytes 2097152 | tf_op jit(solution)/shard_map/pallas_call | solution.py:18
  56.8 1.9 %collective-permute-start.6 = (bf16[32,16,128]{2,1,0:T(8,128)(2,1)S(1)}, bf16[32,16,128]{2,1,0:T(8,128)(2,1)S(1)}, u32[]{:S(2)}, u32[]{:S(2)}) collective-permute-start(bf16[32,16,128]{2,1,0:T(8,128)(2,1)S(1)} %get-tuple-element.8), channel_id=1, source_target_pairs={{0,2},{1,3},{2,0},{3,1},{4,6},{5,7},{6,4},{7,5},{8,10},{9,11},{10,... | collective-permute-start | bytes 393224 | tf_op jit(solution)/shard_map/ppermute | solution.py:226
  58.7 5.8 %collective-permute-done.6.got = bf16[32,16,128]{2,1,0:T(8,128)(2,1)S(1)} collective-permute-done((bf16[32,16,128]{2,1,0:T(8,128)(2,1)S(1)}, bf16[32,16,128]{2,1,0:T(8,128)(2,1)S(1)}, u32[]{:S(2)}, u32[]{:S(2)}) %collective-permute-start.6) | collective-permute-done | bytes 131104 | tf_op jit(solution)/shard_map/ppermute | solution.py:226
  64.5 1.2 %shard_map.45 = bf16[16,2,32,128]{3,2,1,0:T(8,128)(2,1)} custom-call(bf16[32,16,128]{2,1,0:T(8,128)(2,1)S(1)} %get-tuple-element.7.kept, bf16[32,16,128]{2,1,0:T(8,128)(2,1)S(1)} %collective-permute-done.6.got), custom_call_target="tpu_custom_call" | custom-call | bytes 524288 | tf_op jit(solution)/shard_map/pallas_call | solution.py:18
  (4 shorter events, 0.0 us)
Async XLA Ops:
  0.0 0.9 %copy-start = (bf16[16,2,32,128]{3,2,1,0:T(8,128)(2,1)S(1)}, bf16[16,2,32,128]{3,2,1,0:T(8,128)(2,1)}, u32[]{:S(2)}) copy-start(bf16[16,2,32,128]{3,2,1,0:T(8,128)(2,1)} %vol.1) | copy-start | bytes 786436
  1.3 24.3 %copy-start.2 = (f32[16]{0:T(128)S(1)}, f32[16]{0:T(128)}, u32[]{:S(2)}) copy-start(f32[16]{0:T(128)} %param.5) | copy-start | bytes 196
  1.3 24.4 %copy-start.1 = (bf16[16,128,3,3,3]{1,0,4,3,2:T(8,128)(2,1)S(1)}, bf16[16,128,3,3,3]{1,0,4,3,2:T(8,128)(2,1)}, u32[]{:S(2)}) copy-start(bf16[16,128,3,3,3]{1,0,4,3,2:T(8,128)(2,1)} %param.4) | copy-start | bytes 331780
  23.7 31.2 %collective-permute-start = (bf16[4,34,16,128]{3,2,1,0:T(8,128)(2,1)S(1)}, bf16[4,34,16,128]{3,2,1,0:T(8,128)(2,1)S(1)}, u32[]{:S(2)}, u32[]{:S(2)}) collective-permute-start(bf16[4,34,16,128]{3,2,1,0:T(8,128)(2,1)S(1)} %all_to_all.5.mine), channel_id=1, source_target_pairs={{0,1},{1,0},{2,3},{3,2},{4,5},{5,4},{6,7},{7,6},{8,9},{9,8},{10,11... | collective-permute-start | bytes 1671176 | tf_op jit(solution)/shard_map/ppermute | solution.py:226
  25.8 28.9 %collective-permute-start.1 = (bf16[448,128]{1,0:T(8,128)(2,1)S(1)}, bf16[448,128]{1,0:T(8,128)(2,1)S(1)}, u32[]{:S(2)}, u32[]{:S(2)}) collective-permute-start(bf16[448,128]{1,0:T(8,128)(2,1)S(1)} %fusion.1.own), channel_id=1, source_target_pairs={{0,2},{1,3},{2,0},{3,1},{4,6},{5,7},{6,4},{7,5},{8,10},{9,11},{10,... | collective-permute-start | bytes 344072 | tf_op jit(solution)/shard_map/ppermute | solution.py:226
  28.2 7.9 %collective-permute-start.2 = (bf16[128,128]{1,0:T(8,128)(2,1)S(1)}, bf16[128,128]{1,0:T(8,128)(2,1)S(1)}, u32[]{:S(2)}, u32[]{:S(2)}) collective-permute-start(bf16[128,128]{1,0:T(8,128)(2,1)S(1)} %shard_map.40), channel_id=1, source_target_pairs={{2,64},{3,65},{6,68},{7,69},{64,2},{65,3},{66,128},{67,129},{68,6}... | collective-permute-start | bytes 98312 | tf_op jit(solution)/shard_map/ppermute | solution.py:222
  36.2 9.6 %collective-permute-start.4 = (bf16[128,128]{1,0:T(8,128)(2,1)S(1)}, bf16[128,128]{1,0:T(8,128)(2,1)S(1)}, u32[]{:S(2)}, u32[]{:S(2)}) collective-permute-start(bf16[128,128]{1,0:T(8,128)(2,1)S(1)} %shard_map.42), channel_id=1, source_target_pairs={{8,4},{9,5},{10,6},{11,7},{12,0},{13,1},{14,2},{15,3},{16,12},{17,... | collective-permute-start | bytes 98312 | tf_op jit(solution)/shard_map/ppermute | solution.py:211
  43.9 8.8 %collective-permute-start.3 = (bf16[128,128]{1,0:T(8,128)(2,1)S(1)}, bf16[128,128]{1,0:T(8,128)(2,1)S(1)}, u32[]{:S(2)}, u32[]{:S(2)}) collective-permute-start(bf16[128,128]{1,0:T(8,128)(2,1)S(1)} %shard_map.42), channel_id=1, source_target_pairs={{0,12},{1,13},{2,14},{3,15},{4,8},{5,9},{6,10},{7,11},{8,20},{9,21... | collective-permute-start | bytes 98312 | tf_op jit(solution)/shard_map/ppermute | solution.py:211
  52.8 3.1 %collective-permute-start.5 = (bf16[256,128]{1,0:T(8,128)(2,1)S(1)}, bf16[256,128]{1,0:T(8,128)(2,1)S(1)}, u32[]{:S(2)}, u32[]{:S(2)}) collective-permute-start(bf16[256,128]{1,0:T(8,128)(2,1)S(1)} %shard_map.43.halo), channel_id=1, source_target_pairs={{0,1},{1,0},{2,3},{3,2},{4,5},{5,4},{6,7},{7,6},{8,9},{9,8},{10,11... | collective-permute-start | bytes 196616 | tf_op jit(solution)/shard_map/ppermute | solution.py:226
  56.8 7.7 %collective-permute-start.6 = (bf16[32,16,128]{2,1,0:T(8,128)(2,1)S(1)}, bf16[32,16,128]{2,1,0:T(8,128)(2,1)S(1)}, u32[]{:S(2)}, u32[]{:S(2)}) collective-permute-start(bf16[32,16,128]{2,1,0:T(8,128)(2,1)S(1)} %get-tuple-element.8), channel_id=1, source_target_pairs={{0,2},{1,3},{2,0},{3,1},{4,6},{5,7},{6,4},{7,5},{8,10},{9,11},{10,... | collective-permute-start | bytes 393224 | tf_op jit(solution)/shard_map/ppermute | solution.py:226

commit v6 on v4

v6 whole, which is shorter than its diff:
```python
import jax
import jax.numpy as jnp
from jax import lax
from jax.experimental import pallas as pl
from jax.experimental.pallas import tpu as pltpu
from jax.sharding import PartitionSpec as P


BF = jnp.bfloat16
F32 = jnp.float32
CORES = [[0, 2, 4, 6], [1, 3, 5, 7]]
GRANT = 20 << 20


def call(kernel, out_shapes, scratch, *args, flops=0, moved=0):
    vmem = pl.BlockSpec(memory_space=pltpu.VMEM)
    many = isinstance(out_shapes, (list, tuple))
    return pl.pallas_call(
        kernel,
        out_shape=out_shapes,
        in_specs=[vmem] * len(args),
        out_specs=[vmem] * len(out_shapes) if many else vmem,
        scratch_shapes=scratch,
        cost_estimate=pl.CostEstimate(flops=flops, bytes_accessed=moved, transcendentals=0),
        compiler_params=pltpu.CompilerParams(vmem_limit_bytes=GRANT),
    )(*args)


def shaped(*shape, dtype=BF):
    return jax.ShapeDtypeStruct(shape, dtype)


def lanes_of(shape):
    return lax.broadcasted_iota(jnp.int32, shape, len(shape) - 1)


def pack_kernel(vol, blocks, first, last, cols, flat):
    flat[...] = vol[...].reshape(1024, 128).astype(F32)
    for z in range(2):
        for row in range(32):
            tile = flat[pl.ds(z * 32 + row, 16, stride=64), :].astype(BF)
            for chip in range(4):
                blocks[chip, z * 32 + row] = tile
            if row == 0:
                first[pl.ds(z * 16, 16)] = tile
            if row == 31:
                last[pl.ds(z * 16, 16)] = tile
    lane = lanes_of((32, 128))
    both = jnp.zeros((32, 128), F32)
    for z in range(2):
        for c in range(16):
            tile = flat[pl.ds(c * 64 + z * 32, 32), :]
            j = z * 16 + c
            both = jnp.where(lane == j, pltpu.roll(tile, j, 1) if j else tile, both)
            both = jnp.where(lane == 32 + j, pltpu.roll(tile, 33 + j, 1), both)
    cols[...] = both.astype(BF)


def beside_kernel(first, last, left, right, up, down, beside):
    lane = lanes_of((32, 128))
    both = jnp.where(
        lane < 32,
        pltpu.roll(left[...].astype(F32), 96, 1),
        jnp.where(lane < 64, pltpu.roll(right[...].astype(F32), 32, 1), 0.0),
    )
    beside[...] = both
    nothing = jnp.zeros((15, 128), F32)
    up[pl.ds(0, 32)] = last[...]
    up[pl.ds(32, 16)] = jnp.concatenate([both[31:32], nothing], axis=0).astype(BF)
    down[pl.ds(0, 32)] = first[...]
    down[pl.ds(32, 16)] = jnp.concatenate([both[0:1], nothing], axis=0).astype(BF)


def halo_kernel(above, below, beside, out, buf):
    buf[...] = jnp.zeros((40, 128), F32)
    buf[pl.ds(0, 1), :] = above[pl.ds(32, 16)].astype(F32)[0:1]
    buf[pl.ds(1, 32), :] = beside[...]
    buf[pl.ds(33, 1), :] = below[pl.ds(32, 16)].astype(F32)[0:1]
    low, high = buf[pl.ds(0, 24), :], buf[pl.ds(16, 24), :]
    both = jnp.where(lanes_of((24, 128)) < 64, low, pltpu.roll(high, 64, 1)).astype(BF)
    for d in range(8):
        out[d, pl.ds(0, 32)] = above[pl.ds(0, 32)]
        out[d, pl.ds(32, 32)] = below[pl.ds(0, 32)]
        out[d, pl.ds(64, 24)] = both


def taps_kernel(own, taps):
    odd = lax.rem(lax.axis_index("ch"), 2) == 1
    even_block = lax.rem(lanes_of((16, 128)) // 16, 2) == 0
    for a in range(3):
        for b in range(3):
            for e in range(3):
                tile = own[pl.ds((a * 9 + b * 3 + e) * 16, 16)].astype(F32)
                swapped = jnp.where(even_block, pltpu.roll(tile, 112, 1), pltpu.roll(tile, 16, 1))
                tile = jnp.where(odd, swapped, tile).astype(BF)
                for zo in range(2):
                    zi = a - 1 + zo
                    if 0 <= zi < 2:
                        taps[pl.ds(((b * 3 + e) * 2 + zo) * 16, 16), pl.ds(zi * 128, 128)] = tile


def aligned(total, lane):
    before = jnp.where(lane == 0, 0.0, pltpu.roll(total[0:32], 1, 1))
    after = jnp.where(lane == 127, 0.0, pltpu.roll(total[64:96], 127, 1))
    return total[32:64] + (before + after)


def inner_kernel(mine, theirs, taps, pre, sums):
    lane = lanes_of((32, 128))

    def row_of(row):
        return jnp.concatenate(
            [held[chip, z * 32 + row] for z in range(2) for chip in range(4) for held in (mine, theirs)], axis=0
        )

    for p in range(16):
        pair = jnp.concatenate([row_of(2 * p), row_of(2 * p + 1)], axis=1)
        got = jnp.dot(taps[...], pair, preferred_element_type=F32)
        for h in range(2):
            for b in range(3):
                row = 2 * p + h + 1 - b
                if not 0 <= row < 32:
                    continue
                part = got[b * 96 : (b + 1) * 96, h * 128 : (h + 1) * 128]
                if not (b == 0 or (b == 1 and row == 0)):
                    part = part + sums[row]
                if b == 2 or (b == 1 and row == 31):
                    pre[row] = aligned(part, lane)
                else:
                    sums[row] = part


def outer_kernel(pre, taps, halo, bias, out, flat):
    core = lax.rem(lax.axis_index("ch"), 2)
    sources = [2 * chip + (core ^ t) for chip in range(4) for t in range(2)]
    lane40 = lanes_of((40, 128))
    total = [[jnp.zeros((40, 128), F32) for _ in range(2)] for _ in range(2)]
    for j, source in enumerate(sources):
        both = halo[source, pl.ds(64, 24)].astype(F32)
        both = jnp.concatenate([both, pltpu.roll(both[8:24], 64, 1)], axis=0)
        for side in range(2):
            for z in range(2):
                shift = (j * 16 - side * 32 - z * 16) % 128
                piece = pltpu.roll(both, shift, 1) if shift else both
                total[side][z] = jnp.where(lane40 // 16 == j, piece, total[side][z])
    beside = jnp.concatenate(
        [jnp.concatenate(total[0], axis=1), jnp.concatenate(total[1], axis=1), jnp.zeros((48, 256), F32)], axis=0
    ).astype(BF)
    edge = lax.dot_general(taps[...], beside, (((1,), (1,)), ((), ())), preferred_element_type=F32)
    before, after = (
        edge[e * 32 : e * 32 + 32]
        + pltpu.roll(edge[96 + e * 32 : 128 + e * 32], 127, 1)
        + pltpu.roll(edge[192 + e * 32 : 224 + e * 32], 126, 1)
        for e in (0, 2)
    )
    lane = lanes_of((32, 128))
    ends = []
    for side in range(2):
        beyond = jnp.concatenate(
            [halo[source, pl.ds(side * 32 + z * 16, 16)] for z in range(2) for source in sources], axis=0
        )
        near = taps[pl.ds(side * 192, 96)]
        ends.append(aligned(jnp.dot(near, beyond, preferred_element_type=F32), lane))
    offset = jnp.concatenate([bias[...], bias[...]], axis=0)
    for row in range(32):
        total = pre[row] + offset
        if row == 0:
            total = total + ends[0]
        if row == 31:
            total = total + ends[1]
        total = total + jnp.where(lane == 0, before[:, row : row + 1], 0.0)
        total = total + jnp.where(lane == 127, after[:, 40 + row : 41 + row], 0.0)
        total = jnp.where(total >= 0, total, 0.3 * total)
        for z in range(2):
            flat[pl.ds(z * 32 + row, 16, stride=64), :] = total[z * 16 : z * 16 + 16]
    out[...] = flat[...].reshape(16, 2, 32, 128).astype(BF)


def shifts(array, axis, up=True):
    size = lax.axis_size(axis)
    pairs = [(i, i + 1) for i in range(size - 1)]
    return lax.ppermute(array, axis, pairs if up else [(j, i) for i, j in pairs])


def swapped(array, t):
    return lax.ppermute(array, "ch", [(d, d ^ t) for d in range(8)])


def stages(volume, weights, bias):
    blocks, first, last, cols = call(
        pack_kernel,
        [shaped(4, 64, 16, 128), shaped(32, 128), shaped(32, 128), shaped(32, 128)],
        [pltpu.VMEM((1024, 128), F32)],
        volume,
        moved=1 << 20,
    )
    mine = lax.all_to_all(blocks, "ch", split_axis=0, concat_axis=0, tiled=True, axis_index_groups=CORES)
    left = shifts(cols, "sy", True)
    right = shifts(cols, "sy", False)
    own = weights.transpose(2, 3, 4, 0, 1).reshape(432, 128)
    taps = call(taps_kernel, shaped(288, 256), [], own, moved=1 << 19)
    spread = jnp.broadcast_to(bias[:, None], (16, 128))
    up, down, beside = call(
        beside_kernel,
        [shaped(48, 128), shaped(48, 128), shaped(32, 128, dtype=F32)],
        [],
        first,
        last,
        left,
        right,
        moved=1 << 16,
    )
    above = shifts(up, "sx", True)
    below = shifts(down, "sx", False)
    theirs = swapped(mine, 1)
    halo = call(halo_kernel, shaped(8, 88, 128), [pltpu.VMEM((40, 128), F32)], above, below, beside, moved=1 << 17)
    halo = lax.all_to_all(halo, "ch", split_axis=0, concat_axis=0, tiled=True)
    pre = call(
        inner_kernel,
        shaped(32, 32, 128, dtype=F32),
        [pltpu.VMEM((32, 96, 128), F32)],
        mine,
        theirs,
        taps,
        flops=2 * 288 * 256 * 4096,
        moved=3 << 20,
    )
    return call(
        outer_kernel,
        shaped(16, 2, 32, 128),
        [pltpu.VMEM((1024, 128), F32)],
        pre,
        taps,
        halo,
        spread,
        flops=2 * 288 * 256 * 256,
        moved=2 << 20,
    )


def solution(mesh):
    in_specs = (P("ch", None, "sx", "sy"), P("ch", None, None, None, None), P("ch"))
    out_specs = P("ch", None, "sx", "sy")
    return jax.shard_map(stages, mesh=mesh, in_specs=in_specs, out_specs=out_specs, check_vma=False)
```

time: 65.1 us -> 79.9 us (1.23)
  blocking collectives: 0 us -> 32.8 us
  starting transfers between devices: 38 us -> 22.7 us
  waiting for transfers between devices: 20.4 us -> 18.7 us
  Pallas kernels: 5.06 us -> 4.14 us
    all_to_all x0 -> x1, blocking collectives: none -> 32.8 us  [stages(): lax.all_to_all(blocks, 'ch', split_axis=0, concat_axis=0, tiled=True, axi...]
    ppermute x3 -> x1, waiting for transfers between devices: 9.05 us -> 0.01 us  [swapped(): return lax.ppermute(array, 'ch', [(d, d ^ t) for d in range(8)])]
    all_to_all x1 -> x0, starting transfers between devices: 7.26 us -> none  [stages(): lax.all_to_all(blocks, 'ch', split_axis=0, concat_axis=0, tiled=True, axi...]
    all_to_all x1, waiting for transfers between devices: 0.01 us -> 6.85 us  [stages(): halo = lax.all_to_all(halo, 'ch', split_axis=0, concat_axis=0, tiled=True)]
    ppermute x3 -> x1, starting transfers between devices: 8.46 us -> 1.91 us  [swapped(): return lax.ppermute(array, 'ch', [(d, d ^ t) for d in range(8)])]
    ppermute x4, waiting for transfers between devices: 6.24 us -> 11.9 us  [shifts(): lax.ppermute(array, axis, pairs if up else [(j, i) for i, j in pairs])]
    all_to_all x1 -> x0, waiting for transfers between devices: 5.09 us -> none  [stages(): lax.all_to_all(blocks, 'ch', split_axis=0, concat_axis=0, tiled=True, axi...]
    all_to_all x1, starting transfers between devices: 5.13 us -> 3.52 us  [stages(): halo = lax.all_to_all(halo, 'ch', split_axis=0, concat_axis=0, tiled=True)]
  transfers between devices with their start and end apart: 9 -> 6, of which waited for: 5 -> 3; matrix products, arithmetic and copies ran while one was open for 0% -> 0% of each run, Pallas kernels for 3% -> 2%
where the time goes in v6:
time: 79.9 us; the launch traced here: 79.5 us
  blocking collectives  32.8 us (41%)
  starting transfers between devices  22.7 us (28%)
  waiting for transfers between devices  18.7 us (23%)
  Pallas kernels  4.14 us (5%)
  local copies, waits for them, and re-layouts  1.03 us (1%)
    all_to_all x1, blocking collectives, stages(): lax.all_to_all(blocks, 'ch', split_axis=0, concat_axis=0, tiled=True, axi...  32.8 us
    ppermute x4, starting transfers between devices, shifts(): lax.ppermute(array, axis, pairs if up else [(j, i) for i, j in pairs])  17.3 us
    ppermute x4, waiting for transfers between devices, shifts(): lax.ppermute(array, axis, pairs if up else [(j, i) for i, j in pairs])  11.9 us
    all_to_all x1, waiting for transfers between devices, stages(): halo = lax.all_to_all(halo, 'ch', split_axis=0, concat_axis=0, tiled=True)  6.85 us
    pallas_call x6, Pallas kernels, call(): pl.pallas_call(kernel, out_shape=out_shapes, in_specs=[vmem] * len(args),...  4.14 us
    all_to_all x1, starting transfers between devices, stages(): halo = lax.all_to_all(halo, 'ch', split_axis=0, concat_axis=0, tiled=True)  3.52 us
    ppermute x1, starting transfers between devices, swapped(): return lax.ppermute(array, 'ch', [(d, d ^ t) for d in range(8)])  1.91 us
  transfers between devices with their start and end apart: 6, of which 3 were waited for; matrix products, arithmetic and copies ran while one was open for 0% of the time, Pallas kernels for 2%

profile of v6, /device:TPU:30, one launch (start us, length us, event | category | flops | bytes accessed | tf_op | source)
XLA Modules:
  0.0 79.5 jit_solution(3352666671389353418)
XLA Ops:
  0.0 0.0 copy-start
  0.0 0.9 %copy-done = bf16[16,2,32,128]{3,2,1,0:T(8,128)(2,1)S(1)} copy-done((bf16[16,2,32,128]{3,2,1,0:T(8,128)(2,1)S(1)}, bf16[16,2,32,128]{3,2,1,0:T(8,128)(2,1)}, u32[]{:S(2)}) %copy-start) | copy-done | bytes 262168
  1.0 0.5 shard_map.37
  1.4 32.8 %all_to_all.10.mine = bf16[4,64,16,128]{3,2,1,0:T(8,128)(2,1)S(1)} all-to-all(bf16[4,64,16,128]{3,2,1,0:T(8,128)(2,1)S(1)} %get-tuple-element.12), channel_id=1, replica_groups={{0,2,4,6},{1,3,5,7},{8,10,12,14},{9,11,13,15},{16,18,20,22},{17,19,21,2..., dimensions={0} | all-to-all | bytes 2097152 | tf_op jit(solution)/shard_map/all_to_all | solution.py:197
  34.2 1.9 %collective-permute-start = (bf16[4,64,16,128]{3,2,1,0:T(8,128)(2,1)S(1)}, bf16[4,64,16,128]{3,2,1,0:T(8,128)(2,1)S(1)}, u32[]{:S(2)}, u32[]{:S(2)}) collective-permute-start(bf16[4,64,16,128]{3,2,1,0:T(8,128)(2,1)S(1)} %all_to_all.10.mine), channel_id=1, source_target_pairs={{0,1},{1,0},{2,3},{3,2},{4,5},{5,4},{6,7},{7,6},{8,9},{9,8},{10,11... | collective-permute-start | bytes 3145736 | tf_op jit(solution)/shard_map/ppermute | solution.py:186
  36.1 8.2 %collective-permute-start.1 = (bf16[32,128]{1,0:T(8,128)(2,1)S(1)}, bf16[32,128]{1,0:T(8,128)(2,1)S(1)}, u32[]{:S(2)}, u32[]{:S(2)}) collective-permute-start(bf16[32,128]{1,0:T(8,128)(2,1)S(1)} %get-tuple-element.15), channel_id=1, source_target_pairs={{0,8},{8,16},{16,24},{24,32},{32,40},{40,48},{48,56},{1,9},{9,17},... | collective-permute-start | bytes 24584 | tf_op jit(solution)/shard_map/ppermute | solution.py:182
  44.4 2.4 %collective-permute-start.2 = (bf16[32,128]{1,0:T(8,128)(2,1)S(1)}, bf16[32,128]{1,0:T(8,128)(2,1)S(1)}, u32[]{:S(2)}, u32[]{:S(2)}) collective-permute-start(bf16[32,128]{1,0:T(8,128)(2,1)S(1)} %get-tuple-element.15), channel_id=1, source_target_pairs={{8,0},{16,8},{24,16},{32,24},{40,32},{48,40},{56,48},{9,1},{17,9},... | collective-permute-start | bytes 24584 | tf_op jit(solution)/shard_map/ppermute | solution.py:182
  46.8 0.0 collective-permute-done.1.left
  46.8 7.0 %collective-permute-done.2.right = bf16[32,128]{1,0:T(8,128)(2,1)S(1)} collective-permute-done((bf16[32,128]{1,0:T(8,128)(2,1)S(1)}, bf16[32,128]{1,0:T(8,128)(2,1)S(1)}, u32[]{:S(2)}, u32[]{:S(2)}) %collective-permute-start.2) | collective-permute-done | bytes 8224 | tf_op jit(solution)/shard_map/ppermute | solution.py:182
  53.8 0.1 shard_map.40
  53.9 4.7 %collective-permute-start.3 = (bf16[48,128]{1,0:T(8,128)(2,1)S(1)}, bf16[48,128]{1,0:T(8,128)(2,1)S(1)}, u32[]{:S(2)}, u32[]{:S(2)}) collective-permute-start(bf16[48,128]{1,0:T(8,128)(2,1)S(1)} %get-tuple-element.16), channel_id=1, source_target_pairs={{0,64},{64,128},{128,192},{192,256},{256,320},{320,384},{384,448},... | collective-permute-start | bytes 36872 | tf_op jit(solution)/shard_map/ppermute | solution.py:182
  58.6 1.9 %collective-permute-start.4 = (bf16[48,128]{1,0:T(8,128)(2,1)S(1)}, bf16[48,128]{1,0:T(8,128)(2,1)S(1)}, u32[]{:S(2)}, u32[]{:S(2)}) collective-permute-start(bf16[48,128]{1,0:T(8,128)(2,1)S(1)} %get-tuple-element.17), channel_id=1, source_target_pairs={{64,0},{128,64},{192,128},{256,192},{320,256},{384,320},{448,384},... | collective-permute-start | bytes 36872 | tf_op jit(solution)/shard_map/ppermute | solution.py:182
  60.5 0.0 collective-permute-done.3.above
  60.5 4.9 %collective-permute-done.4.below = bf16[48,128]{1,0:T(8,128)(2,1)S(1)} collective-permute-done((bf16[48,128]{1,0:T(8,128)(2,1)S(1)}, bf16[48,128]{1,0:T(8,128)(2,1)S(1)}, u32[]{:S(2)}, u32[]{:S(2)}) %collective-permute-start.4) | collective-permute-done | bytes 12320 | tf_op jit(solution)/shard_map/ppermute | solution.py:182
  65.4 0.8 shard_map.41
  66.1 0.0 copy-start.1
  66.1 3.5 %all-to-all-start.1 = ((bf16[8,88,128]{2,1,0:T(8,128)(2,1)}), bf16[8,88,128]{2,1,0:T(8,128)(2,1)S(1)}, u32[]{:S(2)}, u32[]{:S(2)}) async-start(bf16[8,88,128]{2,1,0:T(8,128)(2,1)} %shard_map.41), calls=%async_computation.1 | async-start | bytes 360448 | tf_op jit(solution)/shard_map/all_to_all | solution.py:217
  69.7 0.0 copy-done.1
  69.7 0.1 shard_map.38.taps
  69.8 0.0 copy-start.2
  69.8 0.0 collective-permute-done.theirs
  69.8 0.9 %shard_map.39.pre = f32[32,32,128]{2,1,0:T(8,128)S(1)} custom-call(bf16[4,64,16,128]{3,2,1,0:T(8,128)(2,1)S(1)} %all_to_all.10.mine, bf16[4,64,16,128]{3,2,1,0:T(8,128)(2,1)S(1)} %collective-permute-done.theirs, bf16[288,256]{1,0:T(8,128)(2,1)S(1)} %shard_map.38.taps), custom_call_target="tpu_custom_call" | custom-call | flops 603979776 | bytes 3145728 | tf_op jit(solution)/shard_map/pallas_call | solution.py:18
  70.7 6.9 %all-to-all-done.1.halo = bf16[8,88,128]{2,1,0:T(8,128)(2,1)S(1)} async-done(((bf16[8,88,128]{2,1,0:T(8,128)(2,1)}), bf16[8,88,128]{2,1,0:T(8,128)(2,1)S(1)}, u32[]{:S(2)}, u32[]{:S(2)}) %all-to-all-start.1) | async-done | bytes 180256 | tf_op jit(solution)/shard_map/all_to_all | solution.py:217
  77.5 0.0 copy-done.2
  77.5 0.1 broadcast_in_dim.2.bias
  77.6 1.9 %shard_map.42 = bf16[16,2,32,128]{3,2,1,0:T(8,128)(2,1)} custom-call(f32[32,32,128]{2,1,0:T(8,128)S(1)} %shard_map.39.pre, bf16[288,256]{1,0:T(8,128)(2,1)S(1)} %shard_map.38.taps, bf16[8,88,128]{2,1,0:T(8,128)(2,1)S(1)} %all-to-all-done.1.halo, f32[16,128]{1,0:T(8,128)S(1)} %broadcast_in_dim.2.bias), custom_call_target="tpu_custom_call" | custom-call | flops 37748736 | bytes 2097152 | tf_op jit(solution)/shard_map/pallas_call | solution.py:18
Async XLA Ops:
  0.0 0.9 %copy-start = (bf16[16,2,32,128]{3,2,1,0:T(8,128)(2,1)S(1)}, bf16[16,2,32,128]{3,2,1,0:T(8,128)(2,1)}, u32[]{:S(2)}) copy-start(bf16[16,2,32,128]{3,2,1,0:T(8,128)(2,1)} %vol.1) | copy-start | bytes 786436
  34.2 35.6 %collective-permute-start = (bf16[4,64,16,128]{3,2,1,0:T(8,128)(2,1)S(1)}, bf16[4,64,16,128]{3,2,1,0:T(8,128)(2,1)S(1)}, u32[]{:S(2)}, u32[]{:S(2)}) collective-permute-start(bf16[4,64,16,128]{3,2,1,0:T(8,128)(2,1)S(1)} %all_to_all.10.mine), channel_id=1, source_target_pairs={{0,1},{1,0},{2,3},{3,2},{4,5},{5,4},{6,7},{7,6},{8,9},{9,8},{10,11... | collective-permute-start | bytes 3145736 | tf_op jit(solution)/shard_map/ppermute | solution.py:186
  36.1 10.7 %collective-permute-start.1 = (bf16[32,128]{1,0:T(8,128)(2,1)S(1)}, bf16[32,128]{1,0:T(8,128)(2,1)S(1)}, u32[]{:S(2)}, u32[]{:S(2)}) collective-permute-start(bf16[32,128]{1,0:T(8,128)(2,1)S(1)} %get-tuple-element.15), channel_id=1, source_target_pairs={{0,8},{8,16},{16,24},{24,32},{32,40},{40,48},{48,56},{1,9},{9,17},... | collective-permute-start | bytes 24584 | tf_op jit(solution)/shard_map/ppermute | solution.py:182
  44.4 9.5 %collective-permute-start.2 = (bf16[32,128]{1,0:T(8,128)(2,1)S(1)}, bf16[32,128]{1,0:T(8,128)(2,1)S(1)}, u32[]{:S(2)}, u32[]{:S(2)}) collective-permute-start(bf16[32,128]{1,0:T(8,128)(2,1)S(1)} %get-tuple-element.15), channel_id=1, source_target_pairs={{8,0},{16,8},{24,16},{32,24},{40,32},{48,40},{56,48},{9,1},{17,9},... | collective-permute-start | bytes 24584 | tf_op jit(solution)/shard_map/ppermute | solution.py:182
  53.9 6.6 %collective-permute-start.3 = (bf16[48,128]{1,0:T(8,128)(2,1)S(1)}, bf16[48,128]{1,0:T(8,128)(2,1)S(1)}, u32[]{:S(2)}, u32[]{:S(2)}) collective-permute-start(bf16[48,128]{1,0:T(8,128)(2,1)S(1)} %get-tuple-element.16), channel_id=1, source_target_pairs={{0,64},{64,128},{128,192},{192,256},{256,320},{320,384},{384,448},... | collective-permute-start | bytes 36872 | tf_op jit(solution)/shard_map/ppermute | solution.py:182
  58.6 6.8 %collective-permute-start.4 = (bf16[48,128]{1,0:T(8,128)(2,1)S(1)}, bf16[48,128]{1,0:T(8,128)(2,1)S(1)}, u32[]{:S(2)}, u32[]{:S(2)}) collective-permute-start(bf16[48,128]{1,0:T(8,128)(2,1)S(1)} %get-tuple-element.17), channel_id=1, source_target_pairs={{64,0},{128,64},{192,128},{256,192},{320,256},{384,320},{448,384},... | collective-permute-start | bytes 36872 | tf_op jit(solution)/shard_map/ppermute | solution.py:182
  66.1 3.5 %copy-start.1 = (bf16[16,128,3,3,3]{1,0,4,3,2:T(8,128)(2,1)S(1)}, bf16[16,128,3,3,3]{1,0,4,3,2:T(8,128)(2,1)}, u32[]{:S(2)}) copy-start(bf16[16,128,3,3,3]{1,0,4,3,2:T(8,128)(2,1)} %param.4) | copy-start | bytes 331780
  66.1 11.4 %all-to-all-start.1 = ((bf16[8,88,128]{2,1,0:T(8,128)(2,1)}), bf16[8,88,128]{2,1,0:T(8,128)(2,1)S(1)}, u32[]{:S(2)}, u32[]{:S(2)}) async-start(bf16[8,88,128]{2,1,0:T(8,128)(2,1)} %shard_map.41), calls=%async_computation.1 | async-start | bytes 360448 | tf_op jit(solution)/shard_map/all_to_all | solution.py:217
  69.8 7.7 %copy-start.2 = (f32[16]{0:T(128)S(1)}, f32[16]{0:T(128)}, u32[]{:S(2)}) copy-start(f32[16]{0:T(128)} %param.5) | copy-start | bytes 196

commit v7 on v4

--- a/solution.py
+++ b/solution.py
@@ -58,30 +58,29 @@
     cols[...] = both.astype(BF)
 
 
-def beside_kernel(first, last, left, right, up, down, beside):
-    lane = lanes_of((32, 128))
+def corner_kernel(cols, top, bottom, side, buf):
+    both = jnp.concatenate(
+        [top[...].astype(F32), bottom[...].astype(F32), jnp.zeros((64, 128), F32)], axis=0
+    )
+    turned = both.T
+    first, last = turned[0:1, :], turned[127:128, :]
+    lane = lanes_of((1, 128))
+    buf[...] = jnp.zeros((40, 128), F32)
+    buf[pl.ds(1, 32), :] = cols[...].astype(F32)
+    buf[pl.ds(0, 1), :] = jnp.where(lane < 32, first, pltpu.roll(last, 32, 1))
+    buf[pl.ds(33, 1), :] = jnp.where(lane < 32, pltpu.roll(first, 96, 1), last)
+    side[...] = buf[...].astype(BF)
+
+
+def halo_kernel(top, bottom, left, right, out):
+    lane = lanes_of((40, 128))
     both = jnp.where(
-        lane < 32,
-        pltpu.roll(left[...].astype(F32), 96, 1),
-        jnp.where(lane < 64, pltpu.roll(right[...].astype(F32), 32, 1), 0.0),
-    )
-    beside[...] = both
-    nothing = jnp.zeros((15, 128), F32)
-    up[pl.ds(0, 32)] = last[...]
-    up[pl.ds(32, 16)] = jnp.concatenate([both[31:32], nothing], axis=0).astype(BF)
-    down[pl.ds(0, 32)] = first[...]
-    down[pl.ds(32, 16)] = jnp.concatenate([both[0:1], nothing], axis=0).astype(BF)
-
-
-def halo_kernel(above, below, beside, out, buf):
-    buf[...] = jnp.zeros((40, 128), F32)
-    buf[pl.ds(0, 1), :] = above[pl.ds(32, 16)].astype(F32)[0:1]
-    buf[pl.ds(1, 32), :] = beside[...]
-    buf[pl.ds(33, 1), :] = below[pl.ds(32, 16)].astype(F32)[0:1]
+        lane < 32, pltpu.roll(left[...].astype(F32), 96, 1), pltpu.roll(right[...].astype(F32), 32, 1)
+    )
     for d in range(8):
         half = d // 2 % 2
-        out[d, pl.ds(0, 32)] = below[pl.ds(0, 32)] if half else above[pl.ds(0, 32)]
-        out[d, pl.ds(32, 24)] = buf[pl.ds(16 * half, 24), :].astype(BF)
+        out[d, pl.ds(0, 32)] = bottom[...] if half else top[...]
+        out[d, pl.ds(32, 24)] = both[16 * half : 16 * half + 24].astype(BF)
 
 
 def taps_kernel(own, other, taps):
@@ -233,25 +232,16 @@
         moved=1 << 20,
     )
     mine = lax.all_to_all(blocks, "ch", split_axis=0, concat_axis=0, tiled=True, axis_index_groups=CORES)
-    left = shifts(cols, "sy", True)
-    right = shifts(cols, "sy", False)
+    top = shifts(last, "sx", True)
+    bottom = shifts(first, "sx", False)
     own = jnp.concatenate([weights.transpose(2, 3, 4, 0, 1).reshape(432, 128), thirds(bias)], axis=0)
     other = swapped(own, 2)
-    up, down, beside = call(
-        beside_kernel,
-        [shaped(48, 128), shaped(48, 128), shaped(32, 128, dtype=F32)],
-        [],
-        first,
-        last,
-        left,
-        right,
-        moved=1 << 16,
-    )
-    above = shifts(up, "sx", True)
-    below = shifts(down, "sx", False)
+    side = call(corner_kernel, shaped(40, 128), [pltpu.VMEM((40, 128), F32)], cols, top, bottom, moved=1 << 16)
+    left = shifts(side, "sy", True)
+    right = shifts(side, "sy", False)
     theirs = swapped(mine, 1)
     taps = call(taps_kernel, shaped(576, 256), [], own, other, moved=1 << 19)
-    halo = call(halo_kernel, shaped(8, 56, 128), [pltpu.VMEM((40, 128), F32)], above, below, beside, moved=1 << 17)
+    halo = call(halo_kernel, shaped(8, 56, 128), [], top, bottom, left, right, moved=1 << 17)
     halo = lax.all_to_all(halo, "ch", split_axis=0, concat_axis=0, tiled=True)
     pre = call(
         inner_kernel,

time: 65.1 us -> 69 us (1.060)
  the two profiles are of different devices: /device:TPU:30 before, /device:TPU:6 now
where the time goes in v7:
time: 69 us; the launch traced here: 68.5 us
  starting transfers between devices  34.4 us (50%)
  waiting for transfers between devices  27.6 us (40%)
  Pallas kernels  5.2 us (8%)
  local copies, waits for them, and re-layouts  1.05 us (2%)
    ppermute x4, starting transfers between devices, shifts(): lax.ppermute(array, axis, pairs if up else [(j, i) for i, j in pairs])  15.3 us
    all_to_all x1, waiting for transfers between devices, stages(): lax.all_to_all(blocks, 'ch', split_axis=0, concat_axis=0, tiled=True, axi...  10.3 us
    ppermute x3, waiting for transfers between devices, swapped(): return lax.ppermute(array, 'ch', [(d, d ^ t) for d in range(8)])  9.01 us
    ppermute x3, starting transfers between devices, swapped(): return lax.ppermute(array, 'ch', [(d, d ^ t) for d in range(8)])  8.37 us
    ppermute x4, waiting for transfers between devices, shifts(): lax.ppermute(array, axis, pairs if up else [(j, i) for i, j in pairs])  8.34 us
    all_to_all x1, starting transfers between devices, stages(): lax.all_to_all(blocks, 'ch', split_axis=0, concat_axis=0, tiled=True, axi...  7.26 us
    pallas_call x7, Pallas kernels, call(): pl.pallas_call(kernel, out_shape=out_shapes, in_specs=[vmem] * len(args),...  5.2 us
    all_to_all x1, starting transfers between devices, stages(): halo = lax.all_to_all(halo, 'ch', split_axis=0, concat_axis=0, tiled=True)  3.5 us
  transfers between devices with their start and end apart: 9, of which 4 were waited for; matrix products, arithmetic and copies ran while one was open for 0% of the time, Pallas kernels for 3%

profile of v7, /device:TPU:6, one launch (start us, length us, event | category | flops | bytes accessed | tf_op | source)
XLA Modules:
  0.0 68.5 jit_solution(12819367972249999101)
XLA Ops:
  0.0 0.0 copy-start
  0.0 0.9 %copy-done = bf16[16,2,32,128]{3,2,1,0:T(8,128)(2,1)S(1)} copy-done((bf16[16,2,32,128]{3,2,1,0:T(8,128)(2,1)S(1)}, bf16[16,2,32,128]{3,2,1,0:T(8,128)(2,1)}, u32[]{:S(2)}) %copy-start) | copy-done | bytes 262168
  1.0 1.2 %shard_map.37 = (bf16[4,34,16,128]{3,2,1,0:T(8,128)(2,1)}, bf16[32,128]{1,0:T(8,128)(2,1)S(1)}, bf16[32,128]{1,0:T(8,128)(2,1)S(1)}, bf16[32,128]{1,0:T(8,128)(2,1)S(1)}) custom-call(bf16[16,2,32,128]{3,2,1,0:T(8,128)(2,1)S(1)} %copy-done), custom_call_target="tpu_custom_call" | custom-call | bytes 1048576 | tf_op jit(solution)/shard_map/pallas_call | solution.py:18
  2.2 7.3 %all-to-all-start = ((bf16[4,34,16,128]{3,2,1,0:T(8,128)(2,1)}), bf16[4,34,16,128]{3,2,1,0:T(8,128)(2,1)S(1)}, u32[]{:S(2)}, u32[]{:S(2)}) async-start(bf16[4,34,16,128]{3,2,1,0:T(8,128)(2,1)} %get-tuple-element.11), calls=%async_computation | async-start | bytes 1114112 | tf_op jit(solution)/shard_map/all_to_all | solution.py:234
  9.4 0.0 copy-start.2
  9.4 3.6 %collective-permute-start.2 = (bf16[32,128]{1,0:T(8,128)(2,1)S(1)}, bf16[32,128]{1,0:T(8,128)(2,1)S(1)}, u32[]{:S(2)}, u32[]{:S(2)}) collective-permute-start(bf16[32,128]{1,0:T(8,128)(2,1)S(1)} %get-tuple-element.12), channel_id=1, source_target_pairs={{0,64},{64,128},{128,192},{192,256},{256,320},{320,384},{384,448},... | collective-permute-start | bytes 24584 | tf_op jit(solution)/shard_map/ppermute | solution.py:211
  13.0 1.3 %collective-permute-start.3 = (bf16[32,128]{1,0:T(8,128)(2,1)S(1)}, bf16[32,128]{1,0:T(8,128)(2,1)S(1)}, u32[]{:S(2)}, u32[]{:S(2)}) collective-permute-start(bf16[32,128]{1,0:T(8,128)(2,1)S(1)} %get-tuple-element.13), channel_id=1, source_target_pairs={{64,0},{128,64},{192,128},{256,192},{320,256},{384,320},{448,384},... | collective-permute-start | bytes 24584 | tf_op jit(solution)/shard_map/ppermute | solution.py:211
  14.3 10.3 %all-to-all-done.mine = bf16[4,34,16,128]{3,2,1,0:T(8,128)(2,1)S(1)} async-done(((bf16[4,34,16,128]{3,2,1,0:T(8,128)(2,1)}), bf16[4,34,16,128]{3,2,1,0:T(8,128)(2,1)S(1)}, u32[]{:S(2)}, u32[]{:S(2)}) %all-to-all-start) | async-done | bytes 557088 | tf_op jit(solution)/shard_map/all_to_all | solution.py:234
  24.6 1.9 %collective-permute-start = (bf16[4,34,16,128]{3,2,1,0:T(8,128)(2,1)S(1)}, bf16[4,34,16,128]{3,2,1,0:T(8,128)(2,1)S(1)}, u32[]{:S(2)}, u32[]{:S(2)}) collective-permute-start(bf16[4,34,16,128]{3,2,1,0:T(8,128)(2,1)S(1)} %all-to-all-done.mine), channel_id=1, source_target_pairs={{0,1},{1,0},{2,3},{3,2},{4,5},{5,4},{6,7},{7,6},{8,9},{9,8},{10,11... | collective-permute-start | bytes 1671176 | tf_op jit(solution)/shard_map/ppermute | solution.py:215
  26.5 0.0 copy-done.2
  26.6 0.0 collective-permute-done.2.top
  26.6 0.0 collective-permute-done.3.bottom
  26.6 0.2 shard_map.40
  26.7 8.5 %collective-permute-start.5 = (bf16[40,128]{1,0:T(8,128)(2,1)S(1)}, bf16[40,128]{1,0:T(8,128)(2,1)S(1)}, u32[]{:S(2)}, u32[]{:S(2)}) collective-permute-start(bf16[40,128]{1,0:T(8,128)(2,1)S(1)} %shard_map.40), channel_id=1, source_target_pairs={{8,0},{16,8},{24,16},{32,24},{40,32},{48,40},{56,48},{9,1},{17,9},... | collective-permute-start | bytes 30728 | tf_op jit(solution)/shard_map/ppermute | solution.py:211
  35.3 1.9 %collective-permute-start.4 = (bf16[40,128]{1,0:T(8,128)(2,1)S(1)}, bf16[40,128]{1,0:T(8,128)(2,1)S(1)}, u32[]{:S(2)}, u32[]{:S(2)}) collective-permute-start(bf16[40,128]{1,0:T(8,128)(2,1)S(1)} %shard_map.40), channel_id=1, source_target_pairs={{0,8},{8,16},{16,24},{24,32},{32,40},{40,48},{48,56},{1,9},{9,17},... | collective-permute-start | bytes 30728 | tf_op jit(solution)/shard_map/ppermute | solution.py:211
  37.2 0.1 copy.7
  37.3 0.0 collective-permute-done.5.right
  37.3 8.3 %collective-permute-done.4.left = bf16[40,128]{1,0:T(8,128)(2,1)S(1)} collective-permute-done((bf16[40,128]{1,0:T(8,128)(2,1)S(1)}, bf16[40,128]{1,0:T(8,128)(2,1)S(1)}, u32[]{:S(2)}, u32[]{:S(2)}) %collective-permute-start.4) | collective-permute-done | bytes 10272 | tf_op jit(solution)/shard_map/ppermute | solution.py:211
  45.6 0.7 %shard_map.41 = bf16[8,56,128]{2,1,0:T(8,128)(2,1)} custom-call(bf16[32,128]{1,0:T(8,128)(2,1)S(1)} %collective-permute-done.2.top, bf16[32,128]{1,0:T(8,128)(2,1)S(1)} %collective-permute-done.3.bottom, bf16[40,128]{1,0:T(8,128)(2,1)S(1)} %collective-permute-done.4.left, bf16[40,128]{1,0:T(8,128)(2,1)S(1)} %collective-permute-done.5.right), custom_call_target="tpu_custom_call" | custom-call | bytes 131072 | tf_op jit(solution)/shard_map/pallas_call | solution.py:18
  46.4 0.0 copy-start.1
  46.4 3.5 %all-to-all-start.1 = ((bf16[8,56,128]{2,1,0:T(8,128)(2,1)}), bf16[8,56,128]{2,1,0:T(8,128)(2,1)S(1)}, u32[]{:S(2)}, u32[]{:S(2)}) async-start(bf16[8,56,128]{2,1,0:T(8,128)(2,1)} %shard_map.41), calls=%async_computation.1 | async-start | bytes 229376 | tf_op jit(solution)/shard_map/all_to_all | solution.py:245
  49.9 0.0 copy-done.1
  49.9 3.8 %collective-permute-start.1 = (bf16[448,128]{1,0:T(8,128)(2,1)S(1)}, bf16[448,128]{1,0:T(8,128)(2,1)S(1)}, u32[]{:S(2)}, u32[]{:S(2)}) collective-permute-start(bf16[448,128]{1,0:T(8,128)(2,1)S(1)} %fusion.1.own), channel_id=1, source_target_pairs={{0,2},{1,3},{2,0},{3,1},{4,6},{5,7},{6,4},{7,5},{8,10},{9,11},{10,... | collective-permute-start | bytes 344072 | tf_op jit(solution)/shard_map/ppermute | solution.py:215
  53.7 4.4 %collective-permute-done.1.other = bf16[448,128]{1,0:T(8,128)(2,1)S(1)} collective-permute-done((bf16[448,128]{1,0:T(8,128)(2,1)S(1)}, bf16[448,128]{1,0:T(8,128)(2,1)S(1)}, u32[]{:S(2)}, u32[]{:S(2)}) %collective-permute-start.1) | collective-permute-done | bytes 114720 | tf_op jit(solution)/shard_map/ppermute | solution.py:215
  58.2 0.2 shard_map.38.taps
  58.3 0.0 collective-permute-done.theirs
  58.3 0.9 %shard_map.39.pre = f32[16,64,128]{2,1,0:T(8,128)S(1)} custom-call(bf16[4,34,16,128]{3,2,1,0:T(8,128)(2,1)S(1)} %all-to-all-done.mine, bf16[4,34,16,128]{3,2,1,0:T(8,128)(2,1)S(1)} %collective-permute-done.theirs, bf16[576,256]{1,0:T(8,128)(2,1)S(1)} %shard_map.38.taps), custom_call_target="tpu_custom_call" | custom-call | flops 603979776 | bytes 3145728 | tf_op jit(solution)/shard_map/pallas_call | solution.py:18
  59.2 0.0 all-to-all-done.1.halo
  59.2 0.9 %shard_map.42 = (bf16[32,16,128]{2,1,0:T(8,128)(2,1)S(1)}, bf16[32,16,128]{2,1,0:T(8,128)(2,1)S(1)}) custom-call(f32[16,64,128]{2,1,0:T(8,128)S(1)} %shard_map.39.pre, bf16[576,256]{1,0:T(8,128)(2,1)S(1)} %shard_map.38.taps, bf16[4,34,16,128]{3,2,1,0:T(8,128)(2,1)S(1)} %all-to-all-done.mine, bf16[4,34,16,128]{3,2,1,0:T(8,128)(2,1)S(1)} %collective-permute-done.theirs, ...), custom_call_target="tpu_custom_call" | custom-call | flops 75497472 | bytes 2097152 | tf_op jit(solution)/shard_map/pallas_call | solution.py:18
  60.1 2.6 %collective-permute-start.6 = (bf16[32,16,128]{2,1,0:T(8,128)(2,1)S(1)}, bf16[32,16,128]{2,1,0:T(8,128)(2,1)S(1)}, u32[]{:S(2)}, u32[]{:S(2)}) collective-permute-start(bf16[32,16,128]{2,1,0:T(8,128)(2,1)S(1)} %get-tuple-element.16), channel_id=1, source_target_pairs={{0,2},{1,3},{2,0},{3,1},{4,6},{5,7},{6,4},{7,5},{8,10},{9,11},{10,... | collective-permute-start | bytes 393224 | tf_op jit(solution)/shard_map/ppermute | solution.py:215
  62.8 4.6 %collective-permute-done.6.got = bf16[32,16,128]{2,1,0:T(8,128)(2,1)S(1)} collective-permute-done((bf16[32,16,128]{2,1,0:T(8,128)(2,1)S(1)}, bf16[32,16,128]{2,1,0:T(8,128)(2,1)S(1)}, u32[]{:S(2)}, u32[]{:S(2)}) %collective-permute-start.6) | collective-permute-done | bytes 131104 | tf_op jit(solution)/shard_map/ppermute | solution.py:215
  67.4 1.2 %shard_map.43 = bf16[16,2,32,128]{3,2,1,0:T(8,128)(2,1)} custom-call(bf16[32,16,128]{2,1,0:T(8,128)(2,1)S(1)} %get-tuple-element.15.kept, bf16[32,16,128]{2,1,0:T(8,128)(2,1)S(1)} %collective-permute-done.6.got), custom_call_target="tpu_custom_call" | custom-call | bytes 524288 | tf_op jit(solution)/shard_map/pallas_call | solution.py:18
  (3 shorter events, 0.0 us)
Async XLA Ops:
  0.0 0.9 %copy-start = (bf16[16,2,32,128]{3,2,1,0:T(8,128)(2,1)S(1)}, bf16[16,2,32,128]{3,2,1,0:T(8,128)(2,1)}, u32[]{:S(2)}) copy-start(bf16[16,2,32,128]{3,2,1,0:T(8,128)(2,1)} %vol.1) | copy-start | bytes 786436
  2.2 22.5 %all-to-all-start = ((bf16[4,34,16,128]{3,2,1,0:T(8,128)(2,1)}), bf16[4,34,16,128]{3,2,1,0:T(8,128)(2,1)S(1)}, u32[]{:S(2)}, u32[]{:S(2)}) async-start(bf16[4,34,16,128]{3,2,1,0:T(8,128)(2,1)} %get-tuple-element.11), calls=%async_computation | async-start | bytes 1114112 | tf_op jit(solution)/shard_map/all_to_all | solution.py:234
  9.4 17.1 %copy-start.2 = (f32[16]{0:T(128)S(1)}, f32[16]{0:T(128)}, u32[]{:S(2)}) copy-start(f32[16]{0:T(128)} %param.5) | copy-start | bytes 196
  9.4 17.1 %collective-permute-start.2 = (bf16[32,128]{1,0:T(8,128)(2,1)S(1)}, bf16[32,128]{1,0:T(8,128)(2,1)S(1)}, u32[]{:S(2)}, u32[]{:S(2)}) collective-permute-start(bf16[32,128]{1,0:T(8,128)(2,1)S(1)} %get-tuple-element.12), channel_id=1, source_target_pairs={{0,64},{64,128},{128,192},{192,256},{256,320},{320,384},{384,448},... | collective-permute-start | bytes 24584 | tf_op jit(solution)/shard_map/ppermute | solution.py:211
  13.0 13.5 %collective-permute-start.3 = (bf16[32,128]{1,0:T(8,128)(2,1)S(1)}, bf16[32,128]{1,0:T(8,128)(2,1)S(1)}, u32[]{:S(2)}, u32[]{:S(2)}) collective-permute-start(bf16[32,128]{1,0:T(8,128)(2,1)S(1)} %get-tuple-element.13), channel_id=1, source_target_pairs={{64,0},{128,64},{192,128},{256,192},{320,256},{384,320},{448,384},... | collective-permute-start | bytes 24584 | tf_op jit(solution)/shard_map/ppermute | solution.py:211
  24.6 33.7 %collective-permute-start = (bf16[4,34,16,128]{3,2,1,0:T(8,128)(2,1)S(1)}, bf16[4,34,16,128]{3,2,1,0:T(8,128)(2,1)S(1)}, u32[]{:S(2)}, u32[]{:S(2)}) collective-permute-start(bf16[4,34,16,128]{3,2,1,0:T(8,128)(2,1)S(1)} %all-to-all-done.mine), channel_id=1, source_target_pairs={{0,1},{1,0},{2,3},{3,2},{4,5},{5,4},{6,7},{7,6},{8,9},{9,8},{10,11... | collective-permute-start | bytes 1671176 | tf_op jit(solution)/shard_map/ppermute | solution.py:215
  26.7 10.6 %collective-permute-start.5 = (bf16[40,128]{1,0:T(8,128)(2,1)S(1)}, bf16[40,128]{1,0:T(8,128)(2,1)S(1)}, u32[]{:S(2)}, u32[]{:S(2)}) collective-permute-start(bf16[40,128]{1,0:T(8,128)(2,1)S(1)} %shard_map.40), channel_id=1, source_target_pairs={{8,0},{16,8},{24,16},{32,24},{40,32},{48,40},{56,48},{9,1},{17,9},... | collective-permute-start | bytes 30728 | tf_op jit(solution)/shard_map/ppermute | solution.py:211
  35.3 10.4 %collective-permute-start.4 = (bf16[40,128]{1,0:T(8,128)(2,1)S(1)}, bf16[40,128]{1,0:T(8,128)(2,1)S(1)}, u32[]{:S(2)}, u32[]{:S(2)}) collective-permute-start(bf16[40,128]{1,0:T(8,128)(2,1)S(1)} %shard_map.40), channel_id=1, source_target_pairs={{0,8},{8,16},{16,24},{24,32},{32,40},{40,48},{48,56},{1,9},{9,17},... | collective-permute-start | bytes 30728 | tf_op jit(solution)/shard_map/ppermute | solution.py:211
  46.4 3.5 %copy-start.1 = (bf16[16,128,3,3,3]{1,0,4,3,2:T(8,128)(2,1)S(1)}, bf16[16,128,3,3,3]{1,0,4,3,2:T(8,128)(2,1)}, u32[]{:S(2)}) copy-start(bf16[16,128,3,3,3]{1,0,4,3,2:T(8,128)(2,1)} %param.4) | copy-start | bytes 331780
  46.4 12.9 %all-to-all-start.1 = ((bf16[8,56,128]{2,1,0:T(8,128)(2,1)}), bf16[8,56,128]{2,1,0:T(8,128)(2,1)S(1)}, u32[]{:S(2)}, u32[]{:S(2)}) async-start(bf16[8,56,128]{2,1,0:T(8,128)(2,1)} %shard_map.41), calls=%async_computation.1 | async-start | bytes 229376 | tf_op jit(solution)/shard_map/all_to_all | solution.py:245
  49.9 8.3 %collective-permute-start.1 = (bf16[448,128]{1,0:T(8,128)(2,1)S(1)}, bf16[448,128]{1,0:T(8,128)(2,1)S(1)}, u32[]{:S(2)}, u32[]{:S(2)}) collective-permute-start(bf16[448,128]{1,0:T(8,128)(2,1)S(1)} %fusion.1.own), channel_id=1, source_target_pairs={{0,2},{1,3},{2,0},{3,1},{4,6},{5,7},{6,4},{7,5},{8,10},{9,11},{10,... | collective-permute-start | bytes 344072 | tf_op jit(solution)/shard_map/ppermute | solution.py:215
  60.1 7.2 %collective-permute-start.6 = (bf16[32,16,128]{2,1,0:T(8,128)(2,1)S(1)}, bf16[32,16,128]{2,1,0:T(8,128)(2,1)S(1)}, u32[]{:S(2)}, u32[]{:S(2)}) collective-permute-start(bf16[32,16,128]{2,1,0:T(8,128)(2,1)S(1)} %get-tuple-element.16), channel_id=1, source_target_pairs={{0,2},{1,3},{2,0},{3,1},{4,6},{5,7},{6,4},{7,5},{8,10},{9,11},{10,... | collective-permute-start | bytes 393224 | tf_op jit(solution)/shard_map/ppermute | solution.py:215

commit v8 on v4

v8 whole, which is shorter than its diff:
```python
import jax
import jax.numpy as jnp
from jax import lax
from jax.experimental import pallas as pl
from jax.experimental.pallas import tpu as pltpu
from jax.sharding import PartitionSpec as P


BF = jnp.bfloat16
F32 = jnp.float32
CORES = [[0, 2, 4, 6], [1, 3, 5, 7]]
GRANT = 16 << 20


def call(kernel, out_shapes, scratch, *args, flops=0, moved=0, place=None, shared=None):
    vmem = pl.BlockSpec(memory_space=pltpu.VMEM)
    many = isinstance(out_shapes, (list, tuple))
    in_specs = [vmem] * len(args)
    for i in shared or {}:
        in_specs[i] = pl.BlockSpec(memory_space=pl.ANY)
    return pl.pallas_call(
        kernel,
        out_shape=out_shapes,
        in_specs=in_specs,
        out_specs=[vmem] * len(out_shapes) if many else place or vmem,
        scratch_shapes=scratch,
        input_output_aliases=shared or {},
        cost_estimate=pl.CostEstimate(flops=flops, bytes_accessed=moved, transcendentals=0),
        compiler_params=pltpu.CompilerParams(vmem_limit_bytes=GRANT),
    )(*args)


def shaped(*shape, dtype=BF):
    return jax.ShapeDtypeStruct(shape, dtype)


def lanes_of(shape):
    return lax.broadcasted_iota(jnp.int32, shape, len(shape) - 1)


def columns_kernel(vol, cols):
    lane = lanes_of((32, 128))
    both = jnp.zeros((32, 128), F32)
    for z in range(2):
        for c in range(16):
            tile = vol[c, z].astype(F32)
            j = z * 16 + c
            both = jnp.where(lane == j, pltpu.roll(tile, j, 1) if j else tile, both)
            both = jnp.where(lane == 32 + j, pltpu.roll(tile, 33 + j, 1), both)
    cols[...] = both.astype(BF)


def pack_kernel(vol, blocks, first, last, flat):
    flat[...] = vol[...].reshape(1024, 128).astype(F32)
    for z in range(2):
        for row in range(32):
            tile = flat[pl.ds(z * 32 + row, 16, stride=64), :].astype(BF)
            for chip in range(4):
                at = row - 15 * (chip % 2)
                if 0 <= at < 17:
                    blocks[chip, z * 17 + at] = tile
            if row == 0:
                first[pl.ds(z * 16, 16)] = tile
            if row == 31:
                last[pl.ds(z * 16, 16)] = tile


def beside_kernel(first, last, left, right, up, down, beside):
    lane = lanes_of((32, 128))
    both = jnp.where(
        lane < 32,
        pltpu.roll(left[...].astype(F32), 96, 1),
        jnp.where(lane < 64, pltpu.roll(right[...].astype(F32), 32, 1), 0.0),
    )
    beside[...] = both
    nothing = jnp.zeros((15, 128), F32)
    up[pl.ds(0, 32)] = last[...]
    up[pl.ds(32, 16)] = jnp.concatenate([both[31:32], nothing], axis=0).astype(BF)
    down[pl.ds(0, 32)] = first[...]
    down[pl.ds(32, 16)] = jnp.concatenate([both[0:1], nothing], axis=0).astype(BF)


def halo_kernel(above, below, beside, out, buf):
    buf[...] = jnp.zeros((40, 128), F32)
    buf[pl.ds(0, 1), :] = above[pl.ds(32, 16)].astype(F32)[0:1]
    buf[pl.ds(1, 32), :] = beside[...]
    buf[pl.ds(33, 1), :] = below[pl.ds(32, 16)].astype(F32)[0:1]
    for d in range(8):
        half = d // 2 % 2
        out[d, pl.ds(0, 32)] = below[pl.ds(0, 32)] if half else above[pl.ds(0, 32)]
        out[d, pl.ds(32, 24)] = buf[pl.ds(16 * half, 24), :].astype(BF)


def taps_kernel(own, other, taps, taps2):
    odd = lax.rem(lax.axis_index("ch"), 2) == 1
    even_block = lax.rem(lanes_of((16, 128)) // 16, 2) == 0
    for filters, to in ((own, taps), (other, taps2)):
        for a in range(3):
            for b in range(3):
                for e in range(3):
                    tile = filters[pl.ds((a * 9 + b * 3 + e) * 16, 16)].astype(F32)
                    swapped = jnp.where(even_block, pltpu.roll(tile, 112, 1), pltpu.roll(tile, 16, 1))
                    tile = jnp.where(odd, swapped, tile).astype(BF)
                    for zo in range(2):
                        zi = a - 1 + zo
                        if 0 <= zi < 2:
                            to[pl.ds(((b * 3 + e) * 2 + zo) * 16, 16), pl.ds(zi * 128, 128)] = tile


def half_of():
    return lax.rem(lax.axis_index("ch") // 2, 2)


def aligned(total, lane):
    before = jnp.where(lane == 0, 0.0, pltpu.roll(total[0:32], 1, 1))
    after = jnp.where(lane == 127, 0.0, pltpu.roll(total[64:96], 127, 1))
    return total[32:64] + (before + after)


def inner_kernel(mine, theirs, taps, taps2, pre, pre2, sums):
    half = half_of()
    lane = lanes_of((32, 128))

    def row_of(row):
        return jnp.concatenate(
            [held[chip, z * 17 + row + half] for z in range(2) for chip in range(4) for held in (mine, theirs)],
            axis=0,
        )

    for p in range(8):
        pair = jnp.concatenate([row_of(2 * p), row_of(2 * p + 1)], axis=1)
        for t, (weights, to) in enumerate(((taps, pre), (taps2, pre2))):
            got = jnp.dot(weights[...], pair, preferred_element_type=F32)
            for h in range(2):
                for b in range(3):
                    row = 2 * p + h + 1 - b
                    if not 0 <= row < 16:
                        continue
                    part = got[b * 96 : (b + 1) * 96, h * 128 : (h + 1) * 128]
                    if not (b == 0 or (b == 1 and row == 0)):
                        part = part + sums[t, row]
                    if b == 2 or (b == 1 and row == 15):
                        to[row] = aligned(part, lane)
                    else:
                        sums[t, row] = part


def outer_kernel(pre, taps, mine, theirs, halo, filters, out):
    me = lax.axis_index("ch")
    half, core = half_of(), lax.rem(me, 2)
    parts = filters[pl.ds(432, 16)].astype(F32)
    offset = (parts[:, 0:1] + parts[:, 1:2]) + parts[:, 2:3]
    offset = jnp.concatenate([offset, offset], axis=0)
    sources = [2 * chip + (core ^ t) for chip in range(4) for t in range(2)]
    lane24 = lanes_of((24, 128))
    total = [[jnp.zeros((24, 128), F32) for _ in range(2)] for _ in range(2)]
    for j, source in enumerate(sources):
        both = halo[source, pl.ds(32, 24)].astype(F32)
        for side in range(2):
            for z in range(2):
                shift = (j * 16 - side * 32 - z * 16) % 128
                piece = pltpu.roll(both, shift, 1) if shift else both
                total[side][z] = jnp.where(lane24 // 16 == j, piece, total[side][z])
    beside = jnp.concatenate(
        [jnp.concatenate(total[0], axis=1), jnp.concatenate(total[1], axis=1), jnp.zeros((80, 256), F32)], axis=0
    ).astype(BF)
    edge = lax.dot_general(taps[...], beside, (((1,), (1,)), ((), ())), preferred_element_type=F32)
    before, after = (
        edge[e * 32 : e * 32 + 32]
        + pltpu.roll(edge[96 + e * 32 : 128 + e * 32], 127, 1)
        + pltpu.roll(edge[192 + e * 32 : 224 + e * 32], 126, 1)
        for e in (0, 2)
    )
    lane = lanes_of((32, 128))
    far = jnp.concatenate(
        [halo[source, pl.ds(z * 16, 16)] for z in range(2) for source in sources], axis=0
    ).astype(F32)
    near = jnp.concatenate(
        [
            held[chip, z * 17 + 16 * (1 - half)]
            for z in range(2)
            for chip in range(4)
            for held in (mine, theirs)
        ],
        axis=0,
    ).astype(F32)
    first_half = half == 0
    above = jnp.where(first_half, far, near).astype(BF)
    below = jnp.where(first_half, near, far).astype(BF)
    above = aligned(jnp.dot(taps[pl.ds(0, 96)], above, preferred_element_type=F32), lane)
    below = aligned(jnp.dot(taps[pl.ds(192, 96)], below, preferred_element_type=F32), lane)
    for row in range(16):
        total = pre[row] + offset
        if row == 0:
            total = total + above
        if row == 15:
            total = total + below
        total = total + jnp.where(lane == 0, before[:, row : row + 1], 0.0)
        total = total + jnp.where(lane == 127, after[:, 24 + row : 25 + row], 0.0)
        done = jnp.where(total >= 0, total, 0.3 * total).astype(BF)
        for z in range(2):
            out[z * 16 + row] = done[z * 16 : z * 16 + 16]


def store(held, out, start, flat, ready, sem):
    for z in range(2):
        for row in range(16):
            flat[pl.ds(z * 16 + row, 16, stride=32), :] = held[z * 16 + row].astype(F32)
    ready[...] = flat[...].reshape(16, 2, 16, 128).astype(BF)
    copy = pltpu.make_async_copy(ready, out.at[:, :, pl.ds(pl.multiple_of(start, 16), 16)], sem)
    copy.start()
    copy.wait()


def keep_kernel(kept, out, flat, ready, sem):
    store(kept, out, 16 * half_of(), flat, ready, sem)


def unpack_kernel(got, held, out, flat, ready, sem):
    store(got, out, 16 * (1 - half_of()), flat, ready, sem)


def shifts(array, axis, up=True):
    size = lax.axis_size(axis)
    pairs = [(i, i + 1) for i in range(size - 1)]
    return lax.ppermute(array, axis, pairs if up else [(j, i) for i, j in pairs])


def swapped(array, t):
    return lax.ppermute(array, "ch", [(d, d ^ t) for d in range(8)])


def thirds(bias):
    high = bias.astype(BF)
    rest = bias - high.astype(F32)
    middle = rest.astype(BF)
    low = (rest - middle.astype(F32)).astype(BF)
    return jnp.pad(jnp.stack([high, middle, low], axis=1), ((0, 0), (0, 125)))


def stages(volume, weights, bias):
    cols = call(columns_kernel, shaped(32, 128), [], volume, moved=1 << 19)
    blocks, first, last = call(
        pack_kernel,
        [shaped(4, 34, 16, 128), shaped(32, 128), shaped(32, 128)],
        [pltpu.VMEM((1024, 128), F32)],
        volume,
        moved=1 << 20,
    )
    mine = lax.all_to_all(blocks, "ch", split_axis=0, concat_axis=0, tiled=True, axis_index_groups=CORES)
    left = shifts(cols, "sy", True)
    right = shifts(cols, "sy", False)
    own = jnp.concatenate([weights.transpose(2, 3, 4, 0, 1).reshape(432, 128), thirds(bias)], axis=0)
    other = swapped(own, 2)
    up, down, beside = call(
        beside_kernel,
        [shaped(48, 128), shaped(48, 128), shaped(32, 128, dtype=F32)],
        [],
        first,
        last,
        left,
        right,
        moved=1 << 16,
    )
    above = shifts(up, "sx", True)
    below = shifts(down, "sx", False)
    theirs = swapped(mine, 1)
    taps, taps2 = call(taps_kernel, [shaped(288, 256)] * 2, [], own, other, moved=1 << 19)
    halo = call(halo_kernel, shaped(8, 56, 128), [pltpu.VMEM((40, 128), F32)], above, below, beside, moved=1 << 17)
    halo = lax.all_to_all(halo, "ch", split_axis=0, concat_axis=0, tiled=True)
    pre, pre2 = call(
        inner_kernel,
        [shaped(16, 32, 128, dtype=F32)] * 2,
        [pltpu.VMEM((2, 16, 96, 128), F32)],
        mine,
        theirs,
        taps,
        taps2,
        flops=2 * 576 * 256 * 2048,
        moved=3 << 20,
    )
    cost = dict(flops=2 * 288 * 256 * 256, moved=1 << 20)
    sent = call(outer_kernel, shaped(32, 16, 128), [], pre2, taps2, mine, theirs, halo, other, **cost)
    got = swapped(sent, 2)
    kept = call(outer_kernel, shaped(32, 16, 128), [], pre, taps, mine, theirs, halo, own, **cost)
    scratch = [pltpu.VMEM((512, 128), F32), pltpu.VMEM((16, 2, 16, 128), BF), pltpu.SemaphoreType.DMA]
    space = pl.BlockSpec(memory_space=pl.ANY)
    result = call(keep_kernel, shaped(16, 2, 32, 128), scratch, kept, moved=1 << 18, place=space)
    return call(unpack_kernel, shaped(16, 2, 32, 128), scratch, got, result, moved=1 << 18, place=space, shared={1: 0})


def solution(mesh):
    in_specs = (P("ch", None, "sx", "sy"), P("ch", None, None, None, None), P("ch"))
    out_specs = P("ch", None, "sx", "sy")
    return jax.shard_map(stages, mesh=mesh, in_specs=in_specs, out_specs=out_specs, check_vma=False)
```

time: 65.1 us -> 64.8 us (level)
  waiting for transfers between devices: 20.4 us -> 18.8 us
  Pallas kernels: 5.06 us -> 6.24 us
    ppermute x3, waiting for transfers between devices: 9.05 us -> 7.48 us  [swapped(): return lax.ppermute(array, 'ch', [(d, d ^ t) for d in range(8)])]
    pallas_call x7 -> x10, Pallas kernels: 5.06 us -> 6.24 us  [call(): pl.pallas_call(kernel, out_shape=out_shapes, in_specs=in_specs, out_specs...]
  transfers between devices with their start and end apart: 9 -> 9, of which waited for: 5 -> 5; matrix products, arithmetic and copies ran while one was open for 0% -> 0% of each run, Pallas kernels for 3% -> 6%
where the time goes in v8:
time: 64.8 us; the launch traced here: 64.3 us
  starting transfers between devices  38 us (59%)
  waiting for transfers between devices  18.8 us (29%)
  Pallas kernels  6.24 us (10%)
  local copies, waits for them, and re-layouts  1.06 us (2%)
    ppermute x4, starting transfers between devices, shifts(): lax.ppermute(array, axis, pairs if up else [(j, i) for i, j in pairs])  17 us
    ppermute x3, starting transfers between devices, swapped(): return lax.ppermute(array, 'ch', [(d, d ^ t) for d in range(8)])  8.47 us
    ppermute x3, waiting for transfers between devices, swapped(): return lax.ppermute(array, 'ch', [(d, d ^ t) for d in range(8)])  7.48 us
    all_to_all x1, starting transfers between devices, stages(): lax.all_to_all(blocks, 'ch', split_axis=0, concat_axis=0, tiled=True, axi...  7.39 us
    ppermute x4, waiting for transfers between devices, shifts(): lax.ppermute(array, axis, pairs if up else [(j, i) for i, j in pairs])  6.34 us
    pallas_call x10, Pallas kernels, call(): pl.pallas_call(kernel, out_shape=out_shapes, in_specs=in_specs, out_specs...  6.24 us
    all_to_all x1, starting transfers between devices, stages(): halo = lax.all_to_all(halo, 'ch', split_axis=0, concat_axis=0, tiled=True)  5.13 us
    all_to_all x1, waiting for transfers between devices, stages(): lax.all_to_all(blocks, 'ch', split_axis=0, concat_axis=0, tiled=True, axi...  5 us
  transfers between devices with their start and end apart: 9, of which 5 were waited for; matrix products, arithmetic and copies ran while one was open for 0% of the time, Pallas kernels for 6%

profile of v8, /device:TPU:30, one launch (start us, length us, event | category | flops | bytes accessed | tf_op | source)
XLA Modules:
  0.0 64.3 jit_solution(5205365214059019249)
XLA Ops:
  0.0 0.0 copy-start
  0.0 0.9 %copy-done = bf16[16,2,32,128]{3,2,1,0:T(8,128)(2,1)S(1)} copy-done((bf16[16,2,32,128]{3,2,1,0:T(8,128)(2,1)S(1)}, bf16[16,2,32,128]{3,2,1,0:T(8,128)(2,1)}, u32[]{:S(2)}) %copy-start) | copy-done | bytes 262168
  1.0 1.1 %shard_map.37 = (bf16[4,34,16,128]{3,2,1,0:T(8,128)(2,1)}, bf16[32,128]{1,0:T(8,128)(2,1)S(1)}, bf16[32,128]{1,0:T(8,128)(2,1)S(1)}) custom-call(bf16[16,2,32,128]{3,2,1,0:T(8,128)(2,1)S(1)} %copy-done), custom_call_target="tpu_custom_call" | custom-call | bytes 1048576 | tf_op jit(solution)/shard_map/pallas_call | solution.py:21
  2.1 0.0 copy-start.1
  2.1 7.4 %all-to-all-start = ((bf16[4,34,16,128]{3,2,1,0:T(8,128)(2,1)}), bf16[4,34,16,128]{3,2,1,0:T(8,128)(2,1)S(1)}, u32[]{:S(2)}, u32[]{:S(2)}) async-start(bf16[4,34,16,128]{3,2,1,0:T(8,128)(2,1)} %get-tuple-element.15), calls=%async_computation | async-start | bytes 1114112 | tf_op jit(solution)/shard_map/all_to_all | solution.py:250
  9.5 0.0 copy-done.1
  9.5 0.0 copy-start.3
  9.5 0.2 shard_map.40
  9.7 8.5 %collective-permute-start.3 = (bf16[32,128]{1,0:T(8,128)(2,1)S(1)}, bf16[32,128]{1,0:T(8,128)(2,1)S(1)}, u32[]{:S(2)}, u32[]{:S(2)}) collective-permute-start(bf16[32,128]{1,0:T(8,128)(2,1)S(1)} %shard_map.40), channel_id=1, source_target_pairs={{8,0},{16,8},{24,16},{32,24},{40,32},{48,40},{56,48},{9,1},{17,9},... | collective-permute-start | bytes 24584 | tf_op jit(solution)/shard_map/ppermute | solution.py:226
  18.2 1.9 %collective-permute-start.2 = (bf16[32,128]{1,0:T(8,128)(2,1)S(1)}, bf16[32,128]{1,0:T(8,128)(2,1)S(1)}, u32[]{:S(2)}, u32[]{:S(2)}) collective-permute-start(bf16[32,128]{1,0:T(8,128)(2,1)S(1)} %shard_map.40), channel_id=1, source_target_pairs={{0,8},{8,16},{16,24},{24,32},{32,40},{40,48},{48,56},{1,9},{9,17},... | collective-permute-start | bytes 24584 | tf_op jit(solution)/shard_map/ppermute | solution.py:226
  20.1 5.0 %all-to-all-done.mine = bf16[4,34,16,128]{3,2,1,0:T(8,128)(2,1)S(1)} async-done(((bf16[4,34,16,128]{3,2,1,0:T(8,128)(2,1)}), bf16[4,34,16,128]{3,2,1,0:T(8,128)(2,1)S(1)}, u32[]{:S(2)}, u32[]{:S(2)}) %all-to-all-start) | async-done | bytes 557088 | tf_op jit(solution)/shard_map/all_to_all | solution.py:250
  25.1 1.9 %collective-permute-start = (bf16[4,34,16,128]{3,2,1,0:T(8,128)(2,1)S(1)}, bf16[4,34,16,128]{3,2,1,0:T(8,128)(2,1)S(1)}, u32[]{:S(2)}, u32[]{:S(2)}) collective-permute-start(bf16[4,34,16,128]{3,2,1,0:T(8,128)(2,1)S(1)} %all-to-all-done.mine), channel_id=1, source_target_pairs={{0,1},{1,0},{2,3},{3,2},{4,5},{5,4},{6,7},{7,6},{8,9},{9,8},{10,11... | collective-permute-start | bytes 1671176 | tf_op jit(solution)/shard_map/ppermute | solution.py:230
  27.0 0.0 copy-done.3
  27.1 0.0 collective-permute-done.3.right
  27.1 1.6 %collective-permute-done.2.left = bf16[32,128]{1,0:T(8,128)(2,1)S(1)} collective-permute-done((bf16[32,128]{1,0:T(8,128)(2,1)S(1)}, bf16[32,128]{1,0:T(8,128)(2,1)S(1)}, u32[]{:S(2)}, u32[]{:S(2)}) %collective-permute-start.2) | collective-permute-done | bytes 8224 | tf_op jit(solution)/shard_map/ppermute | solution.py:226
  28.6 0.1 shard_map.41
  28.7 4.7 %collective-permute-start.4 = (bf16[48,128]{1,0:T(8,128)(2,1)S(1)}, bf16[48,128]{1,0:T(8,128)(2,1)S(1)}, u32[]{:S(2)}, u32[]{:S(2)}) collective-permute-start(bf16[48,128]{1,0:T(8,128)(2,1)S(1)} %get-tuple-element.21), channel_id=1, source_target_pairs={{0,64},{64,128},{128,192},{192,256},{256,320},{320,384},{384,448},... | collective-permute-start | bytes 36872 | tf_op jit(solution)/shard_map/ppermute | solution.py:226
  33.4 1.9 %collective-permute-start.5 = (bf16[48,128]{1,0:T(8,128)(2,1)S(1)}, bf16[48,128]{1,0:T(8,128)(2,1)S(1)}, u32[]{:S(2)}, u32[]{:S(2)}) collective-permute-start(bf16[48,128]{1,0:T(8,128)(2,1)S(1)} %get-tuple-element.22), channel_id=1, source_target_pairs={{64,0},{128,64},{192,128},{256,192},{320,256},{384,320},{448,384},... | collective-permute-start | bytes 36872 | tf_op jit(solution)/shard_map/ppermute | solution.py:226
  35.4 0.1 copy.8
  35.5 0.0 collective-permute-done.4.above
  35.5 4.8 %collective-permute-done.5.below = bf16[48,128]{1,0:T(8,128)(2,1)S(1)} collective-permute-done((bf16[48,128]{1,0:T(8,128)(2,1)S(1)}, bf16[48,128]{1,0:T(8,128)(2,1)S(1)}, u32[]{:S(2)}, u32[]{:S(2)}) %collective-permute-start.5) | collective-permute-done | bytes 12320 | tf_op jit(solution)/shard_map/ppermute | solution.py:226
  40.2 0.7 %shard_map.42 = bf16[8,56,128]{2,1,0:T(8,128)(2,1)} custom-call(bf16[48,128]{1,0:T(8,128)(2,1)S(1)} %collective-permute-done.4.above, bf16[48,128]{1,0:T(8,128)(2,1)S(1)} %collective-permute-done.5.below, f32[32,128]{1,0:T(8,128)S(1)} %get-tuple-element.23.beside), custom_call_target="tpu_custom_call" | custom-call | bytes 131072 | tf_op jit(solution)/shard_map/pallas_call | solution.py:21
  40.9 0.0 copy-start.2
  40.9 5.1 %all-to-all-start.1 = ((bf16[8,56,128]{2,1,0:T(8,128)(2,1)}), bf16[8,56,128]{2,1,0:T(8,128)(2,1)S(1)}, u32[]{:S(2)}, u32[]{:S(2)}) async-start(bf16[8,56,128]{2,1,0:T(8,128)(2,1)} %shard_map.42), calls=%async_computation.1 | async-start | bytes 229376 | tf_op jit(solution)/shard_map/all_to_all | solution.py:270
  46.0 0.0 copy-done.2
  46.0 3.9 %collective-permute-start.1 = (bf16[448,128]{1,0:T(8,128)(2,1)S(1)}, bf16[448,128]{1,0:T(8,128)(2,1)S(1)}, u32[]{:S(2)}, u32[]{:S(2)}) collective-permute-start(bf16[448,128]{1,0:T(8,128)(2,1)S(1)} %fusion.1.own.filters), channel_id=1, source_target_pairs={{0,2},{1,3},{2,0},{3,1},{4,6},{5,7},{6,4},{7,5},{8,10},{9,11},{10,... | collective-permute-start | bytes 344072 | tf_op jit(solution)/shard_map/ppermute | solution.py:230
  50.0 4.4 %collective-permute-done.1.other.filters = bf16[448,128]{1,0:T(8,128)(2,1)S(1)} collective-permute-done((bf16[448,128]{1,0:T(8,128)(2,1)S(1)}, bf16[448,128]{1,0:T(8,128)(2,1)S(1)}, u32[]{:S(2)}, u32[]{:S(2)}) %collective-permute-start.1) | collective-permute-done | bytes 114720 | tf_op jit(solution)/shard_map/ppermute | solution.py:230
  54.4 0.2 shard_map.38
  54.6 0.0 collective-permute-done.theirs
  54.6 0.9 %shard_map.39 = (f32[16,32,128]{2,1,0:T(8,128)S(1)}, f32[16,32,128]{2,1,0:T(8,128)S(1)}) custom-call(bf16[4,34,16,128]{3,2,1,0:T(8,128)(2,1)S(1)} %all-to-all-done.mine, bf16[4,34,16,128]{3,2,1,0:T(8,128)(2,1)S(1)} %collective-permute-done.theirs, bf16[288,256]{1,0:T(8,128)(2,1)S(1)} %get-tuple-element.16.taps, bf16[288,256]{1,0:T(8,128)(2,1)S(1)} %get-tuple-element.17.taps2.taps), custom_call_target="tpu_custom_call" | custom-call | flops 603979776 | bytes 3145728 | tf_op jit(solution)/shard_map/pallas_call | solution.py:21
  55.5 0.0 all-to-all-done.1.halo
  55.5 0.7 %shard_map.43 = bf16[32,16,128]{2,1,0:T(8,128)(2,1)S(1)} custom-call(f32[16,32,128]{2,1,0:T(8,128)S(1)} %get-tuple-element.18.pre, bf16[288,256]{1,0:T(8,128)(2,1)S(1)} %get-tuple-element.17.taps2.taps, bf16[4,34,16,128]{3,2,1,0:T(8,128)(2,1)S(1)} %all-to-all-done.mine, bf16[4,34,16,128]{3,2,1,0:T(8,128)(2,1)S(1)} %collective-permute-done.theirs, ...), custom_call_target="tpu_custom_call" | custom-call | flops 37748736 | bytes 1048576 | tf_op jit(solution)/shard_map/pallas_call | solution.py:21
  56.2 2.6 %collective-permute-start.6 = (bf16[32,16,128]{2,1,0:T(8,128)(2,1)S(1)}, bf16[32,16,128]{2,1,0:T(8,128)(2,1)S(1)}, u32[]{:S(2)}, u32[]{:S(2)}) collective-permute-start(bf16[32,16,128]{2,1,0:T(8,128)(2,1)S(1)} %shard_map.43), channel_id=1, source_target_pairs={{0,2},{1,3},{2,0},{3,1},{4,6},{5,7},{6,4},{7,5},{8,10},{9,11},{10,... | collective-permute-start | bytes 393224 | tf_op jit(solution)/shard_map/ppermute | solution.py:230
  58.8 0.7 %shard_map.44.kept = bf16[32,16,128]{2,1,0:T(8,128)(2,1)S(1)} custom-call(f32[16,32,128]{2,1,0:T(8,128)S(1)} %get-tuple-element.24.pre, bf16[288,256]{1,0:T(8,128)(2,1)S(1)} %get-tuple-element.16.taps, bf16[4,34,16,128]{3,2,1,0:T(8,128)(2,1)S(1)} %all-to-all-done.mine, bf16[4,34,16,128]{3,2,1,0:T(8,128)(2,1)S(1)} %collective-permute-done.theirs, ...), custom_call_target="tpu_custom_call" | custom-call | flops 37748736 | bytes 1048576 | tf_op jit(solution)/shard_map/pallas_call | solution.py:21
  59.5 0.9 %shard_map.45.held = bf16[16,2,32,128]{3,2,1,0:T(8,128)(2,1)} custom-call(bf16[32,16,128]{2,1,0:T(8,128)(2,1)S(1)} %shard_map.44.kept), custom_call_target="tpu_custom_call" | custom-call | bytes 262144 | tf_op jit(solution)/shard_map/pallas_call | solution.py:21
  60.4 3.0 %collective-permute-done.6.got = bf16[32,16,128]{2,1,0:T(8,128)(2,1)S(1)} collective-permute-done((bf16[32,16,128]{2,1,0:T(8,128)(2,1)S(1)}, bf16[32,16,128]{2,1,0:T(8,128)(2,1)S(1)}, u32[]{:S(2)}, u32[]{:S(2)}) %collective-permute-start.6) | collective-permute-done | bytes 131104 | tf_op jit(solution)/shard_map/ppermute | solution.py:230
  63.4 0.9 %shard_map.46 = bf16[16,2,32,128]{3,2,1,0:T(8,128)(2,1)} custom-call(bf16[32,16,128]{2,1,0:T(8,128)(2,1)S(1)} %collective-permute-done.6.got, bf16[16,2,32,128]{3,2,1,0:T(8,128)(2,1)} %shard_map.45.held), custom_call_target="tpu_custom_call", output_to_operand_aliasing={{}: (1, {})} | custom-call | bytes 262144 | tf_op jit(solution)/shard_map/pallas_call | solution.py:21
  (3 shorter events, 0.0 us)
Async XLA Ops:
  0.0 0.9 %copy-start = (bf16[16,2,32,128]{3,2,1,0:T(8,128)(2,1)S(1)}, bf16[16,2,32,128]{3,2,1,0:T(8,128)(2,1)}, u32[]{:S(2)}) copy-start(bf16[16,2,32,128]{3,2,1,0:T(8,128)(2,1)} %vol.3) | copy-start | bytes 786436
  2.1 7.4 %copy-start.1 = (bf16[16,2,32,128]{3,2,1,0:T(8,128)(2,1)S(1)}, bf16[16,2,32,128]{3,2,1,0:T(8,128)(2,1)}, u32[]{:S(2)}) copy-start(bf16[16,2,32,128]{3,2,1,0:T(8,128)(2,1)} %vol.3) | copy-start | bytes 786436
  2.1 23.0 %all-to-all-start = ((bf16[4,34,16,128]{3,2,1,0:T(8,128)(2,1)}), bf16[4,34,16,128]{3,2,1,0:T(8,128)(2,1)S(1)}, u32[]{:S(2)}, u32[]{:S(2)}) async-start(bf16[4,34,16,128]{3,2,1,0:T(8,128)(2,1)} %get-tuple-element.15), calls=%async_computation | async-start | bytes 1114112 | tf_op jit(solution)/shard_map/all_to_all | solution.py:250
  9.5 17.5 %copy-start.3 = (f32[16]{0:T(128)S(1)}, f32[16]{0:T(128)}, u32[]{:S(2)}) copy-start(f32[16]{0:T(128)} %param.5) | copy-start | bytes 196
  9.7 17.4 %collective-permute-start.3 = (bf16[32,128]{1,0:T(8,128)(2,1)S(1)}, bf16[32,128]{1,0:T(8,128)(2,1)S(1)}, u32[]{:S(2)}, u32[]{:S(2)}) collective-permute-start(bf16[32,128]{1,0:T(8,128)(2,1)S(1)} %shard_map.40), channel_id=1, source_target_pairs={{8,0},{16,8},{24,16},{32,24},{40,32},{48,40},{56,48},{9,1},{17,9},... | collective-permute-start | bytes 24584 | tf_op jit(solution)/shard_map/ppermute | solution.py:226
  18.2 10.5 %collective-permute-start.2 = (bf16[32,128]{1,0:T(8,128)(2,1)S(1)}, bf16[32,128]{1,0:T(8,128)(2,1)S(1)}, u32[]{:S(2)}, u32[]{:S(2)}) collective-permute-start(bf16[32,128]{1,0:T(8,128)(2,1)S(1)} %shard_map.40), channel_id=1, source_target_pairs={{0,8},{8,16},{16,24},{24,32},{32,40},{40,48},{48,56},{1,9},{9,17},... | collective-permute-start | bytes 24584 | tf_op jit(solution)/shard_map/ppermute | solution.py:226
  25.1 29.5 %collective-permute-start = (bf16[4,34,16,128]{3,2,1,0:T(8,128)(2,1)S(1)}, bf16[4,34,16,128]{3,2,1,0:T(8,128)(2,1)S(1)}, u32[]{:S(2)}, u32[]{:S(2)}) collective-permute-start(bf16[4,34,16,128]{3,2,1,0:T(8,128)(2,1)S(1)} %all-to-all-done.mine), channel_id=1, source_target_pairs={{0,1},{1,0},{2,3},{3,2},{4,5},{5,4},{6,7},{7,6},{8,9},{9,8},{10,11... | collective-permute-start | bytes 1671176 | tf_op jit(solution)/shard_map/ppermute | solution.py:230
  28.7 6.7 %collective-permute-start.4 = (bf16[48,128]{1,0:T(8,128)(2,1)S(1)}, bf16[48,128]{1,0:T(8,128)(2,1)S(1)}, u32[]{:S(2)}, u32[]{:S(2)}) collective-permute-start(bf16[48,128]{1,0:T(8,128)(2,1)S(1)} %get-tuple-element.21), channel_id=1, source_target_pairs={{0,64},{64,128},{128,192},{192,256},{256,320},{320,384},{384,448},... | collective-permute-start | bytes 36872 | tf_op jit(solution)/shard_map/ppermute | solution.py:226
  33.4 6.8 %collective-permute-start.5 = (bf16[48,128]{1,0:T(8,128)(2,1)S(1)}, bf16[48,128]{1,0:T(8,128)(2,1)S(1)}, u32[]{:S(2)}, u32[]{:S(2)}) collective-permute-start(bf16[48,128]{1,0:T(8,128)(2,1)S(1)} %get-tuple-element.22), channel_id=1, source_target_pairs={{64,0},{128,64},{192,128},{256,192},{320,256},{384,320},{448,384},... | collective-permute-start | bytes 36872 | tf_op jit(solution)/shard_map/ppermute | solution.py:226
  40.9 5.1 %copy-start.2 = (bf16[16,128,3,3,3]{1,0,4,3,2:T(8,128)(2,1)S(1)}, bf16[16,128,3,3,3]{1,0,4,3,2:T(8,128)(2,1)}, u32[]{:S(2)}) copy-start(bf16[16,128,3,3,3]{1,0,4,3,2:T(8,128)(2,1)} %param.4) | copy-start | bytes 331780
  40.9 14.6 %all-to-all-start.1 = ((bf16[8,56,128]{2,1,0:T(8,128)(2,1)}), bf16[8,56,128]{2,1,0:T(8,128)(2,1)S(1)}, u32[]{:S(2)}, u32[]{:S(2)}) async-start(bf16[8,56,128]{2,1,0:T(8,128)(2,1)} %shard_map.42), calls=%async_computation.1 | async-start | bytes 229376 | tf_op jit(solution)/shard_map/all_to_all | solution.py:270
  46.0 8.4 %collective-permute-start.1 = (bf16[448,128]{1,0:T(8,128)(2,1)S(1)}, bf16[448,128]{1,0:T(8,128)(2,1)S(1)}, u32[]{:S(2)}, u32[]{:S(2)}) collective-permute-start(bf16[448,128]{1,0:T(8,128)(2,1)S(1)} %fusion.1.own.filters), channel_id=1, source_target_pairs={{0,2},{1,3},{2,0},{3,1},{4,6},{5,7},{6,4},{7,5},{8,10},{9,11},{10,... | collective-permute-start | bytes 344072 | tf_op jit(solution)/shard_map/ppermute | solution.py:230
  56.2 7.3 %collective-permute-start.6 = (bf16[32,16,128]{2,1,0:T(8,128)(2,1)S(1)}, bf16[32,16,128]{2,1,0:T(8,128)(2,1)S(1)}, u32[]{:S(2)}, u32[]{:S(2)}) collective-permute-start(bf16[32,16,128]{2,1,0:T(8,128)(2,1)S(1)} %shard_map.43), channel_id=1, source_target_pairs={{0,2},{1,3},{2,0},{3,1},{4,6},{5,7},{6,4},{7,5},{8,10},{9,11},{10,... | collective-permute-start | bytes 393224 | tf_op jit(solution)/shard_map/ppermute | solution.py:230

commit v9 on v8

--- a/solution.py
+++ b/solution.py
@@ -85,10 +85,17 @@
     buf[pl.ds(0, 1), :] = above[pl.ds(32, 16)].astype(F32)[0:1]
     buf[pl.ds(1, 32), :] = beside[...]
     buf[pl.ds(33, 1), :] = below[pl.ds(32, 16)].astype(F32)[0:1]
+    lane = lanes_of((16, 128))
+    sides = [
+        jnp.where(
+            lane < 64, buf[pl.ds(16 * half, 16), :], pltpu.roll(buf[pl.ds(16 * half + 8, 16), :], 64, 1)
+        ).astype(BF)
+        for half in range(2)
+    ]
     for d in range(8):
         half = d // 2 % 2
         out[d, pl.ds(0, 32)] = below[pl.ds(0, 32)] if half else above[pl.ds(0, 32)]
-        out[d, pl.ds(32, 24)] = buf[pl.ds(16 * half, 24), :].astype(BF)
+        out[d, pl.ds(32, 16)] = sides[half]
 
 
 def taps_kernel(own, other, taps, taps2):
@@ -145,7 +152,7 @@
                         sums[t, row] = part
 
 
-def outer_kernel(pre, taps, mine, theirs, halo, filters, out):
+def outer_kernel(pre, taps, mine, theirs, halo, filters, out, flat):
     me = lax.axis_index("ch")
     half, core = half_of(), lax.rem(me, 2)
     parts = filters[pl.ds(432, 16)].astype(F32)
@@ -155,7 +162,8 @@
     lane24 = lanes_of((24, 128))
     total = [[jnp.zeros((24, 128), F32) for _ in range(2)] for _ in range(2)]
     for j, source in enumerate(sources):
-        both = halo[source, pl.ds(32, 24)].astype(F32)
+        both = halo[source, pl.ds(32, 16)].astype(F32)
+        both = jnp.concatenate([both, pltpu.roll(both[8:16], 64, 1)], axis=0)
         for side in range(2):
             for z in range(2):
                 shift = (j * 16 - side * 32 - z * 16) % 128
@@ -197,27 +205,25 @@
             total = total + below
         total = total + jnp.where(lane == 0, before[:, row : row + 1], 0.0)
         total = total + jnp.where(lane == 127, after[:, 24 + row : 25 + row], 0.0)
-        done = jnp.where(total >= 0, total, 0.3 * total).astype(BF)
+        total = jnp.where(total >= 0, total, 0.3 * total)
         for z in range(2):
-            out[z * 16 + row] = done[z * 16 : z * 16 + 16]
-
-
-def store(held, out, start, flat, ready, sem):
-    for z in range(2):
-        for row in range(16):
-            flat[pl.ds(z * 16 + row, 16, stride=32), :] = held[z * 16 + row].astype(F32)
-    ready[...] = flat[...].reshape(16, 2, 16, 128).astype(BF)
+            flat[pl.ds(z * 16 + row, 16, stride=32), :] = total[z * 16 : z * 16 + 16]
+    out[...] = flat[...].reshape(16, 2, 16, 128).astype(BF)
+
+
+def place(ready, out, start, sem):
     copy = pltpu.make_async_copy(ready, out.at[:, :, pl.ds(pl.multiple_of(start, 16), 16)], sem)
     copy.start()
     copy.wait()
 
 
-def keep_kernel(kept, out, flat, ready, sem):
-    store(kept, out, 16 * half_of(), flat, ready, sem)
-
-
-def unpack_kernel(got, held, out, flat, ready, sem):
-    store(got, out, 16 * (1 - half_of()), flat, ready, sem)
+def kept_kernel(pre, taps, mine, theirs, halo, filters, out, flat, ready, sem):
+    outer_kernel(pre, taps, mine, theirs, halo, filters, ready, flat)
+    place(ready, out, 16 * half_of(), sem)
+
+
+def unpack_kernel(got, held, out, sem):
+    place(got, out, 16 * (1 - half_of()), sem)
 
 
 def shifts(array, axis, up=True):
@@ -266,7 +272,7 @@
     below = shifts(down, "sx", False)
     theirs = swapped(mine, 1)
     taps, taps2 = call(taps_kernel, [shaped(288, 256)] * 2, [], own, other, moved=1 << 19)
-    halo = call(halo_kernel, shaped(8, 56, 128), [pltpu.VMEM((40, 128), F32)], above, below, beside, moved=1 << 17)
+    halo = call(halo_kernel, shaped(8, 48, 128), [pltpu.VMEM((40, 128), F32)], above, below, beside, moved=1 << 17)
     halo = lax.all_to_all(halo, "ch", split_axis=0, concat_axis=0, tiled=True)
     pre, pre2 = call(
         inner_kernel,
@@ -280,13 +286,25 @@
         moved=3 << 20,
     )
     cost = dict(flops=2 * 288 * 256 * 256, moved=1 << 20)
-    sent = call(outer_kernel, shaped(32, 16, 128), [], pre2, taps2, mine, theirs, halo, other, **cost)
+    flat = pltpu.VMEM((512, 128), F32)
+    ready, sem = pltpu.VMEM((16, 2, 16, 128), BF), pltpu.SemaphoreType.DMA
+    space = pl.BlockSpec(memory_space=pl.ANY)
+    sent = call(outer_kernel, shaped(16, 2, 16, 128), [flat], pre2, taps2, mine, theirs, halo, other, **cost)
     got = swapped(sent, 2)
-    kept = call(outer_kernel, shaped(32, 16, 128), [], pre, taps, mine, theirs, halo, own, **cost)
-    scratch = [pltpu.VMEM((512, 128), F32), pltpu.VMEM((16, 2, 16, 128), BF), pltpu.SemaphoreType.DMA]
-    space = pl.BlockSpec(memory_space=pl.ANY)
-    result = call(keep_kernel, shaped(16, 2, 32, 128), scratch, kept, moved=1 << 18, place=space)
-    return call(unpack_kernel, shaped(16, 2, 32, 128), scratch, got, result, moved=1 << 18, place=space, shared={1: 0})
+    result = call(
+        kept_kernel,
+        shaped(16, 2, 32, 128),
+        [flat, ready, sem],
+        pre,
+        taps,
+        mine,
+        theirs,
+        halo,
+        own,
+        place=space,
+        **cost,
+    )
+    return call(unpack_kernel, shaped(16, 2, 32, 128), [sem], got, result, moved=1 << 18, place=space, shared={1: 0})
 
 
 def solution(mesh):

time: 64.8 us -> 64.6 us (level)
    pallas_call x10 -> x9, Pallas kernels: 6.24 us -> 6.19 us  [call(): pl.pallas_call(kernel, out_shape=out_shapes, in_specs=in_specs, out_specs...]
where the time goes in v9:
time: 64.6 us; the launch traced here: 64.1 us
  starting transfers between devices  38.2 us (59%)
  waiting for transfers between devices  18.5 us (29%)
  Pallas kernels  6.19 us (10%)
  local copies, waits for them, and re-layouts  1.06 us (2%)
    ppermute x4, starting transfers between devices, shifts(): lax.ppermute(array, axis, pairs if up else [(j, i) for i, j in pairs])  17 us
    ppermute x3, starting transfers between devices, swapped(): return lax.ppermute(array, 'ch', [(d, d ^ t) for d in range(8)])  8.67 us
    all_to_all x1, starting transfers between devices, stages(): lax.all_to_all(blocks, 'ch', split_axis=0, concat_axis=0, tiled=True, axi...  7.39 us
    ppermute x3, waiting for transfers between devices, swapped(): return lax.ppermute(array, 'ch', [(d, d ^ t) for d in range(8)])  7.15 us
    ppermute x4, waiting for transfers between devices, shifts(): lax.ppermute(array, axis, pairs if up else [(j, i) for i, j in pairs])  6.34 us
    pallas_call x9, Pallas kernels, call(): pl.pallas_call(kernel, out_shape=out_shapes, in_specs=in_specs, out_specs...  6.19 us
    all_to_all x1, starting transfers between devices, stages(): halo = lax.all_to_all(halo, 'ch', split_axis=0, concat_axis=0, tiled=True)  5.13 us
    all_to_all x1, waiting for transfers between devices, stages(): lax.all_to_all(blocks, 'ch', split_axis=0, concat_axis=0, tiled=True, axi...  5 us
  transfers between devices with their start and end apart: 9, of which 5 were waited for; matrix products, arithmetic and copies ran while one was open for 0% of the time, Pallas kernels for 6%

profile of v9, /device:TPU:30, one launch (start us, length us, event | category | flops | bytes accessed | tf_op | source)
XLA Modules:
  0.0 64.1 jit_solution(7597812687595303624)
XLA Ops:
  0.0 0.0 copy-start
  0.0 0.9 %copy-done = bf16[16,2,32,128]{3,2,1,0:T(8,128)(2,1)S(1)} copy-done((bf16[16,2,32,128]{3,2,1,0:T(8,128)(2,1)S(1)}, bf16[16,2,32,128]{3,2,1,0:T(8,128)(2,1)}, u32[]{:S(2)}) %copy-start) | copy-done | bytes 262168
  1.0 1.1 %shard_map.37 = (bf16[4,34,16,128]{3,2,1,0:T(8,128)(2,1)}, bf16[32,128]{1,0:T(8,128)(2,1)S(1)}, bf16[32,128]{1,0:T(8,128)(2,1)S(1)}) custom-call(bf16[16,2,32,128]{3,2,1,0:T(8,128)(2,1)S(1)} %copy-done), custom_call_target="tpu_custom_call" | custom-call | bytes 1048576 | tf_op jit(solution)/shard_map/pallas_call | solution.py:21
  2.1 0.0 copy-start.1
  2.1 7.4 %all-to-all-start = ((bf16[4,34,16,128]{3,2,1,0:T(8,128)(2,1)}), bf16[4,34,16,128]{3,2,1,0:T(8,128)(2,1)S(1)}, u32[]{:S(2)}, u32[]{:S(2)}) async-start(bf16[4,34,16,128]{3,2,1,0:T(8,128)(2,1)} %get-tuple-element.15), calls=%async_computation | async-start | bytes 1114112 | tf_op jit(solution)/shard_map/all_to_all | solution.py:256
  9.5 0.0 copy-done.1
  9.5 0.0 copy-start.3
  9.5 0.2 shard_map.40
  9.7 8.5 %collective-permute-start.3 = (bf16[32,128]{1,0:T(8,128)(2,1)S(1)}, bf16[32,128]{1,0:T(8,128)(2,1)S(1)}, u32[]{:S(2)}, u32[]{:S(2)}) collective-permute-start(bf16[32,128]{1,0:T(8,128)(2,1)S(1)} %shard_map.40), channel_id=1, source_target_pairs={{8,0},{16,8},{24,16},{32,24},{40,32},{48,40},{56,48},{9,1},{17,9},... | collective-permute-start | bytes 24584 | tf_op jit(solution)/shard_map/ppermute | solution.py:232
  18.2 1.9 %collective-permute-start.2 = (bf16[32,128]{1,0:T(8,128)(2,1)S(1)}, bf16[32,128]{1,0:T(8,128)(2,1)S(1)}, u32[]{:S(2)}, u32[]{:S(2)}) collective-permute-start(bf16[32,128]{1,0:T(8,128)(2,1)S(1)} %shard_map.40), channel_id=1, source_target_pairs={{0,8},{8,16},{16,24},{24,32},{32,40},{40,48},{48,56},{1,9},{9,17},... | collective-permute-start | bytes 24584 | tf_op jit(solution)/shard_map/ppermute | solution.py:232
  20.1 5.0 %all-to-all-done.mine = bf16[4,34,16,128]{3,2,1,0:T(8,128)(2,1)S(1)} async-done(((bf16[4,34,16,128]{3,2,1,0:T(8,128)(2,1)}), bf16[4,34,16,128]{3,2,1,0:T(8,128)(2,1)S(1)}, u32[]{:S(2)}, u32[]{:S(2)}) %all-to-all-start) | async-done | bytes 557088 | tf_op jit(solution)/shard_map/all_to_all | solution.py:256
  25.1 1.9 %collective-permute-start = (bf16[4,34,16,128]{3,2,1,0:T(8,128)(2,1)S(1)}, bf16[4,34,16,128]{3,2,1,0:T(8,128)(2,1)S(1)}, u32[]{:S(2)}, u32[]{:S(2)}) collective-permute-start(bf16[4,34,16,128]{3,2,1,0:T(8,128)(2,1)S(1)} %all-to-all-done.mine), channel_id=1, source_target_pairs={{0,1},{1,0},{2,3},{3,2},{4,5},{5,4},{6,7},{7,6},{8,9},{9,8},{10,11... | collective-permute-start | bytes 1671176 | tf_op jit(solution)/shard_map/ppermute | solution.py:236
  27.0 0.0 copy-done.3
  27.1 0.0 collective-permute-done.3.right
  27.1 1.6 %collective-permute-done.2.left = bf16[32,128]{1,0:T(8,128)(2,1)S(1)} collective-permute-done((bf16[32,128]{1,0:T(8,128)(2,1)S(1)}, bf16[32,128]{1,0:T(8,128)(2,1)S(1)}, u32[]{:S(2)}, u32[]{:S(2)}) %collective-permute-start.2) | collective-permute-done | bytes 8224 | tf_op jit(solution)/shard_map/ppermute | solution.py:232
  28.6 0.1 shard_map.41
  28.7 4.7 %collective-permute-start.4 = (bf16[48,128]{1,0:T(8,128)(2,1)S(1)}, bf16[48,128]{1,0:T(8,128)(2,1)S(1)}, u32[]{:S(2)}, u32[]{:S(2)}) collective-permute-start(bf16[48,128]{1,0:T(8,128)(2,1)S(1)} %get-tuple-element.21), channel_id=1, source_target_pairs={{0,64},{64,128},{128,192},{192,256},{256,320},{320,384},{384,448},... | collective-permute-start | bytes 36872 | tf_op jit(solution)/shard_map/ppermute | solution.py:232
  33.4 1.9 %collective-permute-start.5 = (bf16[48,128]{1,0:T(8,128)(2,1)S(1)}, bf16[48,128]{1,0:T(8,128)(2,1)S(1)}, u32[]{:S(2)}, u32[]{:S(2)}) collective-permute-start(bf16[48,128]{1,0:T(8,128)(2,1)S(1)} %get-tuple-element.22), channel_id=1, source_target_pairs={{64,0},{128,64},{192,128},{256,192},{320,256},{384,320},{448,384},... | collective-permute-start | bytes 36872 | tf_op jit(solution)/shard_map/ppermute | solution.py:232
  35.4 0.1 copy.8
  35.5 0.0 collective-permute-done.4.above
  35.5 4.8 %collective-permute-done.5.below = bf16[48,128]{1,0:T(8,128)(2,1)S(1)} collective-permute-done((bf16[48,128]{1,0:T(8,128)(2,1)S(1)}, bf16[48,128]{1,0:T(8,128)(2,1)S(1)}, u32[]{:S(2)}, u32[]{:S(2)}) %collective-permute-start.5) | collective-permute-done | bytes 12320 | tf_op jit(solution)/shard_map/ppermute | solution.py:232
  40.2 0.7 %shard_map.42 = bf16[8,48,128]{2,1,0:T(8,128)(2,1)} custom-call(bf16[48,128]{1,0:T(8,128)(2,1)S(1)} %collective-permute-done.4.above, bf16[48,128]{1,0:T(8,128)(2,1)S(1)} %collective-permute-done.5.below, f32[32,128]{1,0:T(8,128)S(1)} %get-tuple-element.23.beside), custom_call_target="tpu_custom_call" | custom-call | bytes 131072 | tf_op jit(solution)/shard_map/pallas_call | solution.py:21
  40.9 0.0 copy-start.2
  40.9 5.1 %all-to-all-start.1 = ((bf16[8,48,128]{2,1,0:T(8,128)(2,1)}), bf16[8,48,128]{2,1,0:T(8,128)(2,1)S(1)}, u32[]{:S(2)}, u32[]{:S(2)}) async-start(bf16[8,48,128]{2,1,0:T(8,128)(2,1)} %shard_map.42), calls=%async_computation.1 | async-start | bytes 196608 | tf_op jit(solution)/shard_map/all_to_all | solution.py:276
  46.1 0.0 copy-done.2
  46.1 3.9 %collective-permute-start.1 = (bf16[448,128]{1,0:T(8,128)(2,1)S(1)}, bf16[448,128]{1,0:T(8,128)(2,1)S(1)}, u32[]{:S(2)}, u32[]{:S(2)}) collective-permute-start(bf16[448,128]{1,0:T(8,128)(2,1)S(1)} %fusion.1.own.filters), channel_id=1, source_target_pairs={{0,2},{1,3},{2,0},{3,1},{4,6},{5,7},{6,4},{7,5},{8,10},{9,11},{10,... | collective-permute-start | bytes 344072 | tf_op jit(solution)/shard_map/ppermute | solution.py:236
  50.0 4.2 %collective-permute-done.1.other.filters = bf16[448,128]{1,0:T(8,128)(2,1)S(1)} collective-permute-done((bf16[448,128]{1,0:T(8,128)(2,1)S(1)}, bf16[448,128]{1,0:T(8,128)(2,1)S(1)}, u32[]{:S(2)}, u32[]{:S(2)}) %collective-permute-start.1) | collective-permute-done | bytes 114720 | tf_op jit(solution)/shard_map/ppermute | solution.py:236
  54.3 0.2 shard_map.38
  54.4 0.0 collective-permute-done.theirs
  54.5 0.9 %shard_map.39 = (f32[16,32,128]{2,1,0:T(8,128)S(1)}, f32[16,32,128]{2,1,0:T(8,128)S(1)}) custom-call(bf16[4,34,16,128]{3,2,1,0:T(8,128)(2,1)S(1)} %all-to-all-done.mine, bf16[4,34,16,128]{3,2,1,0:T(8,128)(2,1)S(1)} %collective-permute-done.theirs, bf16[288,256]{1,0:T(8,128)(2,1)S(1)} %get-tuple-element.16.taps, bf16[288,256]{1,0:T(8,128)(2,1)S(1)} %get-tuple-element.17.taps2.taps), custom_call_target="tpu_custom_call" | custom-call | flops 603979776 | bytes 3145728 | tf_op jit(solution)/shard_map/pallas_call | solution.py:21
  55.3 0.0 all-to-all-done.1.halo
  55.4 0.8 %shard_map.43 = bf16[16,2,16,128]{3,2,1,0:T(8,128)(2,1)S(1)} custom-call(f32[16,32,128]{2,1,0:T(8,128)S(1)} %get-tuple-element.18.pre, bf16[288,256]{1,0:T(8,128)(2,1)S(1)} %get-tuple-element.17.taps2.taps, bf16[4,34,16,128]{3,2,1,0:T(8,128)(2,1)S(1)} %all-to-all-done.mine, bf16[4,34,16,128]{3,2,1,0:T(8,128)(2,1)S(1)} %collective-permute-done.theirs, ...), custom_call_target="tpu_custom_call" | custom-call | flops 37748736 | bytes 1048576 | tf_op jit(solution)/shard_map/pallas_call | solution.py:21
  56.2 2.8 %collective-permute-start.6 = (bf16[16,2,16,128]{3,2,1,0:T(8,128)(2,1)S(1)}, bf16[16,2,16,128]{3,2,1,0:T(8,128)(2,1)S(1)}, u32[]{:S(2)}, u32[]{:S(2)}) collective-permute-start(bf16[16,2,16,128]{3,2,1,0:T(8,128)(2,1)S(1)} %shard_map.43), channel_id=1, source_target_pairs={{0,2},{1,3},{2,0},{3,1},{4,6},{5,7},{6,4},{7,5},{8,10},{9,11},{10,... | collective-permute-start | bytes 393224 | tf_op jit(solution)/shard_map/ppermute | solution.py:236
  59.0 1.5 %shard_map.44.held = bf16[16,2,32,128]{3,2,1,0:T(8,128)(2,1)} custom-call(f32[16,32,128]{2,1,0:T(8,128)S(1)} %get-tuple-element.24.pre, bf16[288,256]{1,0:T(8,128)(2,1)S(1)} %get-tuple-element.16.taps, bf16[4,34,16,128]{3,2,1,0:T(8,128)(2,1)S(1)} %all-to-all-done.mine, bf16[4,34,16,128]{3,2,1,0:T(8,128)(2,1)S(1)} %collective-permute-done.theirs, ...), custom_call_target="tpu_custom_call" | custom-call | flops 37748736 | bytes 1048576 | tf_op jit(solution)/shard_map/pallas_call | solution.py:21
  60.5 2.9 %collective-permute-done.6.got = bf16[16,2,16,128]{3,2,1,0:T(8,128)(2,1)S(1)} collective-permute-done((bf16[16,2,16,128]{3,2,1,0:T(8,128)(2,1)S(1)}, bf16[16,2,16,128]{3,2,1,0:T(8,128)(2,1)S(1)}, u32[]{:S(2)}, u32[]{:S(2)}) %collective-permute-start.6) | collective-permute-done | bytes 131104 | tf_op jit(solution)/shard_map/ppermute | solution.py:236
  63.5 0.7 %shard_map.45 = bf16[16,2,32,128]{3,2,1,0:T(8,128)(2,1)} custom-call(bf16[16,2,16,128]{3,2,1,0:T(8,128)(2,1)S(1)} %collective-permute-done.6.got, bf16[16,2,32,128]{3,2,1,0:T(8,128)(2,1)} %shard_map.44.held), custom_call_target="tpu_custom_call", output_to_operand_aliasing={{}: (1, {})} | custom-call | bytes 262144 | tf_op jit(solution)/shard_map/pallas_call | solution.py:21
  (3 shorter events, 0.0 us)
Async XLA Ops:
  0.0 0.9 %copy-start = (bf16[16,2,32,128]{3,2,1,0:T(8,128)(2,1)S(1)}, bf16[16,2,32,128]{3,2,1,0:T(8,128)(2,1)}, u32[]{:S(2)}) copy-start(bf16[16,2,32,128]{3,2,1,0:T(8,128)(2,1)} %vol.3) | copy-start | bytes 786436
  2.1 7.4 %copy-start.1 = (bf16[16,2,32,128]{3,2,1,0:T(8,128)(2,1)S(1)}, bf16[16,2,32,128]{3,2,1,0:T(8,128)(2,1)}, u32[]{:S(2)}) copy-start(bf16[16,2,32,128]{3,2,1,0:T(8,128)(2,1)} %vol.3) | copy-start | bytes 786436
  2.1 23.0 %all-to-all-start = ((bf16[4,34,16,128]{3,2,1,0:T(8,128)(2,1)}), bf16[4,34,16,128]{3,2,1,0:T(8,128)(2,1)S(1)}, u32[]{:S(2)}, u32[]{:S(2)}) async-start(bf16[4,34,16,128]{3,2,1,0:T(8,128)(2,1)} %get-tuple-element.15), calls=%async_computation | async-start | bytes 1114112 | tf_op jit(solution)/shard_map/all_to_all | solution.py:256
  9.5 17.5 %copy-start.3 = (f32[16]{0:T(128)S(1)}, f32[16]{0:T(128)}, u32[]{:S(2)}) copy-start(f32[16]{0:T(128)} %param.5) | copy-start | bytes 196
  9.7 17.4 %collective-permute-start.3 = (bf16[32,128]{1,0:T(8,128)(2,1)S(1)}, bf16[32,128]{1,0:T(8,128)(2,1)S(1)}, u32[]{:S(2)}, u32[]{:S(2)}) collective-permute-start(bf16[32,128]{1,0:T(8,128)(2,1)S(1)} %shard_map.40), channel_id=1, source_target_pairs={{8,0},{16,8},{24,16},{32,24},{40,32},{48,40},{56,48},{9,1},{17,9},... | collective-permute-start | bytes 24584 | tf_op jit(solution)/shard_map/ppermute | solution.py:232
  18.2 10.5 %collective-permute-start.2 = (bf16[32,128]{1,0:T(8,128)(2,1)S(1)}, bf16[32,128]{1,0:T(8,128)(2,1)S(1)}, u32[]{:S(2)}, u32[]{:S(2)}) collective-permute-start(bf16[32,128]{1,0:T(8,128)(2,1)S(1)} %shard_map.40), channel_id=1, source_target_pairs={{0,8},{8,16},{16,24},{24,32},{32,40},{40,48},{48,56},{1,9},{9,17},... | collective-permute-start | bytes 24584 | tf_op jit(solution)/shard_map/ppermute | solution.py:232
  25.1 29.3 %collective-permute-start = (bf16[4,34,16,128]{3,2,1,0:T(8,128)(2,1)S(1)}, bf16[4,34,16,128]{3,2,1,0:T(8,128)(2,1)S(1)}, u32[]{:S(2)}, u32[]{:S(2)}) collective-permute-start(bf16[4,34,16,128]{3,2,1,0:T(8,128)(2,1)S(1)} %all-to-all-done.mine), channel_id=1, source_target_pairs={{0,1},{1,0},{2,3},{3,2},{4,5},{5,4},{6,7},{7,6},{8,9},{9,8},{10,11... | collective-permute-start | bytes 1671176 | tf_op jit(solution)/shard_map/ppermute | solution.py:236
  28.7 6.7 %collective-permute-start.4 = (bf16[48,128]{1,0:T(8,128)(2,1)S(1)}, bf16[48,128]{1,0:T(8,128)(2,1)S(1)}, u32[]{:S(2)}, u32[]{:S(2)}) collective-permute-start(bf16[48,128]{1,0:T(8,128)(2,1)S(1)} %get-tuple-element.21), channel_id=1, source_target_pairs={{0,64},{64,128},{128,192},{192,256},{256,320},{320,384},{384,448},... | collective-permute-start | bytes 36872 | tf_op jit(solution)/shard_map/ppermute | solution.py:232
  33.4 6.8 %collective-permute-start.5 = (bf16[48,128]{1,0:T(8,128)(2,1)S(1)}, bf16[48,128]{1,0:T(8,128)(2,1)S(1)}, u32[]{:S(2)}, u32[]{:S(2)}) collective-permute-start(bf16[48,128]{1,0:T(8,128)(2,1)S(1)} %get-tuple-element.22), channel_id=1, source_target_pairs={{64,0},{128,64},{192,128},{256,192},{320,256},{384,320},{448,384},... | collective-permute-start | bytes 36872 | tf_op jit(solution)/shard_map/ppermute | solution.py:232
  40.9 5.1 %copy-start.2 = (bf16[16,128,3,3,3]{1,0,4,3,2:T(8,128)(2,1)S(1)}, bf16[16,128,3,3,3]{1,0,4,3,2:T(8,128)(2,1)}, u32[]{:S(2)}) copy-start(bf16[16,128,3,3,3]{1,0,4,3,2:T(8,128)(2,1)} %param.4) | copy-start | bytes 331780
  40.9 14.4 %all-to-all-start.1 = ((bf16[8,48,128]{2,1,0:T(8,128)(2,1)}), bf16[8,48,128]{2,1,0:T(8,128)(2,1)S(1)}, u32[]{:S(2)}, u32[]{:S(2)}) async-start(bf16[8,48,128]{2,1,0:T(8,128)(2,1)} %shard_map.42), calls=%async_computation.1 | async-start | bytes 196608 | tf_op jit(solution)/shard_map/all_to_all | solution.py:276
  46.1 8.2 %collective-permute-start.1 = (bf16[448,128]{1,0:T(8,128)(2,1)S(1)}, bf16[448,128]{1,0:T(8,128)(2,1)S(1)}, u32[]{:S(2)}, u32[]{:S(2)}) collective-permute-start(bf16[448,128]{1,0:T(8,128)(2,1)S(1)} %fusion.1.own.filters), channel_id=1, source_target_pairs={{0,2},{1,3},{2,0},{3,1},{4,6},{5,7},{6,4},{7,5},{8,10},{9,11},{10,... | collective-permute-start | bytes 344072 | tf_op jit(solution)/shard_map/ppermute | solution.py:236
  56.2 7.3 %collective-permute-start.6 = (bf16[16,2,16,128]{3,2,1,0:T(8,128)(2,1)S(1)}, bf16[16,2,16,128]{3,2,1,0:T(8,128)(2,1)S(1)}, u32[]{:S(2)}, u32[]{:S(2)}) collective-permute-start(bf16[16,2,16,128]{3,2,1,0:T(8,128)(2,1)S(1)} %shard_map.43), channel_id=1, source_target_pairs={{0,2},{1,3},{2,0},{3,1},{4,6},{5,7},{6,4},{7,5},{8,10},{9,11},{10,... | collective-permute-start | bytes 393224 | tf_op jit(solution)/shard_map/ppermute | solution.py:236

commit v10 on v9

--- a/solution.py
+++ b/solution.py
@@ -8,7 +8,6 @@
 
 BF = jnp.bfloat16
 F32 = jnp.float32
-CORES = [[0, 2, 4, 6], [1, 3, 5, 7]]
 GRANT = 16 << 20
 
 
@@ -50,19 +49,21 @@
     cols[...] = both.astype(BF)
 
 
-def pack_kernel(vol, blocks, first, last, flat):
+def pack_kernel(vol, same, other, first, last, flat):
+    half = half_of()
     flat[...] = vol[...].reshape(1024, 128).astype(F32)
+    for to, start in ((same, 15 * half), (other, 15 * (1 - half))):
+        for z in range(2):
+            for i in range(17):
+                to[z * 17 + i] = flat[pl.ds(start + z * 32 + i, 16, stride=64), :].astype(BF)
     for z in range(2):
-        for row in range(32):
-            tile = flat[pl.ds(z * 32 + row, 16, stride=64), :].astype(BF)
-            for chip in range(4):
-                at = row - 15 * (chip % 2)
-                if 0 <= at < 17:
-                    blocks[chip, z * 17 + at] = tile
-            if row == 0:
-                first[pl.ds(z * 16, 16)] = tile
-            if row == 31:
-                last[pl.ds(z * 16, 16)] = tile
+        first[pl.ds(z * 16, 16)] = flat[pl.ds(z * 32, 16, stride=64), :].astype(BF)
+        last[pl.ds(z * 16, 16)] = flat[pl.ds(z * 32 + 31, 16, stride=64), :].astype(BF)
+
+
+def join_kernel(p0, p1, p2, p3, joined):
+    for m, piece in enumerate((p0, p1, p2, p3)):
+        joined[m] = piece[...]
 
 
 def beside_kernel(first, last, left, right, up, down, beside):
@@ -99,15 +100,22 @@
 
 
 def taps_kernel(own, other, taps, taps2):
-    odd = lax.rem(lax.axis_index("ch"), 2) == 1
-    even_block = lax.rem(lanes_of((16, 128)) // 16, 2) == 0
+    me = lax.axis_index("ch")
+    lane = lanes_of((16, 128))
     for filters, to in ((own, taps), (other, taps2)):
         for a in range(3):
             for b in range(3):
                 for e in range(3):
                     tile = filters[pl.ds((a * 9 + b * 3 + e) * 16, 16)].astype(F32)
-                    swapped = jnp.where(even_block, pltpu.roll(tile, 112, 1), pltpu.roll(tile, 16, 1))
-                    tile = jnp.where(odd, swapped, tile).astype(BF)
+                    for bit in range(3):
+                        width = 16 << bit
+                        swapped = jnp.where(
+                            lax.rem(lane // width, 2) == 0,
+                            pltpu.roll(tile, 128 - width, 1),
+                            pltpu.roll(tile, width, 1),
+                        )
+                        tile = jnp.where(lax.rem(me // (1 << bit), 2) == 1, swapped, tile)
+                    tile = tile.astype(BF)
                     for zo in range(2):
                         zi = a - 1 + zo
                         if 0 <= zi < 2:
@@ -154,11 +162,11 @@
 
 def outer_kernel(pre, taps, mine, theirs, halo, filters, out, flat):
     me = lax.axis_index("ch")
-    half, core = half_of(), lax.rem(me, 2)
+    half = half_of()
     parts = filters[pl.ds(432, 16)].astype(F32)
     offset = (parts[:, 0:1] + parts[:, 1:2]) + parts[:, 2:3]
     offset = jnp.concatenate([offset, offset], axis=0)
-    sources = [2 * chip + (core ^ t) for chip in range(4) for t in range(2)]
+    sources = [me ^ j for j in range(8)]
     lane24 = lanes_of((24, 128))
     total = [[jnp.zeros((24, 128), F32) for _ in range(2)] for _ in range(2)]
     for j, source in enumerate(sources):
@@ -246,14 +254,17 @@
 
 def stages(volume, weights, bias):
     cols = call(columns_kernel, shaped(32, 128), [], volume, moved=1 << 19)
-    blocks, first, last = call(
+    same, rest, first, last = call(
         pack_kernel,
-        [shaped(4, 34, 16, 128), shaped(32, 128), shaped(32, 128)],
+        [shaped(34, 16, 128), shaped(34, 16, 128), shaped(32, 128), shaped(32, 128)],
         [pltpu.VMEM((1024, 128), F32)],
         volume,
         moved=1 << 20,
     )
-    mine = lax.all_to_all(blocks, "ch", split_axis=0, concat_axis=0, tiled=True, axis_index_groups=CORES)
+    piece3 = swapped(rest, 6)
+    piece2 = swapped(same, 4)
+    piece1 = swapped(rest, 2)
+    mine = call(join_kernel, shaped(4, 34, 16, 128), [], same, piece1, piece2, piece3, moved=1 << 20)
     left = shifts(cols, "sy", True)
     right = shifts(cols, "sy", False)
     own = jnp.concatenate([weights.transpose(2, 3, 4, 0, 1).reshape(432, 128), thirds(bias)], axis=0)

time: 64.6 us -> 71.2 us (1.10)
  starting transfers between devices: 38.2 us -> 42.3 us
  Pallas kernels: 6.19 us -> 8.83 us
    ppermute x3 -> x6, starting transfers between devices: 8.67 us -> 21 us  [swapped(): return lax.ppermute(array, 'ch', [(d, d ^ t) for d in range(8)])]
    all_to_all x1 -> x0, starting transfers between devices: 7.39 us -> none  [stages(): lax.all_to_all(blocks, 'ch', split_axis=0, concat_axis=0, tiled=True, axi...]
    all_to_all x1 -> x0, waiting for transfers between devices: 5 us -> none  [stages(): lax.all_to_all(blocks, 'ch', split_axis=0, concat_axis=0, tiled=True, axi...]
    ppermute x4, waiting for transfers between devices: 6.34 us -> 11.1 us  [shifts(): lax.ppermute(array, axis, pairs if up else [(j, i) for i, j in pairs])]
    pallas_call x9 -> x10, Pallas kernels: 6.19 us -> 8.83 us  [call(): pl.pallas_call(kernel, out_shape=out_shapes, in_specs=in_specs, out_specs...]
    all_to_all x1, starting transfers between devices: 5.13 us -> 4.32 us  [stages(): halo = lax.all_to_all(halo, 'ch', split_axis=0, concat_axis=0, tiled=True)]
    ppermute x3 -> x6, waiting for transfers between devices: 7.15 us -> 7.16 us  [swapped(): return lax.ppermute(array, 'ch', [(d, d ^ t) for d in range(8)])]
  transfers between devices with their start and end apart: 9 -> 11, of which waited for: 5 -> 4; matrix products, arithmetic and copies ran while one was open for 0% -> 0% of each run, Pallas kernels for 6% -> 10%
where the time goes in v10:
time: 71.2 us; the launch traced here: 70.7 us
  starting transfers between devices  42.3 us (59%)
  waiting for transfers between devices  18.3 us (26%)
  Pallas kernels  8.83 us (12%)
  local copies, waits for them, and re-layouts  1.05 us (1%)
    ppermute x6, starting transfers between devices, swapped(): return lax.ppermute(array, 'ch', [(d, d ^ t) for d in range(8)])  21 us
    ppermute x4, starting transfers between devices, shifts(): lax.ppermute(array, axis, pairs if up else [(j, i) for i, j in pairs])  17 us
    ppermute x4, waiting for transfers between devices, shifts(): lax.ppermute(array, axis, pairs if up else [(j, i) for i, j in pairs])  11.1 us
    pallas_call x10, Pallas kernels, call(): pl.pallas_call(kernel, out_shape=out_shapes, in_specs=in_specs, out_specs...  8.83 us
    ppermute x6, waiting for transfers between devices, swapped(): return lax.ppermute(array, 'ch', [(d, d ^ t) for d in range(8)])  7.16 us
    all_to_all x1, starting transfers between devices, stages(): halo = lax.all_to_all(halo, 'ch', split_axis=0, concat_axis=0, tiled=True)  4.32 us
  transfers between devices with their start and end apart: 11, of which 4 were waited for; matrix products, arithmetic and copies ran while one was open for 0% of the time, Pallas kernels for 10%

profile of v10, /device:TPU:30, one launch (start us, length us, event | category | flops | bytes accessed | tf_op | source)
XLA Modules:
  0.0 70.7 jit_solution(8011290815673314802)
XLA Ops:
  0.0 0.0 copy-start
  0.0 0.9 %copy-done = bf16[16,2,32,128]{3,2,1,0:T(8,128)(2,1)S(1)} copy-done((bf16[16,2,32,128]{3,2,1,0:T(8,128)(2,1)S(1)}, bf16[16,2,32,128]{3,2,1,0:T(8,128)(2,1)}, u32[]{:S(2)}) %copy-start) | copy-done | bytes 262168
  1.0 0.4 shard_map.37
  1.3 6.1 %collective-permute-start.1 = (bf16[34,16,128]{2,1,0:T(8,128)(2,1)S(1)}, bf16[34,16,128]{2,1,0:T(8,128)(2,1)S(1)}, u32[]{:S(2)}, u32[]{:S(2)}) collective-permute-start(bf16[34,16,128]{2,1,0:T(8,128)(2,1)S(1)} %get-tuple-element.16.p0), channel_id=1, source_target_pairs={{0,4},{1,5},{2,6},{3,7},{4,0},{5,1},{6,2},{7,3},{8,12},{9,13},{10,... | collective-permute-start | bytes 417800 | tf_op jit(solution)/shard_map/ppermute | solution.py:244
  7.4 3.7 %collective-permute-start.2 = (bf16[34,16,128]{2,1,0:T(8,128)(2,1)S(1)}, bf16[34,16,128]{2,1,0:T(8,128)(2,1)S(1)}, u32[]{:S(2)}, u32[]{:S(2)}) collective-permute-start(bf16[34,16,128]{2,1,0:T(8,128)(2,1)S(1)} %get-tuple-element.17), channel_id=1, source_target_pairs={{0,6},{1,7},{2,4},{3,5},{4,2},{5,3},{6,0},{7,1},{8,14},{9,15},{10,... | collective-permute-start | bytes 417800 | tf_op jit(solution)/shard_map/ppermute | solution.py:244
  11.2 2.5 %collective-permute-start = (bf16[34,16,128]{2,1,0:T(8,128)(2,1)S(1)}, bf16[34,16,128]{2,1,0:T(8,128)(2,1)S(1)}, u32[]{:S(2)}, u32[]{:S(2)}) collective-permute-start(bf16[34,16,128]{2,1,0:T(8,128)(2,1)S(1)} %get-tuple-element.17), channel_id=1, source_target_pairs={{0,2},{1,3},{2,0},{3,1},{4,6},{5,7},{6,4},{7,5},{8,10},{9,11},{10,... | collective-permute-start | bytes 417800 | tf_op jit(solution)/shard_map/ppermute | solution.py:244
  13.6 0.2 shard_map.41
  13.8 0.0 copy-start.2
  13.9 8.5 %collective-permute-start.6 = (bf16[32,128]{1,0:T(8,128)(2,1)S(1)}, bf16[32,128]{1,0:T(8,128)(2,1)S(1)}, u32[]{:S(2)}, u32[]{:S(2)}) collective-permute-start(bf16[32,128]{1,0:T(8,128)(2,1)S(1)} %shard_map.41), channel_id=1, source_target_pairs={{8,0},{16,8},{24,16},{32,24},{40,32},{48,40},{56,48},{9,1},{17,9},... | collective-permute-start | bytes 24584 | tf_op jit(solution)/shard_map/ppermute | solution.py:240
  22.3 1.9 %collective-permute-start.5 = (bf16[32,128]{1,0:T(8,128)(2,1)S(1)}, bf16[32,128]{1,0:T(8,128)(2,1)S(1)}, u32[]{:S(2)}, u32[]{:S(2)}) collective-permute-start(bf16[32,128]{1,0:T(8,128)(2,1)S(1)} %shard_map.41), channel_id=1, source_target_pairs={{0,8},{8,16},{16,24},{24,32},{32,40},{40,48},{48,56},{1,9},{9,17},... | collective-permute-start | bytes 24584 | tf_op jit(solution)/shard_map/ppermute | solution.py:240
  24.3 0.0 collective-permute-done.1.p2
  24.3 0.0 collective-permute-done.2.p3
  24.3 0.0 collective-permute-done.p1
  24.4 1.9 %collective-permute-start.3 = (bf16[4,34,16,128]{3,2,1,0:T(8,128)(2,1)S(1)}, bf16[4,34,16,128]{3,2,1,0:T(8,128)(2,1)S(1)}, u32[]{:S(2)}, u32[]{:S(2)}) collective-permute-start(bf16[4,34,16,128]{3,2,1,0:T(8,128)(2,1)S(1)} %shard_map.38.mine), channel_id=1, source_target_pairs={{0,1},{1,0},{2,3},{3,2},{4,5},{5,4},{6,7},{7,6},{8,9},{9,8},{10,11... | collective-permute-start | bytes 1671176 | tf_op jit(solution)/shard_map/ppermute | solution.py:244
  26.3 0.0 copy-done.2
  26.3 0.0 collective-permute-done.6.right
  26.3 6.4 %collective-permute-done.5.left = bf16[32,128]{1,0:T(8,128)(2,1)S(1)} collective-permute-done((bf16[32,128]{1,0:T(8,128)(2,1)S(1)}, bf16[32,128]{1,0:T(8,128)(2,1)S(1)}, u32[]{:S(2)}, u32[]{:S(2)}) %collective-permute-start.5) | collective-permute-done | bytes 8224 | tf_op jit(solution)/shard_map/ppermute | solution.py:240
  32.7 0.1 shard_map.42
  32.8 4.7 %collective-permute-start.7 = (bf16[48,128]{1,0:T(8,128)(2,1)S(1)}, bf16[48,128]{1,0:T(8,128)(2,1)S(1)}, u32[]{:S(2)}, u32[]{:S(2)}) collective-permute-start(bf16[48,128]{1,0:T(8,128)(2,1)S(1)} %get-tuple-element.23), channel_id=1, source_target_pairs={{0,64},{64,128},{128,192},{192,256},{256,320},{320,384},{384,448},... | collective-permute-start | bytes 36872 | tf_op jit(solution)/shard_map/ppermute | solution.py:240
  37.5 1.9 %collective-permute-start.8 = (bf16[48,128]{1,0:T(8,128)(2,1)S(1)}, bf16[48,128]{1,0:T(8,128)(2,1)S(1)}, u32[]{:S(2)}, u32[]{:S(2)}) collective-permute-start(bf16[48,128]{1,0:T(8,128)(2,1)S(1)} %get-tuple-element.24), channel_id=1, source_target_pairs={{64,0},{128,64},{192,128},{256,192},{320,256},{384,320},{448,384},... | collective-permute-start | bytes 36872 | tf_op jit(solution)/shard_map/ppermute | solution.py:240
  39.4 0.1 copy.8
  39.5 0.0 collective-permute-done.7.above
  39.5 4.8 %collective-permute-done.8.below = bf16[48,128]{1,0:T(8,128)(2,1)S(1)} collective-permute-done((bf16[48,128]{1,0:T(8,128)(2,1)S(1)}, bf16[48,128]{1,0:T(8,128)(2,1)S(1)}, u32[]{:S(2)}, u32[]{:S(2)}) %collective-permute-start.8) | collective-permute-done | bytes 12320 | tf_op jit(solution)/shard_map/ppermute | solution.py:240
  44.3 0.7 %shard_map.43 = bf16[8,48,128]{2,1,0:T(8,128)(2,1)} custom-call(bf16[48,128]{1,0:T(8,128)(2,1)S(1)} %collective-permute-done.7.above, bf16[48,128]{1,0:T(8,128)(2,1)S(1)} %collective-permute-done.8.below, f32[32,128]{1,0:T(8,128)S(1)} %get-tuple-element.25.beside), custom_call_target="tpu_custom_call" | custom-call | bytes 131072 | tf_op jit(solution)/shard_map/pallas_call | solution.py:20
  45.0 0.0 copy-start.1
  45.0 4.3 %all-to-all-start = ((bf16[8,48,128]{2,1,0:T(8,128)(2,1)}), bf16[8,48,128]{2,1,0:T(8,128)(2,1)S(1)}, u32[]{:S(2)}, u32[]{:S(2)}) async-start(bf16[8,48,128]{2,1,0:T(8,128)(2,1)} %shard_map.43), calls=%async_computation | async-start | bytes 196608 | tf_op jit(solution)/shard_map/all_to_all | solution.py:287
  49.3 0.0 copy-done.1
  49.3 3.9 %collective-permute-start.4 = (bf16[448,128]{1,0:T(8,128)(2,1)S(1)}, bf16[448,128]{1,0:T(8,128)(2,1)S(1)}, u32[]{:S(2)}, u32[]{:S(2)}) collective-permute-start(bf16[448,128]{1,0:T(8,128)(2,1)S(1)} %fusion.1.own.filters), channel_id=1, source_target_pairs={{0,2},{1,3},{2,0},{3,1},{4,6},{5,7},{6,4},{7,5},{8,10},{9,11},{10,... | collective-permute-start | bytes 344072 | tf_op jit(solution)/shard_map/ppermute | solution.py:244
  53.3 4.2 %collective-permute-done.4.other.filters = bf16[448,128]{1,0:T(8,128)(2,1)S(1)} collective-permute-done((bf16[448,128]{1,0:T(8,128)(2,1)S(1)}, bf16[448,128]{1,0:T(8,128)(2,1)S(1)}, u32[]{:S(2)}, u32[]{:S(2)}) %collective-permute-start.4) | collective-permute-done | bytes 114720 | tf_op jit(solution)/shard_map/ppermute | solution.py:244
  57.5 3.6 %shard_map.39 = (bf16[288,256]{1,0:T(8,128)(2,1)S(1)}, bf16[288,256]{1,0:T(8,128)(2,1)S(1)}) custom-call(bf16[448,128]{1,0:T(8,128)(2,1)S(1)} %fusion.1.own.filters, bf16[448,128]{1,0:T(8,128)(2,1)S(1)} %collective-permute-done.4.other.filters), custom_call_target="tpu_custom_call" | custom-call | bytes 524288 | tf_op jit(solution)/shard_map/pallas_call | solution.py:20
  61.1 0.0 collective-permute-done.3.theirs
  61.1 0.9 %shard_map.40 = (f32[16,32,128]{2,1,0:T(8,128)S(1)}, f32[16,32,128]{2,1,0:T(8,128)S(1)}) custom-call(bf16[4,34,16,128]{3,2,1,0:T(8,128)(2,1)S(1)} %shard_map.38.mine, bf16[4,34,16,128]{3,2,1,0:T(8,128)(2,1)S(1)} %collective-permute-done.3.theirs, bf16[288,256]{1,0:T(8,128)(2,1)S(1)} %get-tuple-element.18.taps, bf16[288,256]{1,0:T(8,128)(2,1)S(1)} %get-tuple-element.19.taps2.taps), custom_call_target="tpu_custom_call" | custom-call | flops 603979776 | bytes 3145728 | tf_op jit(solution)/shard_map/pallas_call | solution.py:20
  62.0 0.0 all-to-all-done.halo
  62.0 0.8 %shard_map.44 = bf16[16,2,16,128]{3,2,1,0:T(8,128)(2,1)S(1)} custom-call(f32[16,32,128]{2,1,0:T(8,128)S(1)} %get-tuple-element.20.pre, bf16[288,256]{1,0:T(8,128)(2,1)S(1)} %get-tuple-element.19.taps2.taps, bf16[4,34,16,128]{3,2,1,0:T(8,128)(2,1)S(1)} %shard_map.38.mine, bf16[4,34,16,128]{3,2,1,0:T(8,128)(2,1)S(1)} %collective-permute-done.3.theirs, ...), custom_call_target="tpu_custom_call" | custom-call | flops 37748736 | bytes 1048576 | tf_op jit(solution)/shard_map/pallas_call | solution.py:20
  62.8 2.8 %collective-permute-start.9 = (bf16[16,2,16,128]{3,2,1,0:T(8,128)(2,1)S(1)}, bf16[16,2,16,128]{3,2,1,0:T(8,128)(2,1)S(1)}, u32[]{:S(2)}, u32[]{:S(2)}) collective-permute-start(bf16[16,2,16,128]{3,2,1,0:T(8,128)(2,1)S(1)} %shard_map.44), channel_id=1, source_target_pairs={{0,2},{1,3},{2,0},{3,1},{4,6},{5,7},{6,4},{7,5},{8,10},{9,11},{10,... | collective-permute-start | bytes 393224 | tf_op jit(solution)/shard_map/ppermute | solution.py:244
  65.7 1.5 %shard_map.45.held = bf16[16,2,32,128]{3,2,1,0:T(8,128)(2,1)} custom-call(f32[16,32,128]{2,1,0:T(8,128)S(1)} %get-tuple-element.26.pre, bf16[288,256]{1,0:T(8,128)(2,1)S(1)} %get-tuple-element.18.taps, bf16[4,34,16,128]{3,2,1,0:T(8,128)(2,1)S(1)} %shard_map.38.mine, bf16[4,34,16,128]{3,2,1,0:T(8,128)(2,1)S(1)} %collective-permute-done.3.theirs, ...), custom_call_target="tpu_custom_call" | custom-call | flops 37748736 | bytes 1048576 | tf_op jit(solution)/shard_map/pallas_call | solution.py:20
  67.2 2.9 %collective-permute-done.9.got = bf16[16,2,16,128]{3,2,1,0:T(8,128)(2,1)S(1)} collective-permute-done((bf16[16,2,16,128]{3,2,1,0:T(8,128)(2,1)S(1)}, bf16[16,2,16,128]{3,2,1,0:T(8,128)(2,1)S(1)}, u32[]{:S(2)}, u32[]{:S(2)}) %collective-permute-start.9) | collective-permute-done | bytes 131104 | tf_op jit(solution)/shard_map/ppermute | solution.py:244
  70.1 0.7 shard_map.46
  (4 shorter events, 0.1 us)
Async XLA Ops:
  0.0 0.9 %copy-start = (bf16[16,2,32,128]{3,2,1,0:T(8,128)(2,1)S(1)}, bf16[16,2,32,128]{3,2,1,0:T(8,128)(2,1)}, u32[]{:S(2)}) copy-start(bf16[16,2,32,128]{3,2,1,0:T(8,128)(2,1)} %vol.3) | copy-start | bytes 786436
  1.3 23.0 %collective-permute-start.1 = (bf16[34,16,128]{2,1,0:T(8,128)(2,1)S(1)}, bf16[34,16,128]{2,1,0:T(8,128)(2,1)S(1)}, u32[]{:S(2)}, u32[]{:S(2)}) collective-permute-start(bf16[34,16,128]{2,1,0:T(8,128)(2,1)S(1)} %get-tuple-element.16.p0), channel_id=1, source_target_pairs={{0,4},{1,5},{2,6},{3,7},{4,0},{5,1},{6,2},{7,3},{8,12},{9,13},{10,... | collective-permute-start | bytes 417800 | tf_op jit(solution)/shard_map/ppermute | solution.py:244
  7.4 16.9 %collective-permute-start.2 = (bf16[34,16,128]{2,1,0:T(8,128)(2,1)S(1)}, bf16[34,16,128]{2,1,0:T(8,128)(2,1)S(1)}, u32[]{:S(2)}, u32[]{:S(2)}) collective-permute-start(bf16[34,16,128]{2,1,0:T(8,128)(2,1)S(1)} %get-tuple-element.17), channel_id=1, source_target_pairs={{0,6},{1,7},{2,4},{3,5},{4,2},{5,3},{6,0},{7,1},{8,14},{9,15},{10,... | collective-permute-start | bytes 417800 | tf_op jit(solution)/shard_map/ppermute | solution.py:244
  11.2 13.1 %collective-permute-start = (bf16[34,16,128]{2,1,0:T(8,128)(2,1)S(1)}, bf16[34,16,128]{2,1,0:T(8,128)(2,1)S(1)}, u32[]{:S(2)}, u32[]{:S(2)}) collective-permute-start(bf16[34,16,128]{2,1,0:T(8,128)(2,1)S(1)} %get-tuple-element.17), channel_id=1, source_target_pairs={{0,2},{1,3},{2,0},{3,1},{4,6},{5,7},{6,4},{7,5},{8,10},{9,11},{10,... | collective-permute-start | bytes 417800 | tf_op jit(solution)/shard_map/ppermute | solution.py:244
  13.8 12.4 %copy-start.2 = (f32[16]{0:T(128)S(1)}, f32[16]{0:T(128)}, u32[]{:S(2)}) copy-start(f32[16]{0:T(128)} %param.5) | copy-start | bytes 196
  13.9 12.5 %collective-permute-start.6 = (bf16[32,128]{1,0:T(8,128)(2,1)S(1)}, bf16[32,128]{1,0:T(8,128)(2,1)S(1)}, u32[]{:S(2)}, u32[]{:S(2)}) collective-permute-start(bf16[32,128]{1,0:T(8,128)(2,1)S(1)} %shard_map.41), channel_id=1, source_target_pairs={{8,0},{16,8},{24,16},{32,24},{40,32},{48,40},{56,48},{9,1},{17,9},... | collective-permute-start | bytes 24584 | tf_op jit(solution)/shard_map/ppermute | solution.py:240
  22.3 10.4 %collective-permute-start.5 = (bf16[32,128]{1,0:T(8,128)(2,1)S(1)}, bf16[32,128]{1,0:T(8,128)(2,1)S(1)}, u32[]{:S(2)}, u32[]{:S(2)}) collective-permute-start(bf16[32,128]{1,0:T(8,128)(2,1)S(1)} %shard_map.41), channel_id=1, source_target_pairs={{0,8},{8,16},{16,24},{24,32},{32,40},{40,48},{48,56},{1,9},{9,17},... | collective-permute-start | bytes 24584 | tf_op jit(solution)/shard_map/ppermute | solution.py:240
  24.4 36.7 %collective-permute-start.3 = (bf16[4,34,16,128]{3,2,1,0:T(8,128)(2,1)S(1)}, bf16[4,34,16,128]{3,2,1,0:T(8,128)(2,1)S(1)}, u32[]{:S(2)}, u32[]{:S(2)}) collective-permute-start(bf16[4,34,16,128]{3,2,1,0:T(8,128)(2,1)S(1)} %shard_map.38.mine), channel_id=1, source_target_pairs={{0,1},{1,0},{2,3},{3,2},{4,5},{5,4},{6,7},{7,6},{8,9},{9,8},{10,11... | collective-permute-start | bytes 1671176 | tf_op jit(solution)/shard_map/ppermute | solution.py:244
  32.8 6.7 %collective-permute-start.7 = (bf16[48,128]{1,0:T(8,128)(2,1)S(1)}, bf16[48,128]{1,0:T(8,128)(2,1)S(1)}, u32[]{:S(2)}, u32[]{:S(2)}) collective-permute-start(bf16[48,128]{1,0:T(8,128)(2,1)S(1)} %get-tuple-element.23), channel_id=1, source_target_pairs={{0,64},{64,128},{128,192},{192,256},{256,320},{320,384},{384,448},... | collective-permute-start | bytes 36872 | tf_op jit(solution)/shard_map/ppermute | solution.py:240
  37.5 6.8 %collective-permute-start.8 = (bf16[48,128]{1,0:T(8,128)(2,1)S(1)}, bf16[48,128]{1,0:T(8,128)(2,1)S(1)}, u32[]{:S(2)}, u32[]{:S(2)}) collective-permute-start(bf16[48,128]{1,0:T(8,128)(2,1)S(1)} %get-tuple-element.24), channel_id=1, source_target_pairs={{64,0},{128,64},{192,128},{256,192},{320,256},{384,320},{448,384},... | collective-permute-start | bytes 36872 | tf_op jit(solution)/shard_map/ppermute | solution.py:240
  45.0 4.3 %copy-start.1 = (bf16[16,128,3,3,3]{1,0,4,3,2:T(8,128)(2,1)S(1)}, bf16[16,128,3,3,3]{1,0,4,3,2:T(8,128)(2,1)}, u32[]{:S(2)}) copy-start(bf16[16,128,3,3,3]{1,0,4,3,2:T(8,128)(2,1)} %param.4) | copy-start | bytes 331780
  45.0 17.0 %all-to-all-start = ((bf16[8,48,128]{2,1,0:T(8,128)(2,1)}), bf16[8,48,128]{2,1,0:T(8,128)(2,1)S(1)}, u32[]{:S(2)}, u32[]{:S(2)}) async-start(bf16[8,48,128]{2,1,0:T(8,128)(2,1)} %shard_map.43), calls=%async_computation | async-start | bytes 196608 | tf_op jit(solution)/shard_map/all_to_all | solution.py:287
  49.3 8.2 %collective-permute-start.4 = (bf16[448,128]{1,0:T(8,128)(2,1)S(1)}, bf16[448,128]{1,0:T(8,128)(2,1)S(1)}, u32[]{:S(2)}, u32[]{:S(2)}) collective-permute-start(bf16[448,128]{1,0:T(8,128)(2,1)S(1)} %fusion.1.own.filters), channel_id=1, source_target_pairs={{0,2},{1,3},{2,0},{3,1},{4,6},{5,7},{6,4},{7,5},{8,10},{9,11},{10,... | collective-permute-start | bytes 344072 | tf_op jit(solution)/shard_map/ppermute | solution.py:244
  62.8 7.3 %collective-permute-start.9 = (bf16[16,2,16,128]{3,2,1,0:T(8,128)(2,1)S(1)}, bf16[16,2,16,128]{3,2,1,0:T(8,128)(2,1)S(1)}, u32[]{:S(2)}, u32[]{:S(2)}) collective-permute-start(bf16[16,2,16,128]{3,2,1,0:T(8,128)(2,1)S(1)} %shard_map.44), channel_id=1, source_target_pairs={{0,2},{1,3},{2,0},{3,1},{4,6},{5,7},{6,4},{7,5},{8,10},{9,11},{10,... | collective-permute-start | bytes 393224 | tf_op jit(solution)/shard_map/ppermute | solution.py:244

commit v11 on v9

--- a/solution.py
+++ b/solution.py
@@ -12,17 +12,15 @@
 GRANT = 16 << 20
 
 
-def call(kernel, out_shapes, scratch, *args, flops=0, moved=0, place=None, shared=None):
-    vmem = pl.BlockSpec(memory_space=pltpu.VMEM)
+def call(kernel, out_shapes, scratch, *args, flops=0, moved=0, far_in=(), far_out=(), shared=None):
+    vmem, far = pl.BlockSpec(memory_space=pltpu.VMEM), pl.BlockSpec(memory_space=pl.ANY)
     many = isinstance(out_shapes, (list, tuple))
-    in_specs = [vmem] * len(args)
-    for i in shared or {}:
-        in_specs[i] = pl.BlockSpec(memory_space=pl.ANY)
+    outs = [far if i in far_out else vmem for i in range(len(out_shapes) if many else 1)]
     return pl.pallas_call(
         kernel,
         out_shape=out_shapes,
-        in_specs=in_specs,
-        out_specs=[vmem] * len(out_shapes) if many else place or vmem,
+        in_specs=[far if i in far_in else vmem for i in range(len(args))],
+        out_specs=outs if many else outs[0],
         scratch_shapes=scratch,
         input_output_aliases=shared or {},
         cost_estimate=pl.CostEstimate(flops=flops, bytes_accessed=moved, transcendentals=0),
@@ -38,31 +36,44 @@
     return lax.broadcasted_iota(jnp.int32, shape, len(shape) - 1)
 
 
-def columns_kernel(vol, cols):
+def columns_kernel(vol, cols, held, sems):
+    copies = [pltpu.make_async_copy(vol.at[c], held.at[c], sems.at[c]) for c in range(16)]
+    for copy in copies:
+        copy.start()
     lane = lanes_of((32, 128))
     both = jnp.zeros((32, 128), F32)
-    for z in range(2):
-        for c in range(16):
-            tile = vol[c, z].astype(F32)
+    for c in range(16):
+        copies[c].wait()
+        for z in range(2):
+            tile = held[c, z].astype(F32)
             j = z * 16 + c
             both = jnp.where(lane == j, pltpu.roll(tile, j, 1) if j else tile, both)
             both = jnp.where(lane == 32 + j, pltpu.roll(tile, 33 + j, 1), both)
     cols[...] = both.astype(BF)
 
 
-def pack_kernel(vol, blocks, first, last, flat):
+def pack_kernel(vol, blocks, first, last, flat, halves, sems):
     flat[...] = vol[...].reshape(1024, 128).astype(F32)
+    copies = []
     for z in range(2):
-        for row in range(32):
-            tile = flat[pl.ds(z * 32 + row, 16, stride=64), :].astype(BF)
-            for chip in range(4):
-                at = row - 15 * (chip % 2)
-                if 0 <= at < 17:
-                    blocks[chip, z * 17 + at] = tile
-            if row == 0:
-                first[pl.ds(z * 16, 16)] = tile
-            if row == 31:
-                last[pl.ds(z * 16, 16)] = tile
+        for half in range(2):
+            for at in range(17):
+                row = 15 * half + at
+                tile = flat[pl.ds(z * 32 + row, 16, stride=64), :].astype(BF)
+                halves[half, z * 17 + at] = tile
+                if row == 0:
+                    first[pl.ds(z * 16, 16)] = tile
+                if row == 31:
+                    last[pl.ds(z * 16, 16)] = tile
+            part = pl.ds(z * 17, 17)
+            for chip in (half, half + 2):
+                copy = pltpu.make_async_copy(
+                    halves.at[half, part], blocks.at[chip, part], sems.at[len(copies)]
+                )
+                copy.start()
+                copies.append(copy)
+    for copy in copies:
+        copy.wait()
 
 
 def beside_kernel(first, last, left, right, up, down, beside):
@@ -211,10 +222,18 @@
     out[...] = flat[...].reshape(16, 2, 16, 128).astype(BF)
 
 
-def place(ready, out, start, sem):
-    copy = pltpu.make_async_copy(ready, out.at[:, :, pl.ds(pl.multiple_of(start, 16), 16)], sem)
-    copy.start()
-    copy.wait()
+def place(ready, out, start, sems):
+    rows = pl.ds(pl.multiple_of(start, 16), 16)
+    copies = [
+        pltpu.make_async_copy(
+            ready.at[pl.ds(4 * i, 4)], out.at[pl.ds(4 * i, 4), :, rows], sems.at[i]
+        )
+        for i in range(4)
+    ]
+    for copy in copies:
+        copy.start()
+    for copy in copies:
+        copy.wait()
 
 
 def kept_kernel(pre, taps, mine, theirs, halo, filters, out, flat, ready, sem):
@@ -245,13 +264,21 @@
 
 
 def stages(volume, weights, bias):
-    cols = call(columns_kernel, shaped(32, 128), [], volume, moved=1 << 19)
+    cols = call(
+        columns_kernel,
+        shaped(32, 128),
+        [pltpu.VMEM((16, 2, 32, 128), BF), pltpu.SemaphoreType.DMA((16,))],
+        volume,
+        moved=1 << 18,
+        far_in=(0,),
+    )
     blocks, first, last = call(
         pack_kernel,
         [shaped(4, 34, 16, 128), shaped(32, 128), shaped(32, 128)],
-        [pltpu.VMEM((1024, 128), F32)],
+        [pltpu.VMEM((1024, 128), F32), pltpu.VMEM((2, 34, 16, 128), BF), pltpu.SemaphoreType.DMA((8,))],
         volume,
         moved=1 << 20,
+        far_out=(0,),
     )
     mine = lax.all_to_all(blocks, "ch", split_axis=0, concat_axis=0, tiled=True, axis_index_groups=CORES)
     left = shifts(cols, "sy", True)
@@ -287,8 +314,7 @@
     )
     cost = dict(flops=2 * 288 * 256 * 256, moved=1 << 20)
     flat = pltpu.VMEM((512, 128), F32)
-    ready, sem = pltpu.VMEM((16, 2, 16, 128), BF), pltpu.SemaphoreType.DMA
-    space = pl.BlockSpec(memory_space=pl.ANY)
+    ready, sem = pltpu.VMEM((16, 2, 16, 128), BF), pltpu.SemaphoreType.DMA((4,))
     sent = call(outer_kernel, shaped(16, 2, 16, 128), [flat], pre2, taps2, mine, theirs, halo, other, **cost)
     got = swapped(sent, 2)
     result = call(
@@ -301,10 +327,20 @@
         theirs,
         halo,
         own,
-        place=space,
+        far_out=(0,),
         **cost,
     )
-    return call(unpack_kernel, shaped(16, 2, 32, 128), [sem], got, result, moved=1 << 18, place=space, shared={1: 0})
+    return call(
+        unpack_kernel,
+        shaped(16, 2, 32, 128),
+        [sem],
+        got,
+        result,
+        moved=1 << 18,
+        far_in=(1,),
+        far_out=(0,),
+        shared={1: 0},
+    )
 
 
 def solution(mesh):

time: 64.6 us -> 66.1 us (1.023)
  Pallas kernels: 6.19 us -> 7.69 us
    all_to_all x1, waiting for transfers between devices: 5 us -> 3.29 us  [stages(): lax.all_to_all(blocks, 'ch', split_axis=0, concat_axis=0, tiled=True, axi...]
    ppermute x4, waiting for transfers between devices: 6.34 us -> 7.95 us  [shifts(): lax.ppermute(array, axis, pairs if up else [(j, i) for i, j in pairs])]
    pallas_call x9, Pallas kernels: 6.19 us -> 7.69 us  [call(): pl.pallas_call(kernel, out_shape=out_shapes, in_specs=[far if i in far_in...]
  transfers between devices with their start and end apart: 9 -> 9, of which waited for: 5 -> 5; matrix products, arithmetic and copies ran while one was open for 0% -> 0% of each run, Pallas kernels for 6% -> 8%
where the time goes in v11:
time: 66.1 us; the launch traced here: 65.6 us
  starting transfers between devices  38.3 us (58%)
  waiting for transfers between devices  18.4 us (28%)
  Pallas kernels  7.69 us (12%)
  local copies, waits for them, and re-layouts  1.06 us (2%)
    ppermute x4, starting transfers between devices, shifts(): lax.ppermute(array, axis, pairs if up else [(j, i) for i, j in pairs])  17 us
    ppermute x3, starting transfers between devices, swapped(): return lax.ppermute(array, 'ch', [(d, d ^ t) for d in range(8)])  8.67 us
    ppermute x4, waiting for transfers between devices, shifts(): lax.ppermute(array, axis, pairs if up else [(j, i) for i, j in pairs])  7.95 us
    pallas_call x9, Pallas kernels, call(): pl.pallas_call(kernel, out_shape=out_shapes, in_specs=[far if i in far_in...  7.69 us
    all_to_all x1, starting transfers between devices, stages(): lax.all_to_all(blocks, 'ch', split_axis=0, concat_axis=0, tiled=True, axi...  7.4 us
    ppermute x3, waiting for transfers between devices, swapped(): return lax.ppermute(array, 'ch', [(d, d ^ t) for d in range(8)])  7.13 us
    all_to_all x1, starting transfers between devices, stages(): halo = lax.all_to_all(halo, 'ch', split_axis=0, concat_axis=0, tiled=True)  5.23 us
    all_to_all x1, waiting for transfers between devices, stages(): lax.all_to_all(blocks, 'ch', split_axis=0, concat_axis=0, tiled=True, axi...  3.29 us
  transfers between devices with their start and end apart: 9, of which 5 were waited for; matrix products, arithmetic and copies ran while one was open for 0% of the time, Pallas kernels for 8%

profile of v11, /device:TPU:30, one launch (start us, length us, event | category | flops | bytes accessed | tf_op | source)
XLA Modules:
  0.0 65.6 jit_solution(14287056659735589660)
XLA Ops:
  0.0 0.0 copy-start
  0.0 0.9 %copy-done = bf16[16,2,32,128]{3,2,1,0:T(8,128)(2,1)S(1)} copy-done((bf16[16,2,32,128]{3,2,1,0:T(8,128)(2,1)S(1)}, bf16[16,2,32,128]{3,2,1,0:T(8,128)(2,1)}, u32[]{:S(2)}) %copy-start) | copy-done | bytes 262168
  1.0 1.1 %shard_map.37 = (bf16[4,34,16,128]{3,2,1,0:T(8,128)(2,1)}, bf16[32,128]{1,0:T(8,128)(2,1)S(1)}, bf16[32,128]{1,0:T(8,128)(2,1)S(1)}) custom-call(bf16[16,2,32,128]{3,2,1,0:T(8,128)(2,1)S(1)} %copy-done), custom_call_target="tpu_custom_call" | custom-call | bytes 1048576 | tf_op jit(solution)/shard_map/pallas_call | solution.py:19
  2.0 0.0 copy-start.1
  2.0 7.4 %all-to-all-start = ((bf16[4,34,16,128]{3,2,1,0:T(8,128)(2,1)}), bf16[4,34,16,128]{3,2,1,0:T(8,128)(2,1)S(1)}, u32[]{:S(2)}, u32[]{:S(2)}) async-start(bf16[4,34,16,128]{3,2,1,0:T(8,128)(2,1)} %get-tuple-element.15), calls=%async_computation | async-start | bytes 1114112 | tf_op jit(solution)/shard_map/all_to_all | solution.py:283
  9.4 0.0 copy-done.1
  9.4 0.0 copy-start.3
  9.4 1.7 %shard_map.40 = bf16[32,128]{1,0:T(8,128)(2,1)S(1)} custom-call(bf16[16,2,32,128]{3,2,1,0:T(8,128)(2,1)S(1)} %copy-done.1), custom_call_target="tpu_custom_call" | custom-call | bytes 262144 | tf_op jit(solution)/shard_map/pallas_call | solution.py:19
  11.2 8.5 %collective-permute-start.3 = (bf16[32,128]{1,0:T(8,128)(2,1)S(1)}, bf16[32,128]{1,0:T(8,128)(2,1)S(1)}, u32[]{:S(2)}, u32[]{:S(2)}) collective-permute-start(bf16[32,128]{1,0:T(8,128)(2,1)S(1)} %shard_map.40), channel_id=1, source_target_pairs={{8,0},{16,8},{24,16},{32,24},{40,32},{48,40},{56,48},{9,1},{17,9},... | collective-permute-start | bytes 24584 | tf_op jit(solution)/shard_map/ppermute | solution.py:251
  19.7 1.9 %collective-permute-start.2 = (bf16[32,128]{1,0:T(8,128)(2,1)S(1)}, bf16[32,128]{1,0:T(8,128)(2,1)S(1)}, u32[]{:S(2)}, u32[]{:S(2)}) collective-permute-start(bf16[32,128]{1,0:T(8,128)(2,1)S(1)} %shard_map.40), channel_id=1, source_target_pairs={{0,8},{8,16},{16,24},{24,32},{32,40},{40,48},{48,56},{1,9},{9,17},... | collective-permute-start | bytes 24584 | tf_op jit(solution)/shard_map/ppermute | solution.py:251
  21.6 3.3 %all-to-all-done.mine = bf16[4,34,16,128]{3,2,1,0:T(8,128)(2,1)S(1)} async-done(((bf16[4,34,16,128]{3,2,1,0:T(8,128)(2,1)}), bf16[4,34,16,128]{3,2,1,0:T(8,128)(2,1)S(1)}, u32[]{:S(2)}, u32[]{:S(2)}) %all-to-all-start) | async-done | bytes 557088 | tf_op jit(solution)/shard_map/all_to_all | solution.py:283
  24.9 1.9 %collective-permute-start = (bf16[4,34,16,128]{3,2,1,0:T(8,128)(2,1)S(1)}, bf16[4,34,16,128]{3,2,1,0:T(8,128)(2,1)S(1)}, u32[]{:S(2)}, u32[]{:S(2)}) collective-permute-start(bf16[4,34,16,128]{3,2,1,0:T(8,128)(2,1)S(1)} %all-to-all-done.mine), channel_id=1, source_target_pairs={{0,1},{1,0},{2,3},{3,2},{4,5},{5,4},{6,7},{7,6},{8,9},{9,8},{10,11... | collective-permute-start | bytes 1671176 | tf_op jit(solution)/shard_map/ppermute | solution.py:255
  26.8 0.0 copy-done.3
  26.8 0.0 collective-permute-done.3.right
  26.9 3.2 %collective-permute-done.2.left = bf16[32,128]{1,0:T(8,128)(2,1)S(1)} collective-permute-done((bf16[32,128]{1,0:T(8,128)(2,1)S(1)}, bf16[32,128]{1,0:T(8,128)(2,1)S(1)}, u32[]{:S(2)}, u32[]{:S(2)}) %collective-permute-start.2) | collective-permute-done | bytes 8224 | tf_op jit(solution)/shard_map/ppermute | solution.py:251
  30.0 0.1 shard_map.41
  30.1 4.7 %collective-permute-start.4 = (bf16[48,128]{1,0:T(8,128)(2,1)S(1)}, bf16[48,128]{1,0:T(8,128)(2,1)S(1)}, u32[]{:S(2)}, u32[]{:S(2)}) collective-permute-start(bf16[48,128]{1,0:T(8,128)(2,1)S(1)} %get-tuple-element.21), channel_id=1, source_target_pairs={{0,64},{64,128},{128,192},{192,256},{256,320},{320,384},{384,448},... | collective-permute-start | bytes 36872 | tf_op jit(solution)/shard_map/ppermute | solution.py:251
  34.8 1.9 %collective-permute-start.5 = (bf16[48,128]{1,0:T(8,128)(2,1)S(1)}, bf16[48,128]{1,0:T(8,128)(2,1)S(1)}, u32[]{:S(2)}, u32[]{:S(2)}) collective-permute-start(bf16[48,128]{1,0:T(8,128)(2,1)S(1)} %get-tuple-element.22), channel_id=1, source_target_pairs={{64,0},{128,64},{192,128},{256,192},{320,256},{384,320},{448,384},... | collective-permute-start | bytes 36872 | tf_op jit(solution)/shard_map/ppermute | solution.py:251
  36.8 0.1 copy.8
  36.9 0.0 collective-permute-done.4.above
  36.9 4.8 %collective-permute-done.5.below = bf16[48,128]{1,0:T(8,128)(2,1)S(1)} collective-permute-done((bf16[48,128]{1,0:T(8,128)(2,1)S(1)}, bf16[48,128]{1,0:T(8,128)(2,1)S(1)}, u32[]{:S(2)}, u32[]{:S(2)}) %collective-permute-start.5) | collective-permute-done | bytes 12320 | tf_op jit(solution)/shard_map/ppermute | solution.py:251
  41.6 0.7 %shard_map.42 = bf16[8,48,128]{2,1,0:T(8,128)(2,1)} custom-call(bf16[48,128]{1,0:T(8,128)(2,1)S(1)} %collective-permute-done.4.above, bf16[48,128]{1,0:T(8,128)(2,1)S(1)} %collective-permute-done.5.below, f32[32,128]{1,0:T(8,128)S(1)} %get-tuple-element.23.beside), custom_call_target="tpu_custom_call" | custom-call | bytes 131072 | tf_op jit(solution)/shard_map/pallas_call | solution.py:19
  42.3 0.0 copy-start.2
  42.3 5.2 %all-to-all-start.1 = ((bf16[8,48,128]{2,1,0:T(8,128)(2,1)}), bf16[8,48,128]{2,1,0:T(8,128)(2,1)S(1)}, u32[]{:S(2)}, u32[]{:S(2)}) async-start(bf16[8,48,128]{2,1,0:T(8,128)(2,1)} %shard_map.42), calls=%async_computation.1 | async-start | bytes 196608 | tf_op jit(solution)/shard_map/all_to_all | solution.py:303
  47.6 0.0 copy-done.2
  47.6 3.9 %collective-permute-start.1 = (bf16[448,128]{1,0:T(8,128)(2,1)S(1)}, bf16[448,128]{1,0:T(8,128)(2,1)S(1)}, u32[]{:S(2)}, u32[]{:S(2)}) collective-permute-start(bf16[448,128]{1,0:T(8,128)(2,1)S(1)} %fusion.1.own.filters), channel_id=1, source_target_pairs={{0,2},{1,3},{2,0},{3,1},{4,6},{5,7},{6,4},{7,5},{8,10},{9,11},{10,... | collective-permute-start | bytes 344072 | tf_op jit(solution)/shard_map/ppermute | solution.py:255
  51.5 4.2 %collective-permute-done.1.other.filters = bf16[448,128]{1,0:T(8,128)(2,1)S(1)} collective-permute-done((bf16[448,128]{1,0:T(8,128)(2,1)S(1)}, bf16[448,128]{1,0:T(8,128)(2,1)S(1)}, u32[]{:S(2)}, u32[]{:S(2)}) %collective-permute-start.1) | collective-permute-done | bytes 114720 | tf_op jit(solution)/shard_map/ppermute | solution.py:255
  55.8 0.2 shard_map.38
  55.9 0.0 collective-permute-done.theirs
  55.9 0.9 %shard_map.39 = (f32[16,32,128]{2,1,0:T(8,128)S(1)}, f32[16,32,128]{2,1,0:T(8,128)S(1)}) custom-call(bf16[4,34,16,128]{3,2,1,0:T(8,128)(2,1)S(1)} %all-to-all-done.mine, bf16[4,34,16,128]{3,2,1,0:T(8,128)(2,1)S(1)} %collective-permute-done.theirs, bf16[288,256]{1,0:T(8,128)(2,1)S(1)} %get-tuple-element.16.taps, bf16[288,256]{1,0:T(8,128)(2,1)S(1)} %get-tuple-element.17.taps2.taps), custom_call_target="tpu_custom_call" | custom-call | flops 603979776 | bytes 3145728 | tf_op jit(solution)/shard_map/pallas_call | solution.py:19
  56.8 0.0 all-to-all-done.1.halo
  56.8 0.8 %shard_map.43 = bf16[16,2,16,128]{3,2,1,0:T(8,128)(2,1)S(1)} custom-call(f32[16,32,128]{2,1,0:T(8,128)S(1)} %get-tuple-element.18.pre, bf16[288,256]{1,0:T(8,128)(2,1)S(1)} %get-tuple-element.17.taps2.taps, bf16[4,34,16,128]{3,2,1,0:T(8,128)(2,1)S(1)} %all-to-all-done.mine, bf16[4,34,16,128]{3,2,1,0:T(8,128)(2,1)S(1)} %collective-permute-done.theirs, ...), custom_call_target="tpu_custom_call" | custom-call | flops 37748736 | bytes 1048576 | tf_op jit(solution)/shard_map/pallas_call | solution.py:19
  57.7 2.8 %collective-permute-start.6 = (bf16[16,2,16,128]{3,2,1,0:T(8,128)(2,1)S(1)}, bf16[16,2,16,128]{3,2,1,0:T(8,128)(2,1)S(1)}, u32[]{:S(2)}, u32[]{:S(2)}) collective-permute-start(bf16[16,2,16,128]{3,2,1,0:T(8,128)(2,1)S(1)} %shard_map.43), channel_id=1, source_target_pairs={{0,2},{1,3},{2,0},{3,1},{4,6},{5,7},{6,4},{7,5},{8,10},{9,11},{10,... | collective-permute-start | bytes 393224 | tf_op jit(solution)/shard_map/ppermute | solution.py:255
  60.5 1.5 %shard_map.44.held = bf16[16,2,32,128]{3,2,1,0:T(8,128)(2,1)} custom-call(f32[16,32,128]{2,1,0:T(8,128)S(1)} %get-tuple-element.24.pre, bf16[288,256]{1,0:T(8,128)(2,1)S(1)} %get-tuple-element.16.taps, bf16[4,34,16,128]{3,2,1,0:T(8,128)(2,1)S(1)} %all-to-all-done.mine, bf16[4,34,16,128]{3,2,1,0:T(8,128)(2,1)S(1)} %collective-permute-done.theirs, ...), custom_call_target="tpu_custom_call" | custom-call | flops 37748736 | bytes 1048576 | tf_op jit(solution)/shard_map/pallas_call | solution.py:19
  62.0 2.9 %collective-permute-done.6.got = bf16[16,2,16,128]{3,2,1,0:T(8,128)(2,1)S(1)} collective-permute-done((bf16[16,2,16,128]{3,2,1,0:T(8,128)(2,1)S(1)}, bf16[16,2,16,128]{3,2,1,0:T(8,128)(2,1)S(1)}, u32[]{:S(2)}, u32[]{:S(2)}) %collective-permute-start.6) | collective-permute-done | bytes 131104 | tf_op jit(solution)/shard_map/ppermute | solution.py:255
  64.9 0.7 %shard_map.45 = bf16[16,2,32,128]{3,2,1,0:T(8,128)(2,1)} custom-call(bf16[16,2,16,128]{3,2,1,0:T(8,128)(2,1)S(1)} %collective-permute-done.6.got, bf16[16,2,32,128]{3,2,1,0:T(8,128)(2,1)} %shard_map.44.held), custom_call_target="tpu_custom_call", output_to_operand_aliasing={{}: (1, {})} | custom-call | bytes 262144 | tf_op jit(solution)/shard_map/pallas_call | solution.py:19
  (3 shorter events, 0.0 us)
Async XLA Ops:
  0.0 0.9 %copy-start = (bf16[16,2,32,128]{3,2,1,0:T(8,128)(2,1)S(1)}, bf16[16,2,32,128]{3,2,1,0:T(8,128)(2,1)}, u32[]{:S(2)}) copy-start(bf16[16,2,32,128]{3,2,1,0:T(8,128)(2,1)} %vol.3) | copy-start | bytes 786436
  2.0 7.4 %copy-start.1 = (bf16[16,2,32,128]{3,2,1,0:T(8,128)(2,1)S(1)}, bf16[16,2,32,128]{3,2,1,0:T(8,128)(2,1)}, u32[]{:S(2)}) copy-start(bf16[16,2,32,128]{3,2,1,0:T(8,128)(2,1)} %vol.3) | copy-start | bytes 786436
  2.0 22.9 %all-to-all-start = ((bf16[4,34,16,128]{3,2,1,0:T(8,128)(2,1)}), bf16[4,34,16,128]{3,2,1,0:T(8,128)(2,1)S(1)}, u32[]{:S(2)}, u32[]{:S(2)}) async-start(bf16[4,34,16,128]{3,2,1,0:T(8,128)(2,1)} %get-tuple-element.15), calls=%async_computation | async-start | bytes 1114112 | tf_op jit(solution)/shard_map/all_to_all | solution.py:283
  9.4 17.4 %copy-start.3 = (f32[16]{0:T(128)S(1)}, f32[16]{0:T(128)}, u32[]{:S(2)}) copy-start(f32[16]{0:T(128)} %param.5) | copy-start | bytes 196
  11.2 15.7 %collective-permute-start.3 = (bf16[32,128]{1,0:T(8,128)(2,1)S(1)}, bf16[32,128]{1,0:T(8,128)(2,1)S(1)}, u32[]{:S(2)}, u32[]{:S(2)}) collective-permute-start(bf16[32,128]{1,0:T(8,128)(2,1)S(1)} %shard_map.40), channel_id=1, source_target_pairs={{8,0},{16,8},{24,16},{32,24},{40,32},{48,40},{56,48},{9,1},{17,9},... | collective-permute-start | bytes 24584 | tf_op jit(solution)/shard_map/ppermute | solution.py:251
  19.7 10.4 %collective-permute-start.2 = (bf16[32,128]{1,0:T(8,128)(2,1)S(1)}, bf16[32,128]{1,0:T(8,128)(2,1)S(1)}, u32[]{:S(2)}, u32[]{:S(2)}) collective-permute-start(bf16[32,128]{1,0:T(8,128)(2,1)S(1)} %shard_map.40), channel_id=1, source_target_pairs={{0,8},{8,16},{16,24},{24,32},{32,40},{40,48},{48,56},{1,9},{9,17},... | collective-permute-start | bytes 24584 | tf_op jit(solution)/shard_map/ppermute | solution.py:251
  24.9 31.0 %collective-permute-start = (bf16[4,34,16,128]{3,2,1,0:T(8,128)(2,1)S(1)}, bf16[4,34,16,128]{3,2,1,0:T(8,128)(2,1)S(1)}, u32[]{:S(2)}, u32[]{:S(2)}) collective-permute-start(bf16[4,34,16,128]{3,2,1,0:T(8,128)(2,1)S(1)} %all-to-all-done.mine), channel_id=1, source_target_pairs={{0,1},{1,0},{2,3},{3,2},{4,5},{5,4},{6,7},{7,6},{8,9},{9,8},{10,11... | collective-permute-start | bytes 1671176 | tf_op jit(solution)/shard_map/ppermute | solution.py:255
  30.1 6.7 %collective-permute-start.4 = (bf16[48,128]{1,0:T(8,128)(2,1)S(1)}, bf16[48,128]{1,0:T(8,128)(2,1)S(1)}, u32[]{:S(2)}, u32[]{:S(2)}) collective-permute-start(bf16[48,128]{1,0:T(8,128)(2,1)S(1)} %get-tuple-element.21), channel_id=1, source_target_pairs={{0,64},{64,128},{128,192},{192,256},{256,320},{320,384},{384,448},... | collective-permute-start | bytes 36872 | tf_op jit(solution)/shard_map/ppermute | solution.py:251
  34.8 6.8 %collective-permute-start.5 = (bf16[48,128]{1,0:T(8,128)(2,1)S(1)}, bf16[48,128]{1,0:T(8,128)(2,1)S(1)}, u32[]{:S(2)}, u32[]{:S(2)}) collective-permute-start(bf16[48,128]{1,0:T(8,128)(2,1)S(1)} %get-tuple-element.22), channel_id=1, source_target_pairs={{64,0},{128,64},{192,128},{256,192},{320,256},{384,320},{448,384},... | collective-permute-start | bytes 36872 | tf_op jit(solution)/shard_map/ppermute | solution.py:251
  42.3 5.2 %copy-start.2 = (bf16[16,128,3,3,3]{1,0,4,3,2:T(8,128)(2,1)S(1)}, bf16[16,128,3,3,3]{1,0,4,3,2:T(8,128)(2,1)}, u32[]{:S(2)}) copy-start(bf16[16,128,3,3,3]{1,0,4,3,2:T(8,128)(2,1)} %param.4) | copy-start | bytes 331780
  42.3 14.5 %all-to-all-start.1 = ((bf16[8,48,128]{2,1,0:T(8,128)(2,1)}), bf16[8,48,128]{2,1,0:T(8,128)(2,1)S(1)}, u32[]{:S(2)}, u32[]{:S(2)}) async-start(bf16[8,48,128]{2,1,0:T(8,128)(2,1)} %shard_map.42), calls=%async_computation.1 | async-start | bytes 196608 | tf_op jit(solution)/shard_map/all_to_all | solution.py:303
  47.6 8.2 %collective-permute-start.1 = (bf16[448,128]{1,0:T(8,128)(2,1)S(1)}, bf16[448,128]{1,0:T(8,128)(2,1)S(1)}, u32[]{:S(2)}, u32[]{:S(2)}) collective-permute-start(bf16[448,128]{1,0:T(8,128)(2,1)S(1)} %fusion.1.own.filters), channel_id=1, source_target_pairs={{0,2},{1,3},{2,0},{3,1},{4,6},{5,7},{6,4},{7,5},{8,10},{9,11},{10,... | collective-permute-start | bytes 344072 | tf_op jit(solution)/shard_map/ppermute | solution.py:255
  57.7 7.3 %collective-permute-start.6 = (bf16[16,2,16,128]{3,2,1,0:T(8,128)(2,1)S(1)}, bf16[16,2,16,128]{3,2,1,0:T(8,128)(2,1)S(1)}, u32[]{:S(2)}, u32[]{:S(2)}) collective-permute-start(bf16[16,2,16,128]{3,2,1,0:T(8,128)(2,1)S(1)} %shard_map.43), channel_id=1, source_target_pairs={{0,2},{1,3},{2,0},{3,1},{4,6},{5,7},{6,4},{7,5},{8,10},{9,11},{10,... | collective-permute-start | bytes 393224 | tf_op jit(solution)/shard_map/ppermute | solution.py:255

commit v12 on v9

--- a/solution.py
+++ b/solution.py
@@ -124,18 +124,36 @@
     return total[32:64] + (before + after)
 
 
-def inner_kernel(mine, theirs, taps, taps2, pre, pre2, sums):
+def offset_of(filters):
+    parts = filters[pl.ds(432, 16)].astype(F32)
+    offset = (parts[:, 0:1] + parts[:, 1:2]) + parts[:, 2:3]
+    return jnp.concatenate([offset, offset], axis=0)
+
+
+def activated(total):
+    return jnp.where(total >= 0, total, 0.3 * total)
+
+
+def inner_kernel(mine, theirs, taps, taps2, other, pre, pre2, early, sums):
     half = half_of()
     lane = lanes_of((32, 128))
 
     def row_of(row):
         return jnp.concatenate(
-            [held[chip, z * 17 + row + half] for z in range(2) for chip in range(4) for held in (mine, theirs)],
+            [held[chip, z * 17 + row] for z in range(2) for chip in range(4) for held in (mine, theirs)],
             axis=0,
         )
 
+    near = row_of(16 * (1 - half))
+    for weights, to in ((taps, pre), (taps2, pre2)):
+        ends = [
+            aligned(jnp.dot(weights[pl.ds(b * 96, 96)], near, preferred_element_type=F32), lane) for b in (0, 2)
+        ]
+        to[0] = jnp.where(half == 1, ends[0], 0.0)
+        to[15] = jnp.where(half == 0, ends[1], 0.0)
+    offset = offset_of(other)
     for p in range(8):
-        pair = jnp.concatenate([row_of(2 * p), row_of(2 * p + 1)], axis=1)
+        pair = jnp.concatenate([row_of(2 * p + half), row_of(2 * p + 1 + half)], axis=1)
         for t, (weights, to) in enumerate(((taps, pre), (taps2, pre2))):
             got = jnp.dot(weights[...], pair, preferred_element_type=F32)
             for h in range(2):
@@ -147,18 +165,22 @@
                     if not (b == 0 or (b == 1 and row == 0)):
                         part = part + sums[t, row]
                     if b == 2 or (b == 1 and row == 15):
-                        to[row] = aligned(part, lane)
+                        total = aligned(part, lane)
+                        if row in (0, 15):
+                            total = total + to[row]
+                        to[row] = total
+                        if t == 1:
+                            done = activated(total + offset).astype(BF)
+                            for z in range(2):
+                                early[z * 16 + row] = done[z * 16 : z * 16 + 16]
                     else:
                         sums[t, row] = part
 
 
-def outer_kernel(pre, taps, mine, theirs, halo, filters, out, flat):
+def ends_of(taps, halo):
     me = lax.axis_index("ch")
-    half, core = half_of(), lax.rem(me, 2)
-    parts = filters[pl.ds(432, 16)].astype(F32)
-    offset = (parts[:, 0:1] + parts[:, 1:2]) + parts[:, 2:3]
-    offset = jnp.concatenate([offset, offset], axis=0)
-    sources = [2 * chip + (core ^ t) for chip in range(4) for t in range(2)]
+    half = half_of()
+    sources = [2 * chip + (lax.rem(me, 2) ^ t) for chip in range(4) for t in range(2)]
     lane24 = lanes_of((24, 128))
     total = [[jnp.zeros((24, 128), F32) for _ in range(2)] for _ in range(2)]
     for j, source in enumerate(sources):
@@ -182,21 +204,38 @@
     lane = lanes_of((32, 128))
     far = jnp.concatenate(
         [halo[source, pl.ds(z * 16, 16)] for z in range(2) for source in sources], axis=0
-    ).astype(F32)
-    near = jnp.concatenate(
-        [
-            held[chip, z * 17 + 16 * (1 - half)]
-            for z in range(2)
-            for chip in range(4)
-            for held in (mine, theirs)
-        ],
-        axis=0,
-    ).astype(F32)
-    first_half = half == 0
-    above = jnp.where(first_half, far, near).astype(BF)
-    below = jnp.where(first_half, near, far).astype(BF)
-    above = aligned(jnp.dot(taps[pl.ds(0, 96)], above, preferred_element_type=F32), lane)
-    below = aligned(jnp.dot(taps[pl.ds(192, 96)], below, preferred_element_type=F32), lane)
+    )
+    far = [aligned(jnp.dot(taps[pl.ds(b * 96, 96)], far, preferred_element_type=F32), lane) for b in (0, 2)]
+    return jnp.where(half == 0, far[0], 0.0), jnp.where(half == 1, far[1], 0.0), before, after
+
+
+def patch_kernel(pre, taps, halo, filters, patch):
+    half = half_of()
+    above, below, before, after = ends_of(taps, halo)
+    offset = offset_of(filters)
+    lane = lanes_of((32, 128))
+    sides = jnp.zeros((32, 128), F32)
+    end = jnp.zeros((32, 128), F32)
+    for row in range(16):
+        total = pre[row] + offset
+        if row == 0:
+            total = total + above
+        if row == 15:
+            total = total + below
+        first = total[:, 0:1] + before[:, row : row + 1]
+        last = total[:, 127:128] + after[:, 24 + row : 25 + row]
+        sides = jnp.where(lane == row, first, sides)
+        sides = jnp.where(lane == 64 + row, last, sides)
+        if row in (0, 15):
+            end = jnp.where(half == (row != 0), total, end)
+    patch[pl.ds(0, 32)] = activated(end).astype(BF)
+    patch[pl.ds(32, 32)] = activated(sides).astype(BF)
+
+
+def outer_kernel(pre, taps, halo, filters, out, flat):
+    above, below, before, after = ends_of(taps, halo)
+    offset = offset_of(filters)
+    lane = lanes_of((32, 128))
     for row in range(16):
         total = pre[row] + offset
         if row == 0:
@@ -205,7 +244,7 @@
             total = total + below
         total = total + jnp.where(lane == 0, before[:, row : row + 1], 0.0)
         total = total + jnp.where(lane == 127, after[:, 24 + row : 25 + row], 0.0)
-        total = jnp.where(total >= 0, total, 0.3 * total)
+        total = activated(total)
         for z in range(2):
             flat[pl.ds(z * 16 + row, 16, stride=32), :] = total[z * 16 : z * 16 + 16]
     out[...] = flat[...].reshape(16, 2, 16, 128).astype(BF)
@@ -217,13 +256,26 @@
     copy.wait()
 
 
-def kept_kernel(pre, taps, mine, theirs, halo, filters, out, flat, ready, sem):
-    outer_kernel(pre, taps, mine, theirs, halo, filters, ready, flat)
+def kept_kernel(pre, taps, halo, filters, out, flat, ready, sem):
+    outer_kernel(pre, taps, halo, filters, ready, flat)
     place(ready, out, 16 * half_of(), sem)
 
 
-def unpack_kernel(got, held, out, sem):
-    place(got, out, 16 * (1 - half_of()), sem)
+def unpack_kernel(got, patch, held, out, flat, ready, sem):
+    half = half_of()
+    lane = lanes_of((16, 128))
+    for z in range(2):
+        end = patch[pl.ds(z * 16, 16)].astype(F32)
+        sides = patch[pl.ds(32 + z * 16, 16)].astype(F32)
+        for row in range(16):
+            tile = got[z * 16 + row].astype(F32)
+            if row in (0, 15):
+                tile = jnp.where(half == (row == 0), end, tile)
+            tile = jnp.where(lane == 0, sides[:, row : row + 1], tile)
+            tile = jnp.where(lane == 127, sides[:, 64 + row : 65 + row], tile)
+            flat[pl.ds(z * 16 + row, 16, stride=32), :] = tile
+    ready[...] = flat[...].reshape(16, 2, 16, 128).astype(BF)
+    place(ready, out, 16 * (1 - half), sem)
 
 
 def shifts(array, axis, up=True):
@@ -274,14 +326,15 @@
     taps, taps2 = call(taps_kernel, [shaped(288, 256)] * 2, [], own, other, moved=1 << 19)
     halo = call(halo_kernel, shaped(8, 48, 128), [pltpu.VMEM((40, 128), F32)], above, below, beside, moved=1 << 17)
     halo = lax.all_to_all(halo, "ch", split_axis=0, concat_axis=0, tiled=True)
-    pre, pre2 = call(
+    pre, pre2, early = call(
         inner_kernel,
-        [shaped(16, 32, 128, dtype=F32)] * 2,
+        [shaped(16, 32, 128, dtype=F32)] * 2 + [shaped(32, 16, 128)],
         [pltpu.VMEM((2, 16, 96, 128), F32)],
         mine,
         theirs,
         taps,
         taps2,
+        other,
         flops=2 * 576 * 256 * 2048,
         moved=3 << 20,
     )
@@ -289,22 +342,21 @@
     flat = pltpu.VMEM((512, 128), F32)
     ready, sem = pltpu.VMEM((16, 2, 16, 128), BF), pltpu.SemaphoreType.DMA
     space = pl.BlockSpec(memory_space=pl.ANY)
-    sent = call(outer_kernel, shaped(16, 2, 16, 128), [flat], pre2, taps2, mine, theirs, halo, other, **cost)
-    got = swapped(sent, 2)
-    result = call(
-        kept_kernel,
+    got = swapped(early, 2)
+    patch = call(patch_kernel, shaped(64, 128), [], pre2, taps2, halo, other, **cost)
+    patch = swapped(patch, 2)
+    result = call(kept_kernel, shaped(16, 2, 32, 128), [flat, ready, sem], pre, taps, halo, own, place=space, **cost)
+    return call(
+        unpack_kernel,
         shaped(16, 2, 32, 128),
         [flat, ready, sem],
-        pre,
-        taps,
-        mine,
-        theirs,
-        halo,
-        own,
+        got,
+        patch,
+        result,
+        moved=1 << 18,
         place=space,
-        **cost,
-    )
-    return call(unpack_kernel, shaped(16, 2, 32, 128), [sem], got, result, moved=1 << 18, place=space, shared={1: 0})
+        shared={2: 0},
+    )
 
 
 def solution(mesh):

time: 64.6 us -> 76 us (1.18)
  the two profiles are of different devices: /device:TPU:30 before, /device:TPU:28 now
where the time goes in v12:
time: 76 us; the launch traced here: 75.6 us
  starting transfers between devices  31.4 us (41%)
  blocking collectives  22.4 us (29%)
  waiting for transfers between devices  14.7 us (19%)
  Pallas kernels  5.81 us (8%)
  local copies, waits for them, and re-layouts  1.06 us (1%)
    all_to_all x1, blocking collectives, stages(): lax.all_to_all(blocks, 'ch', split_axis=0, concat_axis=0, tiled=True, axi...  22.4 us
    ppermute x4, starting transfers between devices, shifts(): lax.ppermute(array, axis, pairs if up else [(j, i) for i, j in pairs])  17.3 us
    ppermute x4, waiting for transfers between devices, shifts(): lax.ppermute(array, axis, pairs if up else [(j, i) for i, j in pairs])  11.9 us
    ppermute x4, starting transfers between devices, swapped(): return lax.ppermute(array, 'ch', [(d, d ^ t) for d in range(8)])  10.8 us
    pallas_call x9, Pallas kernels, call(): pl.pallas_call(kernel, out_shape=out_shapes, in_specs=in_specs, out_specs...  5.81 us
    all_to_all x1, starting transfers between devices, stages(): halo = lax.all_to_all(halo, 'ch', split_axis=0, concat_axis=0, tiled=True)  3.36 us
  transfers between devices with their start and end apart: 9, of which 4 were waited for; matrix products, arithmetic and copies ran while one was open for 0% of the time, Pallas kernels for 6%

profile of v12, /device:TPU:28, one launch (start us, length us, event | category | flops | bytes accessed | tf_op | source)
XLA Modules:
  0.0 75.6 jit_solution(4106460597311458189)
XLA Ops:
  0.0 0.0 copy-start
  0.0 0.9 %copy-done = bf16[16,2,32,128]{3,2,1,0:T(8,128)(2,1)S(1)} copy-done((bf16[16,2,32,128]{3,2,1,0:T(8,128)(2,1)S(1)}, bf16[16,2,32,128]{3,2,1,0:T(8,128)(2,1)}, u32[]{:S(2)}) %copy-start) | copy-done | bytes 262168
  1.0 0.3 shard_map.37
  1.3 0.0 copy-start.3
  1.3 0.0 copy-start.2
  1.3 0.0 copy-start.1
  1.3 22.4 %all_to_all.10.mine = bf16[4,34,16,128]{3,2,1,0:T(8,128)(2,1)S(1)} all-to-all(bf16[4,34,16,128]{3,2,1,0:T(8,128)(2,1)S(1)} %get-tuple-element.16), channel_id=1, replica_groups={{0,2,4,6},{1,3,5,7},{8,10,12,14},{9,11,13,15},{16,18,20,22},{17,19,21,2..., dimensions={0} | all-to-all | bytes 1114112 | tf_op jit(solution)/shard_map/all_to_all | solution.py:308
  23.7 1.9 %collective-permute-start = (bf16[4,34,16,128]{3,2,1,0:T(8,128)(2,1)S(1)}, bf16[4,34,16,128]{3,2,1,0:T(8,128)(2,1)S(1)}, u32[]{:S(2)}, u32[]{:S(2)}) collective-permute-start(bf16[4,34,16,128]{3,2,1,0:T(8,128)(2,1)S(1)} %all_to_all.10.mine), channel_id=1, source_target_pairs={{0,1},{1,0},{2,3},{3,2},{4,5},{5,4},{6,7},{7,6},{8,9},{9,8},{10,11... | collective-permute-start | bytes 1671176 | tf_op jit(solution)/shard_map/ppermute | solution.py:288
  25.6 0.0 copy-done.3
  25.7 0.1 copy.8
  25.8 0.0 copy-done.2
  25.8 2.4 %collective-permute-start.1 = (bf16[448,128]{1,0:T(8,128)(2,1)S(1)}, bf16[448,128]{1,0:T(8,128)(2,1)S(1)}, u32[]{:S(2)}, u32[]{:S(2)}) collective-permute-start(bf16[448,128]{1,0:T(8,128)(2,1)S(1)} %fusion.1.own.filters), channel_id=1, source_target_pairs={{0,2},{1,3},{2,0},{3,1},{4,6},{5,7},{6,4},{7,5},{8,10},{9,11},{10,... | collective-permute-start | bytes 344072 | tf_op jit(solution)/shard_map/ppermute | solution.py:288
  28.2 0.0 copy-done.1
  28.2 0.2 shard_map.40
  28.4 8.2 %collective-permute-start.3 = (bf16[32,128]{1,0:T(8,128)(2,1)S(1)}, bf16[32,128]{1,0:T(8,128)(2,1)S(1)}, u32[]{:S(2)}, u32[]{:S(2)}) collective-permute-start(bf16[32,128]{1,0:T(8,128)(2,1)S(1)} %shard_map.40), channel_id=1, source_target_pairs={{0,8},{8,16},{16,24},{24,32},{32,40},{40,48},{48,56},{1,9},{9,17},... | collective-permute-start | bytes 24584 | tf_op jit(solution)/shard_map/ppermute | solution.py:284
  36.6 2.4 %collective-permute-start.4 = (bf16[32,128]{1,0:T(8,128)(2,1)S(1)}, bf16[32,128]{1,0:T(8,128)(2,1)S(1)}, u32[]{:S(2)}, u32[]{:S(2)}) collective-permute-start(bf16[32,128]{1,0:T(8,128)(2,1)S(1)} %shard_map.40), channel_id=1, source_target_pairs={{8,0},{16,8},{24,16},{32,24},{40,32},{48,40},{56,48},{9,1},{17,9},... | collective-permute-start | bytes 24584 | tf_op jit(solution)/shard_map/ppermute | solution.py:284
  39.0 0.0 collective-permute-done.3.left
  39.1 7.0 %collective-permute-done.4.right = bf16[32,128]{1,0:T(8,128)(2,1)S(1)} collective-permute-done((bf16[32,128]{1,0:T(8,128)(2,1)S(1)}, bf16[32,128]{1,0:T(8,128)(2,1)S(1)}, u32[]{:S(2)}, u32[]{:S(2)}) %collective-permute-start.4) | collective-permute-done | bytes 8224 | tf_op jit(solution)/shard_map/ppermute | solution.py:284
  46.1 0.1 shard_map.41
  46.1 4.7 %collective-permute-start.5 = (bf16[48,128]{1,0:T(8,128)(2,1)S(1)}, bf16[48,128]{1,0:T(8,128)(2,1)S(1)}, u32[]{:S(2)}, u32[]{:S(2)}) collective-permute-start(bf16[48,128]{1,0:T(8,128)(2,1)S(1)} %get-tuple-element.23), channel_id=1, source_target_pairs={{0,64},{64,128},{128,192},{192,256},{256,320},{320,384},{384,448},... | collective-permute-start | bytes 36872 | tf_op jit(solution)/shard_map/ppermute | solution.py:284
  50.8 1.9 %collective-permute-start.6 = (bf16[48,128]{1,0:T(8,128)(2,1)S(1)}, bf16[48,128]{1,0:T(8,128)(2,1)S(1)}, u32[]{:S(2)}, u32[]{:S(2)}) collective-permute-start(bf16[48,128]{1,0:T(8,128)(2,1)S(1)} %get-tuple-element.24), channel_id=1, source_target_pairs={{64,0},{128,64},{192,128},{256,192},{320,256},{384,320},{448,384},... | collective-permute-start | bytes 36872 | tf_op jit(solution)/shard_map/ppermute | solution.py:284
  52.8 0.0 collective-permute-done.5.above
  52.8 4.9 %collective-permute-done.6.below = bf16[48,128]{1,0:T(8,128)(2,1)S(1)} collective-permute-done((bf16[48,128]{1,0:T(8,128)(2,1)S(1)}, bf16[48,128]{1,0:T(8,128)(2,1)S(1)}, u32[]{:S(2)}, u32[]{:S(2)}) %collective-permute-start.6) | collective-permute-done | bytes 12320 | tf_op jit(solution)/shard_map/ppermute | solution.py:284
  57.6 0.7 shard_map.42
  58.4 3.4 %all-to-all-start.1 = ((bf16[8,48,128]{2,1,0:T(8,128)(2,1)}), bf16[8,48,128]{2,1,0:T(8,128)(2,1)S(1)}, u32[]{:S(2)}, u32[]{:S(2)}) async-start(bf16[8,48,128]{2,1,0:T(8,128)(2,1)} %shard_map.42), calls=%async_computation.1 | async-start | bytes 196608 | tf_op jit(solution)/shard_map/all_to_all | solution.py:328
  61.7 0.0 collective-permute-done.1.other.filters
  61.7 0.2 shard_map.38
  61.9 0.0 collective-permute-done.theirs
  61.9 0.9 %shard_map.39 = (f32[16,32,128]{2,1,0:T(8,128)S(1)}, f32[16,32,128]{2,1,0:T(8,128)S(1)}, bf16[32,16,128]{2,1,0:T(8,128)(2,1)S(1)}) custom-call(bf16[4,34,16,128]{3,2,1,0:T(8,128)(2,1)S(1)} %all_to_all.10.mine, bf16[4,34,16,128]{3,2,1,0:T(8,128)(2,1)S(1)} %collective-permute-done.theirs, bf16[288,256]{1,0:T(8,128)(2,1)S(1)} %get-tuple-element.17.taps, ...), custom_call_target="tpu_custom_call" | custom-call | flops 603979776 | bytes 3145728 | tf_op jit(solution)/shard_map/pallas_call | solution.py:21
  62.9 3.8 %collective-permute-start.2 = (bf16[32,16,128]{2,1,0:T(8,128)(2,1)S(1)}, bf16[32,16,128]{2,1,0:T(8,128)(2,1)S(1)}, u32[]{:S(2)}, u32[]{:S(2)}) collective-permute-start(bf16[32,16,128]{2,1,0:T(8,128)(2,1)S(1)} %get-tuple-element.19), channel_id=1, source_target_pairs={{0,2},{1,3},{2,0},{3,1},{4,6},{5,7},{6,4},{7,5},{8,10},{9,11},{10,... | collective-permute-start | bytes 393224 | tf_op jit(solution)/shard_map/ppermute | solution.py:288
  66.7 1.3 %all-to-all-done.1.halo = bf16[8,48,128]{2,1,0:T(8,128)(2,1)S(1)} async-done(((bf16[8,48,128]{2,1,0:T(8,128)(2,1)}), bf16[8,48,128]{2,1,0:T(8,128)(2,1)S(1)}, u32[]{:S(2)}, u32[]{:S(2)}) %all-to-all-start.1) | async-done | bytes 98336 | tf_op jit(solution)/shard_map/all_to_all | solution.py:328
  68.1 0.9 %shard_map.43 = bf16[64,128]{1,0:T(8,128)(2,1)S(1)} custom-call(f32[16,32,128]{2,1,0:T(8,128)S(1)} %get-tuple-element.20.pre, bf16[288,256]{1,0:T(8,128)(2,1)S(1)} %get-tuple-element.18.taps2.taps, bf16[8,48,128]{2,1,0:T(8,128)(2,1)S(1)} %all-to-all-done.1.halo, bf16[448,128]{1,0:T(8,128)(2,1)S(1)} %collective-permute-done.1.other.filters), custom_call_target="tpu_custom_call" | custom-call | flops 37748736 | bytes 1048576 | tf_op jit(solution)/shard_map/pallas_call | solution.py:21
  69.0 2.6 %collective-permute-start.7 = (bf16[64,128]{1,0:T(8,128)(2,1)S(1)}, bf16[64,128]{1,0:T(8,128)(2,1)S(1)}, u32[]{:S(2)}, u32[]{:S(2)}) collective-permute-start(bf16[64,128]{1,0:T(8,128)(2,1)S(1)} %shard_map.43), channel_id=1, source_target_pairs={{0,2},{1,3},{2,0},{3,1},{4,6},{5,7},{6,4},{7,5},{8,10},{9,11},{10,... | collective-permute-start | bytes 49160 | tf_op jit(solution)/shard_map/ppermute | solution.py:288
  71.6 1.5 %shard_map.44.held = bf16[16,2,32,128]{3,2,1,0:T(8,128)(2,1)} custom-call(f32[16,32,128]{2,1,0:T(8,128)S(1)} %get-tuple-element.26.pre, bf16[288,256]{1,0:T(8,128)(2,1)S(1)} %get-tuple-element.17.taps, bf16[8,48,128]{2,1,0:T(8,128)(2,1)S(1)} %all-to-all-done.1.halo, bf16[448,128]{1,0:T(8,128)(2,1)S(1)} %fusion.1.own.filters), custom_call_target="tpu_custom_call" | custom-call | flops 37748736 | bytes 1048576 | tf_op jit(solution)/shard_map/pallas_call | solution.py:21
  73.1 1.5 %collective-permute-done.7.patch = bf16[64,128]{1,0:T(8,128)(2,1)S(1)} collective-permute-done((bf16[64,128]{1,0:T(8,128)(2,1)S(1)}, bf16[64,128]{1,0:T(8,128)(2,1)S(1)}, u32[]{:S(2)}, u32[]{:S(2)}) %collective-permute-start.7) | collective-permute-done | bytes 16416 | tf_op jit(solution)/shard_map/ppermute | solution.py:288
  74.6 0.0 collective-permute-done.2.got
  74.6 1.0 %shard_map.45 = bf16[16,2,32,128]{3,2,1,0:T(8,128)(2,1)} custom-call(bf16[32,16,128]{2,1,0:T(8,128)(2,1)S(1)} %collective-permute-done.2.got, bf16[64,128]{1,0:T(8,128)(2,1)S(1)} %collective-permute-done.7.patch, bf16[16,2,32,128]{3,2,1,0:T(8,128)(2,1)} %shard_map.44.held), custom_call_target="tpu_custom_call", output_to_operand_aliasing={{}: (2, {})} | custom-call | bytes 262144 | tf_op jit(solution)/shard_map/pallas_call | solution.py:21
  (3 shorter events, 0.0 us)
Async XLA Ops:
  0.0 0.9 %copy-start = (bf16[16,2,32,128]{3,2,1,0:T(8,128)(2,1)S(1)}, bf16[16,2,32,128]{3,2,1,0:T(8,128)(2,1)}, u32[]{:S(2)}) copy-start(bf16[16,2,32,128]{3,2,1,0:T(8,128)(2,1)} %vol.3) | copy-start | bytes 786436
  1.3 24.3 %copy-start.3 = (f32[16]{0:T(128)S(1)}, f32[16]{0:T(128)}, u32[]{:S(2)}) copy-start(f32[16]{0:T(128)} %param.5) | copy-start | bytes 196
  1.3 24.5 %copy-start.2 = (bf16[16,128,3,3,3]{1,0,4,3,2:T(8,128)(2,1)S(1)}, bf16[16,128,3,3,3]{1,0,4,3,2:T(8,128)(2,1)}, u32[]{:S(2)}) copy-start(bf16[16,128,3,3,3]{1,0,4,3,2:T(8,128)(2,1)} %param.4) | copy-start | bytes 331780
  1.3 26.9 %copy-start.1 = (bf16[16,2,32,128]{3,2,1,0:T(8,128)(2,1)S(1)}, bf16[16,2,32,128]{3,2,1,0:T(8,128)(2,1)}, u32[]{:S(2)}) copy-start(bf16[16,2,32,128]{3,2,1,0:T(8,128)(2,1)} %vol.3) | copy-start | bytes 786436
  23.7 38.2 %collective-permute-start = (bf16[4,34,16,128]{3,2,1,0:T(8,128)(2,1)S(1)}, bf16[4,34,16,128]{3,2,1,0:T(8,128)(2,1)S(1)}, u32[]{:S(2)}, u32[]{:S(2)}) collective-permute-start(bf16[4,34,16,128]{3,2,1,0:T(8,128)(2,1)S(1)} %all_to_all.10.mine), channel_id=1, source_target_pairs={{0,1},{1,0},{2,3},{3,2},{4,5},{5,4},{6,7},{7,6},{8,9},{9,8},{10,11... | collective-permute-start | bytes 1671176 | tf_op jit(solution)/shard_map/ppermute | solution.py:288
  25.8 36.0 %collective-permute-start.1 = (bf16[448,128]{1,0:T(8,128)(2,1)S(1)}, bf16[448,128]{1,0:T(8,128)(2,1)S(1)}, u32[]{:S(2)}, u32[]{:S(2)}) collective-permute-start(bf16[448,128]{1,0:T(8,128)(2,1)S(1)} %fusion.1.own.filters), channel_id=1, source_target_pairs={{0,2},{1,3},{2,0},{3,1},{4,6},{5,7},{6,4},{7,5},{8,10},{9,11},{10,... | collective-permute-start | bytes 344072 | tf_op jit(solution)/shard_map/ppermute | solution.py:288
  28.4 10.7 %collective-permute-start.3 = (bf16[32,128]{1,0:T(8,128)(2,1)S(1)}, bf16[32,128]{1,0:T(8,128)(2,1)S(1)}, u32[]{:S(2)}, u32[]{:S(2)}) collective-permute-start(bf16[32,128]{1,0:T(8,128)(2,1)S(1)} %shard_map.40), channel_id=1, source_target_pairs={{0,8},{8,16},{16,24},{24,32},{32,40},{40,48},{48,56},{1,9},{9,17},... | collective-permute-start | bytes 24584 | tf_op jit(solution)/shard_map/ppermute | solution.py:284
  36.6 9.5 %collective-permute-start.4 = (bf16[32,128]{1,0:T(8,128)(2,1)S(1)}, bf16[32,128]{1,0:T(8,128)(2,1)S(1)}, u32[]{:S(2)}, u32[]{:S(2)}) collective-permute-start(bf16[32,128]{1,0:T(8,128)(2,1)S(1)} %shard_map.40), channel_id=1, source_target_pairs={{8,0},{16,8},{24,16},{32,24},{40,32},{48,40},{56,48},{9,1},{17,9},... | collective-permute-start | bytes 24584 | tf_op jit(solution)/shard_map/ppermute | solution.py:284
  46.1 6.6 %collective-permute-start.5 = (bf16[48,128]{1,0:T(8,128)(2,1)S(1)}, bf16[48,128]{1,0:T(8,128)(2,1)S(1)}, u32[]{:S(2)}, u32[]{:S(2)}) collective-permute-start(bf16[48,128]{1,0:T(8,128)(2,1)S(1)} %get-tuple-element.23), channel_id=1, source_target_pairs={{0,64},{64,128},{128,192},{192,256},{256,320},{320,384},{384,448},... | collective-permute-start | bytes 36872 | tf_op jit(solution)/shard_map/ppermute | solution.py:284
  50.8 6.8 %collective-permute-start.6 = (bf16[48,128]{1,0:T(8,128)(2,1)S(1)}, bf16[48,128]{1,0:T(8,128)(2,1)S(1)}, u32[]{:S(2)}, u32[]{:S(2)}) collective-permute-start(bf16[48,128]{1,0:T(8,128)(2,1)S(1)} %get-tuple-element.24), channel_id=1, source_target_pairs={{64,0},{128,64},{192,128},{256,192},{320,256},{384,320},{448,384},... | collective-permute-start | bytes 36872 | tf_op jit(solution)/shard_map/ppermute | solution.py:284
  58.4 9.7 %all-to-all-start.1 = ((bf16[8,48,128]{2,1,0:T(8,128)(2,1)}), bf16[8,48,128]{2,1,0:T(8,128)(2,1)S(1)}, u32[]{:S(2)}, u32[]{:S(2)}) async-start(bf16[8,48,128]{2,1,0:T(8,128)(2,1)} %shard_map.42), calls=%async_computation.1 | async-start | bytes 196608 | tf_op jit(solution)/shard_map/all_to_all | solution.py:328
  62.9 11.8 %collective-permute-start.2 = (bf16[32,16,128]{2,1,0:T(8,128)(2,1)S(1)}, bf16[32,16,128]{2,1,0:T(8,128)(2,1)S(1)}, u32[]{:S(2)}, u32[]{:S(2)}) collective-permute-start(bf16[32,16,128]{2,1,0:T(8,128)(2,1)S(1)} %get-tuple-element.19), channel_id=1, source_target_pairs={{0,2},{1,3},{2,0},{3,1},{4,6},{5,7},{6,4},{7,5},{8,10},{9,11},{10,... | collective-permute-start | bytes 393224 | tf_op jit(solution)/shard_map/ppermute | solution.py:288
  69.0 5.6 %collective-permute-start.7 = (bf16[64,128]{1,0:T(8,128)(2,1)S(1)}, bf16[64,128]{1,0:T(8,128)(2,1)S(1)}, u32[]{:S(2)}, u32[]{:S(2)}) collective-permute-start(bf16[64,128]{1,0:T(8,128)(2,1)S(1)} %shard_map.43), channel_id=1, source_target_pairs={{0,2},{1,3},{2,0},{3,1},{4,6},{5,7},{6,4},{7,5},{8,10},{9,11},{10,... | collective-permute-start | bytes 49160 | tf_op jit(solution)/shard_map/ppermute | solution.py:288

commit v13 on v9

--- a/solution.py
+++ b/solution.py
@@ -134,6 +134,14 @@
             axis=0,
         )
 
+    near = jnp.concatenate(
+        [held[chip, z * 17 + 16 * (1 - half)] for z in range(2) for chip in range(4) for held in (mine, theirs)],
+        axis=0,
+    )
+    ends = [
+        [aligned(jnp.dot(w[pl.ds(b * 96, 96)], near, preferred_element_type=F32), lane) for b in (0, 2)]
+        for w in (taps, taps2)
+    ]
     for p in range(8):
         pair = jnp.concatenate([row_of(2 * p), row_of(2 * p + 1)], axis=1)
         for t, (weights, to) in enumerate(((taps, pre), (taps2, pre2))):
@@ -147,12 +155,17 @@
                     if not (b == 0 or (b == 1 and row == 0)):
                         part = part + sums[t, row]
                     if b == 2 or (b == 1 and row == 15):
-                        to[row] = aligned(part, lane)
+                        total = aligned(part, lane)
+                        if row == 0:
+                            total = total + jnp.where(half == 1, ends[t][0], 0.0)
+                        if row == 15:
+                            total = total + jnp.where(half == 0, ends[t][1], 0.0)
+                        to[row] = total
                     else:
                         sums[t, row] = part
 
 
-def outer_kernel(pre, taps, mine, theirs, halo, filters, out, flat):
+def outer_kernel(pre, taps, halo, filters, out, flat):
     me = lax.axis_index("ch")
     half, core = half_of(), lax.rem(me, 2)
     parts = filters[pl.ds(432, 16)].astype(F32)
@@ -183,20 +196,12 @@
     far = jnp.concatenate(
         [halo[source, pl.ds(z * 16, 16)] for z in range(2) for source in sources], axis=0
     ).astype(F32)
-    near = jnp.concatenate(
-        [
-            held[chip, z * 17 + 16 * (1 - half)]
-            for z in range(2)
-            for chip in range(4)
-            for held in (mine, theirs)
-        ],
-        axis=0,
-    ).astype(F32)
-    first_half = half == 0
-    above = jnp.where(first_half, far, near).astype(BF)
-    below = jnp.where(first_half, near, far).astype(BF)
-    above = aligned(jnp.dot(taps[pl.ds(0, 96)], above, preferred_element_type=F32), lane)
-    below = aligned(jnp.dot(taps[pl.ds(192, 96)], below, preferred_element_type=F32), lane)
+    far = far.astype(BF)
+    ends = [
+        aligned(jnp.dot(taps[pl.ds(b * 96, 96)], far, preferred_element_type=F32), lane) for b in (0, 2)
+    ]
+    above = jnp.where(half == 0, ends[0], 0.0)
+    below = jnp.where(half == 1, ends[1], 0.0)
     for row in range(16):
         total = pre[row] + offset
         if row == 0:
@@ -217,8 +222,8 @@
     copy.wait()
 
 
-def kept_kernel(pre, taps, mine, theirs, halo, filters, out, flat, ready, sem):
-    outer_kernel(pre, taps, mine, theirs, halo, filters, ready, flat)
+def kept_kernel(pre, taps, halo, filters, out, flat, ready, sem):
+    outer_kernel(pre, taps, halo, filters, ready, flat)
     place(ready, out, 16 * half_of(), sem)
 
 
@@ -289,21 +294,9 @@
     flat = pltpu.VMEM((512, 128), F32)
     ready, sem = pltpu.VMEM((16, 2, 16, 128), BF), pltpu.SemaphoreType.DMA
     space = pl.BlockSpec(memory_space=pl.ANY)
-    sent = call(outer_kernel, shaped(16, 2, 16, 128), [flat], pre2, taps2, mine, theirs, halo, other, **cost)
+    sent = call(outer_kernel, shaped(16, 2, 16, 128), [flat], pre2, taps2, halo, other, **cost)
     got = swapped(sent, 2)
-    result = call(
-        kept_kernel,
-        shaped(16, 2, 32, 128),
-        [flat, ready, sem],
-        pre,
-        taps,
-        mine,
-        theirs,
-        halo,
-        own,
-        place=space,
-        **cost,
-    )
+    result = call(kept_kernel, shaped(16, 2, 32, 128), [flat, ready, sem], pre, taps, halo, own, place=space, **cost)
     return call(unpack_kernel, shaped(16, 2, 32, 128), [sem], got, result, moved=1 << 18, place=space, shared={1: 0})
 
 

time: 64.6 us -> 63.8 us (0.988)
  the two profiles are of different devices: /device:TPU:30 before, /device:TPU:24 now
where the time goes in v13:
time: 63.8 us; the launch traced here: 63.4 us
  starting transfers between devices  37.7 us (59%)
  waiting for transfers between devices  18.2 us (29%)
  Pallas kernels  6.24 us (10%)
  local copies, waits for them, and re-layouts  1.06 us (2%)
    ppermute x4, starting transfers between devices, shifts(): lax.ppermute(array, axis, pairs if up else [(j, i) for i, j in pairs])  16.1 us
    ppermute x3, starting transfers between devices, swapped(): return lax.ppermute(array, 'ch', [(d, d ^ t) for d in range(8)])  8.67 us
    all_to_all x1, starting transfers between devices, stages(): lax.all_to_all(blocks, 'ch', split_axis=0, concat_axis=0, tiled=True, axi...  7.39 us
    ppermute x3, waiting for transfers between devices, swapped(): return lax.ppermute(array, 'ch', [(d, d ^ t) for d in range(8)])  7.15 us
    pallas_call x9, Pallas kernels, call(): pl.pallas_call(kernel, out_shape=out_shapes, in_specs=in_specs, out_specs...  6.24 us
    all_to_all x1, waiting for transfers between devices, stages(): lax.all_to_all(blocks, 'ch', split_axis=0, concat_axis=0, tiled=True, axi...  5.81 us
    all_to_all x1, starting transfers between devices, stages(): halo = lax.all_to_all(halo, 'ch', split_axis=0, concat_axis=0, tiled=True)  5.54 us
    ppermute x4, waiting for transfers between devices, shifts(): lax.ppermute(array, axis, pairs if up else [(j, i) for i, j in pairs])  5.25 us
  transfers between devices with their start and end apart: 9, of which 5 were waited for; matrix products, arithmetic and copies ran while one was open for 0% of the time, Pallas kernels for 6%

profile of v13, /device:TPU:24, one launch (start us, length us, event | category | flops | bytes accessed | tf_op | source)
XLA Modules:
  0.0 63.4 jit_solution(15416870284532440957)
XLA Ops:
  0.0 0.0 copy-start
  0.0 0.9 %copy-done = bf16[16,2,32,128]{3,2,1,0:T(8,128)(2,1)S(1)} copy-done((bf16[16,2,32,128]{3,2,1,0:T(8,128)(2,1)S(1)}, bf16[16,2,32,128]{3,2,1,0:T(8,128)(2,1)}, u32[]{:S(2)}) %copy-start) | copy-done | bytes 262168
  1.0 1.1 %shard_map.37 = (bf16[4,34,16,128]{3,2,1,0:T(8,128)(2,1)}, bf16[32,128]{1,0:T(8,128)(2,1)S(1)}, bf16[32,128]{1,0:T(8,128)(2,1)S(1)}) custom-call(bf16[16,2,32,128]{3,2,1,0:T(8,128)(2,1)S(1)} %copy-done), custom_call_target="tpu_custom_call" | custom-call | bytes 1048576 | tf_op jit(solution)/shard_map/pallas_call | solution.py:21
  2.1 0.0 copy-start.1
  2.1 7.4 %all-to-all-start = ((bf16[4,34,16,128]{3,2,1,0:T(8,128)(2,1)}), bf16[4,34,16,128]{3,2,1,0:T(8,128)(2,1)S(1)}, u32[]{:S(2)}, u32[]{:S(2)}) async-start(bf16[4,34,16,128]{3,2,1,0:T(8,128)(2,1)} %get-tuple-element.15), calls=%async_computation | async-start | bytes 1114112 | tf_op jit(solution)/shard_map/all_to_all | solution.py:261
  9.5 0.0 copy-done.1
  9.5 0.0 copy-start.3
  9.5 0.2 shard_map.40
  9.7 8.2 %collective-permute-start.2 = (bf16[32,128]{1,0:T(8,128)(2,1)S(1)}, bf16[32,128]{1,0:T(8,128)(2,1)S(1)}, u32[]{:S(2)}, u32[]{:S(2)}) collective-permute-start(bf16[32,128]{1,0:T(8,128)(2,1)S(1)} %shard_map.40), channel_id=1, source_target_pairs={{0,8},{8,16},{16,24},{24,32},{32,40},{40,48},{48,56},{1,9},{9,17},... | collective-permute-start | bytes 24584 | tf_op jit(solution)/shard_map/ppermute | solution.py:237
  17.9 1.3 %collective-permute-start.3 = (bf16[32,128]{1,0:T(8,128)(2,1)S(1)}, bf16[32,128]{1,0:T(8,128)(2,1)S(1)}, u32[]{:S(2)}, u32[]{:S(2)}) collective-permute-start(bf16[32,128]{1,0:T(8,128)(2,1)S(1)} %shard_map.40), channel_id=1, source_target_pairs={{8,0},{16,8},{24,16},{32,24},{40,32},{48,40},{56,48},{9,1},{17,9},... | collective-permute-start | bytes 24584 | tf_op jit(solution)/shard_map/ppermute | solution.py:237
  19.2 5.8 %all-to-all-done.mine = bf16[4,34,16,128]{3,2,1,0:T(8,128)(2,1)S(1)} async-done(((bf16[4,34,16,128]{3,2,1,0:T(8,128)(2,1)}), bf16[4,34,16,128]{3,2,1,0:T(8,128)(2,1)S(1)}, u32[]{:S(2)}, u32[]{:S(2)}) %all-to-all-start) | async-done | bytes 557088 | tf_op jit(solution)/shard_map/all_to_all | solution.py:261
  25.0 1.9 %collective-permute-start = (bf16[4,34,16,128]{3,2,1,0:T(8,128)(2,1)S(1)}, bf16[4,34,16,128]{3,2,1,0:T(8,128)(2,1)S(1)}, u32[]{:S(2)}, u32[]{:S(2)}) collective-permute-start(bf16[4,34,16,128]{3,2,1,0:T(8,128)(2,1)S(1)} %all-to-all-done.mine), channel_id=1, source_target_pairs={{0,1},{1,0},{2,3},{3,2},{4,5},{5,4},{6,7},{7,6},{8,9},{9,8},{10,11... | collective-permute-start | bytes 1671176 | tf_op jit(solution)/shard_map/ppermute | solution.py:241
  26.9 0.0 copy-done.3
  27.0 0.0 collective-permute-done.2.left
  27.0 0.5 collective-permute-done.3.right
  27.5 0.1 shard_map.41
  27.6 4.7 %collective-permute-start.4 = (bf16[48,128]{1,0:T(8,128)(2,1)S(1)}, bf16[48,128]{1,0:T(8,128)(2,1)S(1)}, u32[]{:S(2)}, u32[]{:S(2)}) collective-permute-start(bf16[48,128]{1,0:T(8,128)(2,1)S(1)} %get-tuple-element.21), channel_id=1, source_target_pairs={{0,64},{64,128},{128,192},{192,256},{256,320},{320,384},{384,448},... | collective-permute-start | bytes 36872 | tf_op jit(solution)/shard_map/ppermute | solution.py:237
  32.2 1.9 %collective-permute-start.5 = (bf16[48,128]{1,0:T(8,128)(2,1)S(1)}, bf16[48,128]{1,0:T(8,128)(2,1)S(1)}, u32[]{:S(2)}, u32[]{:S(2)}) collective-permute-start(bf16[48,128]{1,0:T(8,128)(2,1)S(1)} %get-tuple-element.22), channel_id=1, source_target_pairs={{64,0},{128,64},{192,128},{256,192},{320,256},{384,320},{448,384},... | collective-permute-start | bytes 36872 | tf_op jit(solution)/shard_map/ppermute | solution.py:237
  34.2 0.1 copy.8
  34.3 0.0 collective-permute-done.4.above
  34.3 4.8 %collective-permute-done.5.below = bf16[48,128]{1,0:T(8,128)(2,1)S(1)} collective-permute-done((bf16[48,128]{1,0:T(8,128)(2,1)S(1)}, bf16[48,128]{1,0:T(8,128)(2,1)S(1)}, u32[]{:S(2)}, u32[]{:S(2)}) %collective-permute-start.5) | collective-permute-done | bytes 12320 | tf_op jit(solution)/shard_map/ppermute | solution.py:237
  39.0 0.7 %shard_map.42 = bf16[8,48,128]{2,1,0:T(8,128)(2,1)} custom-call(bf16[48,128]{1,0:T(8,128)(2,1)S(1)} %collective-permute-done.4.above, bf16[48,128]{1,0:T(8,128)(2,1)S(1)} %collective-permute-done.5.below, f32[32,128]{1,0:T(8,128)S(1)} %get-tuple-element.23.beside), custom_call_target="tpu_custom_call" | custom-call | bytes 131072 | tf_op jit(solution)/shard_map/pallas_call | solution.py:21
  39.8 0.0 copy-start.2
  39.8 5.5 %all-to-all-start.1 = ((bf16[8,48,128]{2,1,0:T(8,128)(2,1)}), bf16[8,48,128]{2,1,0:T(8,128)(2,1)S(1)}, u32[]{:S(2)}, u32[]{:S(2)}) async-start(bf16[8,48,128]{2,1,0:T(8,128)(2,1)} %shard_map.42), calls=%async_computation.1 | async-start | bytes 196608 | tf_op jit(solution)/shard_map/all_to_all | solution.py:281
  45.3 0.0 copy-done.2
  45.3 3.9 %collective-permute-start.1 = (bf16[448,128]{1,0:T(8,128)(2,1)S(1)}, bf16[448,128]{1,0:T(8,128)(2,1)S(1)}, u32[]{:S(2)}, u32[]{:S(2)}) collective-permute-start(bf16[448,128]{1,0:T(8,128)(2,1)S(1)} %fusion.1.own.filters), channel_id=1, source_target_pairs={{0,2},{1,3},{2,0},{3,1},{4,6},{5,7},{6,4},{7,5},{8,10},{9,11},{10,... | collective-permute-start | bytes 344072 | tf_op jit(solution)/shard_map/ppermute | solution.py:241
  49.3 4.2 %collective-permute-done.1.other.filters = bf16[448,128]{1,0:T(8,128)(2,1)S(1)} collective-permute-done((bf16[448,128]{1,0:T(8,128)(2,1)S(1)}, bf16[448,128]{1,0:T(8,128)(2,1)S(1)}, u32[]{:S(2)}, u32[]{:S(2)}) %collective-permute-start.1) | collective-permute-done | bytes 114720 | tf_op jit(solution)/shard_map/ppermute | solution.py:241
  53.5 0.2 shard_map.38
  53.7 0.0 collective-permute-done.theirs
  53.7 0.9 %shard_map.39 = (f32[16,32,128]{2,1,0:T(8,128)S(1)}, f32[16,32,128]{2,1,0:T(8,128)S(1)}) custom-call(bf16[4,34,16,128]{3,2,1,0:T(8,128)(2,1)S(1)} %all-to-all-done.mine, bf16[4,34,16,128]{3,2,1,0:T(8,128)(2,1)S(1)} %collective-permute-done.theirs, bf16[288,256]{1,0:T(8,128)(2,1)S(1)} %get-tuple-element.16.taps, bf16[288,256]{1,0:T(8,128)(2,1)S(1)} %get-tuple-element.17.taps2.taps), custom_call_target="tpu_custom_call" | custom-call | flops 603979776 | bytes 3145728 | tf_op jit(solution)/shard_map/pallas_call | solution.py:21
  54.6 0.0 all-to-all-done.1.halo
  54.6 0.8 %shard_map.43 = bf16[16,2,16,128]{3,2,1,0:T(8,128)(2,1)S(1)} custom-call(f32[16,32,128]{2,1,0:T(8,128)S(1)} %get-tuple-element.18.pre, bf16[288,256]{1,0:T(8,128)(2,1)S(1)} %get-tuple-element.17.taps2.taps, bf16[8,48,128]{2,1,0:T(8,128)(2,1)S(1)} %all-to-all-done.1.halo, bf16[448,128]{1,0:T(8,128)(2,1)S(1)} %collective-permute-done.1.other.filters), custom_call_target="tpu_custom_call" | custom-call | flops 37748736 | bytes 1048576 | tf_op jit(solution)/shard_map/pallas_call | solution.py:21
  55.5 2.8 %collective-permute-start.6 = (bf16[16,2,16,128]{3,2,1,0:T(8,128)(2,1)S(1)}, bf16[16,2,16,128]{3,2,1,0:T(8,128)(2,1)S(1)}, u32[]{:S(2)}, u32[]{:S(2)}) collective-permute-start(bf16[16,2,16,128]{3,2,1,0:T(8,128)(2,1)S(1)} %shard_map.43), channel_id=1, source_target_pairs={{0,2},{1,3},{2,0},{3,1},{4,6},{5,7},{6,4},{7,5},{8,10},{9,11},{10,... | collective-permute-start | bytes 393224 | tf_op jit(solution)/shard_map/ppermute | solution.py:241
  58.3 1.5 %shard_map.44.held = bf16[16,2,32,128]{3,2,1,0:T(8,128)(2,1)} custom-call(f32[16,32,128]{2,1,0:T(8,128)S(1)} %get-tuple-element.24.pre, bf16[288,256]{1,0:T(8,128)(2,1)S(1)} %get-tuple-element.16.taps, bf16[8,48,128]{2,1,0:T(8,128)(2,1)S(1)} %all-to-all-done.1.halo, bf16[448,128]{1,0:T(8,128)(2,1)S(1)} %fusion.1.own.filters), custom_call_target="tpu_custom_call" | custom-call | flops 37748736 | bytes 1048576 | tf_op jit(solution)/shard_map/pallas_call | solution.py:21
  59.8 2.9 %collective-permute-done.6.got = bf16[16,2,16,128]{3,2,1,0:T(8,128)(2,1)S(1)} collective-permute-done((bf16[16,2,16,128]{3,2,1,0:T(8,128)(2,1)S(1)}, bf16[16,2,16,128]{3,2,1,0:T(8,128)(2,1)S(1)}, u32[]{:S(2)}, u32[]{:S(2)}) %collective-permute-start.6) | collective-permute-done | bytes 131104 | tf_op jit(solution)/shard_map/ppermute | solution.py:241
  62.7 0.7 %shard_map.45 = bf16[16,2,32,128]{3,2,1,0:T(8,128)(2,1)} custom-call(bf16[16,2,16,128]{3,2,1,0:T(8,128)(2,1)S(1)} %collective-permute-done.6.got, bf16[16,2,32,128]{3,2,1,0:T(8,128)(2,1)} %shard_map.44.held), custom_call_target="tpu_custom_call", output_to_operand_aliasing={{}: (1, {})} | custom-call | bytes 262144 | tf_op jit(solution)/shard_map/pallas_call | solution.py:21
  (3 shorter events, 0.0 us)
Async XLA Ops:
  0.0 0.9 %copy-start = (bf16[16,2,32,128]{3,2,1,0:T(8,128)(2,1)S(1)}, bf16[16,2,32,128]{3,2,1,0:T(8,128)(2,1)}, u32[]{:S(2)}) copy-start(bf16[16,2,32,128]{3,2,1,0:T(8,128)(2,1)} %vol.3) | copy-start | bytes 786436
  2.1 7.4 %copy-start.1 = (bf16[16,2,32,128]{3,2,1,0:T(8,128)(2,1)S(1)}, bf16[16,2,32,128]{3,2,1,0:T(8,128)(2,1)}, u32[]{:S(2)}) copy-start(bf16[16,2,32,128]{3,2,1,0:T(8,128)(2,1)} %vol.3) | copy-start | bytes 786436
  2.1 22.9 %all-to-all-start = ((bf16[4,34,16,128]{3,2,1,0:T(8,128)(2,1)}), bf16[4,34,16,128]{3,2,1,0:T(8,128)(2,1)S(1)}, u32[]{:S(2)}, u32[]{:S(2)}) async-start(bf16[4,34,16,128]{3,2,1,0:T(8,128)(2,1)} %get-tuple-element.15), calls=%async_computation | async-start | bytes 1114112 | tf_op jit(solution)/shard_map/all_to_all | solution.py:261
  9.5 17.5 %copy-start.3 = (f32[16]{0:T(128)S(1)}, f32[16]{0:T(128)}, u32[]{:S(2)}) copy-start(f32[16]{0:T(128)} %param.5) | copy-start | bytes 196
  9.7 17.3 %collective-permute-start.2 = (bf16[32,128]{1,0:T(8,128)(2,1)S(1)}, bf16[32,128]{1,0:T(8,128)(2,1)S(1)}, u32[]{:S(2)}, u32[]{:S(2)}) collective-permute-start(bf16[32,128]{1,0:T(8,128)(2,1)S(1)} %shard_map.40), channel_id=1, source_target_pairs={{0,8},{8,16},{16,24},{24,32},{32,40},{40,48},{48,56},{1,9},{9,17},... | collective-permute-start | bytes 24584 | tf_op jit(solution)/shard_map/ppermute | solution.py:237
  17.9 9.6 %collective-permute-start.3 = (bf16[32,128]{1,0:T(8,128)(2,1)S(1)}, bf16[32,128]{1,0:T(8,128)(2,1)S(1)}, u32[]{:S(2)}, u32[]{:S(2)}) collective-permute-start(bf16[32,128]{1,0:T(8,128)(2,1)S(1)} %shard_map.40), channel_id=1, source_target_pairs={{8,0},{16,8},{24,16},{32,24},{40,32},{48,40},{56,48},{9,1},{17,9},... | collective-permute-start | bytes 24584 | tf_op jit(solution)/shard_map/ppermute | solution.py:237
  25.0 28.7 %collective-permute-start = (bf16[4,34,16,128]{3,2,1,0:T(8,128)(2,1)S(1)}, bf16[4,34,16,128]{3,2,1,0:T(8,128)(2,1)S(1)}, u32[]{:S(2)}, u32[]{:S(2)}) collective-permute-start(bf16[4,34,16,128]{3,2,1,0:T(8,128)(2,1)S(1)} %all-to-all-done.mine), channel_id=1, source_target_pairs={{0,1},{1,0},{2,3},{3,2},{4,5},{5,4},{6,7},{7,6},{8,9},{9,8},{10,11... | collective-permute-start | bytes 1671176 | tf_op jit(solution)/shard_map/ppermute | solution.py:241
  27.6 6.7 %collective-permute-start.4 = (bf16[48,128]{1,0:T(8,128)(2,1)S(1)}, bf16[48,128]{1,0:T(8,128)(2,1)S(1)}, u32[]{:S(2)}, u32[]{:S(2)}) collective-permute-start(bf16[48,128]{1,0:T(8,128)(2,1)S(1)} %get-tuple-element.21), channel_id=1, source_target_pairs={{0,64},{64,128},{128,192},{192,256},{256,320},{320,384},{384,448},... | collective-permute-start | bytes 36872 | tf_op jit(solution)/shard_map/ppermute | solution.py:237
  32.2 6.8 %collective-permute-start.5 = (bf16[48,128]{1,0:T(8,128)(2,1)S(1)}, bf16[48,128]{1,0:T(8,128)(2,1)S(1)}, u32[]{:S(2)}, u32[]{:S(2)}) collective-permute-start(bf16[48,128]{1,0:T(8,128)(2,1)S(1)} %get-tuple-element.22), channel_id=1, source_target_pairs={{64,0},{128,64},{192,128},{256,192},{320,256},{384,320},{448,384},... | collective-permute-start | bytes 36872 | tf_op jit(solution)/shard_map/ppermute | solution.py:237
  39.8 5.5 %copy-start.2 = (bf16[16,128,3,3,3]{1,0,4,3,2:T(8,128)(2,1)S(1)}, bf16[16,128,3,3,3]{1,0,4,3,2:T(8,128)(2,1)}, u32[]{:S(2)}) copy-start(bf16[16,128,3,3,3]{1,0,4,3,2:T(8,128)(2,1)} %param.4) | copy-start | bytes 331780
  39.8 14.9 %all-to-all-start.1 = ((bf16[8,48,128]{2,1,0:T(8,128)(2,1)}), bf16[8,48,128]{2,1,0:T(8,128)(2,1)S(1)}, u32[]{:S(2)}, u32[]{:S(2)}) async-start(bf16[8,48,128]{2,1,0:T(8,128)(2,1)} %shard_map.42), calls=%async_computation.1 | async-start | bytes 196608 | tf_op jit(solution)/shard_map/all_to_all | solution.py:281
  45.3 8.2 %collective-permute-start.1 = (bf16[448,128]{1,0:T(8,128)(2,1)S(1)}, bf16[448,128]{1,0:T(8,128)(2,1)S(1)}, u32[]{:S(2)}, u32[]{:S(2)}) collective-permute-start(bf16[448,128]{1,0:T(8,128)(2,1)S(1)} %fusion.1.own.filters), channel_id=1, source_target_pairs={{0,2},{1,3},{2,0},{3,1},{4,6},{5,7},{6,4},{7,5},{8,10},{9,11},{10,... | collective-permute-start | bytes 344072 | tf_op jit(solution)/shard_map/ppermute | solution.py:241
  55.5 7.3 %collective-permute-start.6 = (bf16[16,2,16,128]{3,2,1,0:T(8,128)(2,1)S(1)}, bf16[16,2,16,128]{3,2,1,0:T(8,128)(2,1)S(1)}, u32[]{:S(2)}, u32[]{:S(2)}) collective-permute-start(bf16[16,2,16,128]{3,2,1,0:T(8,128)(2,1)S(1)} %shard_map.43), channel_id=1, source_target_pairs={{0,2},{1,3},{2,0},{3,1},{4,6},{5,7},{6,4},{7,5},{8,10},{9,11},{10,... | collective-permute-start | bytes 393224 | tf_op jit(solution)/shard_map/ppermute | solution.py:241
